TPU v7x, 32 devices: a whole 2x2x4 slice. The times are simulated.
32 devices in a mesh: seq: 4 (over x, core), shard: 8 (over z, y).
Axes of the slice: x: 2, y: 2, z: 4, core: 2. Of those that a mesh axis runs over, the one named last changes fastest.
Arguments:
- inputs: bfloat16 [16, 2048, 768], P('shard', 'seq'), may hold values from -6 to 6
- first_gain: bfloat16 [768], P(('seq', 'shard')), may hold values from 0.25 to 1.75
- first_shift: bfloat16 [768], P(('seq', 'shard')), may hold values from -3 to 3
- second_gain: bfloat16 [768], P(('seq', 'shard')), may hold values from 0.25 to 1.75
- second_shift: bfloat16 [768], P(('seq', 'shard')), may hold values from -3 to 3
- packed_weight: bfloat16 [768, 2304], P(('seq', 'shard')), may hold values from -1.5 to 1.5
- packed_bias: bfloat16 [3, 768], P(None, ('seq', 'shard')), may hold values from -3 to 3
- output_weight: bfloat16 [768, 768], P(('seq', 'shard')), may hold values from -0.875 to 0.875
- output_bias: bfloat16 [768], P(('seq', 'shard')), may hold values from -3 to 3
- expand_weight: bfloat16 [768, 3072], P(('seq', 'shard')), may hold values from -0.21875 to 0.21875
- expand_bias: bfloat16 [3072], P(('seq', 'shard')), may hold values from -3 to 3
- reduce_weight: bfloat16 [3072, 768], P(('seq', 'shard')), may hold values from -0.109375 to 0.109375
- reduce_bias: bfloat16 [768], P(('seq', 'shard')), may hold values from -3 to 3
- cotangent: bfloat16 [16, 2048, 768], P('shard', 'seq'), may hold values from -6 to 6
Outputs:
- layer_out: bfloat16 [16, 2048, 768], P('shard', 'seq')
- input_grad: bfloat16 [16, 2048, 768], P('shard', 'seq')
- first_gain_grad: float32 [768], P(('seq', 'shard'))
- first_shift_grad: float32 [768], P(('seq', 'shard'))
- second_gain_grad: float32 [768], P(('seq', 'shard'))
- second_shift_grad: float32 [768], P(('seq', 'shard'))
- packed_weight_grad: float32 [768, 2304], P(('seq', 'shard'))
- packed_bias_grad: float32 [3, 768], P(None, ('seq', 'shard'))
- output_weight_grad: float32 [768, 768], P(('seq', 'shard'))
- output_bias_grad: float32 [768], P(('seq', 'shard'))
- expand_weight_grad: float32 [768, 3072], P(('seq', 'shard'))
- expand_bias_grad: float32 [3072], P(('seq', 'shard'))
- reduce_weight_grad: float32 [3072, 768], P(('seq', 'shard'))
- reduce_bias_grad: float32 [768], P(('seq', 'shard'))
All inputs are finite; a program needn't handle non-finite values.
Results may differ from a plain program's by a relative error of at most 0.012.
Values may be sent and summed in bfloat16 or wider, within the bound.
No kernel may reach another device: no remote copies, remote signals or barrier semaphores. Data moves between devices by JAX's collectives and lax.ppermute only.
A program may use at most 448 MiB of HBM per device.

v0:
```python
import functools
import jax, jax.numpy as jnp
from jax import lax
from jax.experimental import pallas as pl
from jax.experimental.pallas import tpu as pltpu
from jax.sharding import Mesh, PartitionSpec as P

HD=64
ROT=16
f32=jnp.float32; bf16=jnp.bfloat16

def dot(a,b): return jnp.dot(a,b,preferred_element_type=f32)

def turn(v,tab,back):
    sgn=-1.0 if back else 1.0
    return v*tab[0]+sgn*(pltpu.roll(v,120,1)*tab[1]+pltpu.roll(v,8,1)*tab[2])

def attn_body(c_ref, own, par, gown, gpar, tab, keep, send, qs, ks, gs, vs, qT, gT, kT, vT, es, oT, dqT, dk, dv, *, blk, length):
    c=c_ref[0]
    nb=length//blk
    lane=lax.broadcasted_iota(jnp.int32,(1,128),1)
    first=lane<HD
    for j,(d,dT) in enumerate(((qs,qT),(ks,kT),(vs,vT),(gs,gT))):
        for h in range(nb//2):
            hr=slice(h*blk,(h+1)*blk)
            a,b=(own[j,hr,:],par[j,hr,:]) if j<3 else (gown[hr,:],gpar[hr,:])
            pa=pl.multiple_of((2*h+c)*blk,blk); pb=pl.multiple_of((2*h+1-c)*blk,blk)
            d[pl.ds(pa,blk),:]=a
            d[pl.ds(pb,blk),:]=b
            dT[2*h+c]=a.T
            dT[2*h+1-c]=b.T
    dk[...]=jnp.zeros_like(dk); dv[...]=jnp.zeros_like(dv)
    kk=HD**-0.5*1.4426950408889634
    rowi=lax.broadcasted_iota(jnp.int32,(blk,blk),0)
    coli=lax.broadcasted_iota(jnp.int32,(blk,blk),1)
    allowed=rowi<=coli
    zero64=jnp.zeros((HD,blk),bf16)

    def block(i,_):
        qt=qT[i]; gt=gT[i]
        qh=[jnp.concatenate([qt[:HD],zero64],0),jnp.concatenate([zero64,qt[HD:]],0)]
        gh=[jnp.concatenate([gt[:HD],zero64],0),jnp.concatenate([zero64,gt[HD:]],0)]
        rows=pl.ds(pl.multiple_of(i*blk,blk),blk)
        q=qs[rows,:]; g=gs[rows,:]
        zq=jnp.zeros_like(q)
        qm=[jnp.where(first,q,zq),jnp.where(first,zq,q)]
        gm=[jnp.where(first,g,zq),jnp.where(first,zq,g)]
        def sA(j,m):
            kr=pl.ds(pl.multiple_of(j*blk,blk),blk)
            k=ks[kr,:]
            out=[]
            for h in range(2):
                s=dot(k,qh[h])
                es[h,kr,:]=s
                out.append(jnp.maximum(m[h],jnp.max(s.reshape(blk//8,8,blk),axis=0)))
            return tuple(out)
        m0=jnp.full((8,blk),-1e30,f32)
        k=ks[rows,:]
        m=[]
        for h in range(2):
            s=jnp.where(allowed,dot(k,qh[h]),-1e30)
            es[h,rows,:]=s
            m.append(jnp.max(s.reshape(blk//8,8,blk),axis=0))
        m=lax.fori_loop(0,i,sA,tuple(m))
        mk=[jnp.max(t,axis=0,keepdims=True)*kk for t in m]
        oT[...]=jnp.zeros_like(oT)
        def sB(j,l):
            kr=pl.ds(pl.multiple_of(j*blk,blk),blk)
            out=[]
            for h in range(2):
                e=jnp.exp2(es[h,kr,:]*kk-mk[h])
                es[h,kr,:]=e
                out.append(l[h]+jnp.sum(e.reshape(blk//8,8,blk),axis=0))
                oT[h*HD:(h+1)*HD,:]+=dot(vT[j,h*HD:(h+1)*HD,:],e.astype(bf16))
            return tuple(out)
        z=jnp.zeros((8,blk),f32)
        l=lax.fori_loop(0,i+1,sB,(z,z))
        r=[1.0/jnp.sum(t,axis=0,keepdims=True) for t in l]
        o=[oT[h*HD:(h+1)*HD,:]*r[h] for h in range(2)]
        D=[jnp.sum(o[h]*gt[h*HD:(h+1)*HD].astype(f32),axis=0,keepdims=True) for h in range(2)]
        oT[...]=jnp.concatenate(o,0)
        dqT[...]=jnp.zeros_like(dqT)
        def sC(j,_):
            kr=pl.ds(pl.multiple_of(j*blk,blk),blk)
            v=vs[kr,:]
            pb=[];db=[]
            for h in range(2):
                p=es[h,kr,:]*r[h]
                ds=(p*(dot(v,gh[h])-D[h])).astype(bf16)
                pb.append(p.astype(bf16)); db.append(ds)
                dqT[h*HD:(h+1)*HD,:]+=dot(kT[j,h*HD:(h+1)*HD,:],ds)
            dv[kr,:]+=dot(pb[0],gm[0])+dot(pb[1],gm[1])
            dk[kr,:]+=dot(db[0],qm[0])+dot(db[1],qm[1])
            return 0
        lax.fori_loop(0,i+1,sC,0)
        qs[rows,:]=(dqT[...].T*HD**-0.5).astype(bf16)
        gs[rows,:]=oT[...].T.astype(bf16)
        return 0
    lax.fori_loop(0,nb,block,0)
    for h in range(nb//2):
        for who,ref in ((c,keep),(1-c,send)):
            rows=pl.ds(pl.multiple_of((2*h+who)*blk,blk),blk)
            dst=slice(h*blk,(h+1)*blk)
            t=[tab[n,rows,:] for n in range(3)]
            ref[0,dst,:]=gs[rows,:]
            ref[1,dst,:]=turn(qs[rows,:].astype(f32),t,True).astype(bf16)
            ref[2,dst,:]=turn((dk[rows,:]*HD**-0.5).astype(bf16).astype(f32),t,True).astype(bf16)
            ref[3,dst,:]=dv[rows,:].astype(bf16)

def attention(c, own, par, gown, gpar, tab, pair, npair=1, blk=512):
    rows=own.shape[1]; length=2*rows
    nb=length//blk
    spec=pl.BlockSpec((3,rows,128),lambda p,c:(0,0,p+pair))
    gspec=pl.BlockSpec((rows,128),lambda p,c:(0,p+pair))
    ospec=pl.BlockSpec((4,rows,128),lambda p,c:(0,0,p))
    V=pltpu.VMEM
    return pl.pallas_call(
        functools.partial(attn_body,blk=blk,length=length),
        out_shape=(jax.ShapeDtypeStruct((4,rows,128*npair),bf16),)*2,
        grid_spec=pltpu.PrefetchScalarGridSpec(num_scalar_prefetch=1,grid=(npair,),
            in_specs=[spec,spec,gspec,gspec,pl.BlockSpec((3,length,128),lambda p,c:(0,0,0),pipeline_mode=pl.Buffered(1))],
            out_specs=[ospec,ospec],
            scratch_shapes=[V((length,128),bf16)]*4+[V((nb,128,blk),bf16)]*4+
              [V((2,length,blk),f32),V((128,blk),f32),V((128,blk),f32),V((length,128),f32),V((length,128),f32)]),
        compiler_params=pltpu.CompilerParams(vmem_limit_bytes=56<<20),
        name="attention",
        cost_estimate=pl.CostEstimate(flops=int(6*2*length*length//2*HD*2*npair*4),transcendentals=length*length*npair,bytes_accessed=16*rows*128*2*npair),
    )(c,own,par,gown,gpar,tab)
eps_norm = 1e-05
rope_base = 10000.0
EXTRA = 128

def dot_nt(a,b): return lax.dot_general(a,b,(((1,),(1,)),((),())),preferred_element_type=f32)
def dot_tn(a,b): return lax.dot_general(a,b,(((0,),(0,)),((),())),preferred_element_type=f32)

def norm_of(x):
    x=x.astype(f32)
    ce=x-jnp.mean(x,axis=-1,keepdims=True)
    inv=lax.rsqrt(jnp.mean(ce*ce,axis=-1,keepdims=True)+eps_norm)
    return ce*inv,inv

def norm_back(up,normed,inv,gain):
    s=up*gain
    return inv*(s-jnp.mean(s,axis=-1,keepdims=True)-normed*jnp.mean(s*normed,axis=-1,keepdims=True))

WHOLE=lambda shape: pl.BlockSpec(shape,lambda *a:(0,)*len(shape),pipeline_mode=pl.Buffered(1))

def pack_body(pk,ow,a,b,c,d,e,f,pb,eb,out,s):
    r=out.shape[0]
    s[...]=jnp.zeros_like(s)
    for k,v in enumerate((a,b,c,d,e,f)): s[k:k+1,0:r]=v[...].astype(f32)[None,:]
    s[6:9,0:r]=pb[...].astype(f32)
    ebv=eb[...].astype(f32)[None,:]
    for k in range(4): s[9+k:10+k,0:r]=ebv[:,k*r:(k+1)*r]
    out[:,:1536]=pk[:,:1536]
    out[:,1536:1536+EXTRA]=s[...].T[0:r,:].astype(bf16)
    out[:,1536+EXTRA:2304+EXTRA]=pk[:,1536:]
    out[:,2304+EXTRA:]=ow[...]
def pack(pk,ow,vecs,pb,eb):
    return pl.pallas_call(pack_body,out_shape=jax.ShapeDtypeStruct((pk.shape[0],3072+EXTRA),bf16),
        scratch_shapes=[pltpu.VMEM((EXTRA,128),f32)],name="pack")(pk,ow,*vecs,pb,eb)

def quarter(me_ref,n):
    return (me_ref[0]^(n//2))*2+(me_ref[1]^(n%2))

def rows_of(me_ref,n,q):
    return pl.ds(pl.multiple_of(quarter(me_ref,n)*q,q),q)

def split(c,value,keep,send,half):
    for k in range(2):
        @pl.when(c==k)
        def _():
            keep[...]=value[:,k*half:(k+1)*half]
            send[...]=value[:,(1-k)*half:(2-k)*half]

def proj_body(me, a, b, *refs):
    qa,qb=refs[:4],refs[4:8]
    tab,keep,send,t,vec,ws,ex=refs[8:]
    i=pl.program_id(0)
    @pl.when(i==0)
    def _():
        for n in range(4):
            rows=rows_of(me,n,qa[n].shape[0])
            ws[rows,:1536]=qa[n][:,:1536]
            ws[rows,1536:]=qb[n][...]
            ex[rows,:]=qa[n][:,1536:].astype(f32)
        vec[...]=ex[...].T[:16,:]
    x=jnp.where(i//2==me[0],a[0],b[...])
    t[...]=x
    normed,_=norm_of(x)
    b1=(normed*vec[0:1,:]+vec[1:2,:]).astype(bf16)
    tb=[tab[n] for n in range(3)]
    for j in range(3):
        v=dot(b1,ws[:,j*768:(j+1)*768])+vec[6+j:7+j,:]
        if j<2: v=jnp.concatenate([turn(v[:,g*128:(g+1)*128],tb,False) for g in range(6)],1)
        split(me[1],v.astype(bf16),keep.at[j],send.at[j],384)

def project(me,mine,other,qa,qb,tab,rb=256):
    n=2*other.shape[0]; per=n//2//rb
    S=jax.ShapeDtypeStruct
    out=pl.BlockSpec((3,rb,384),lambda i,me:(0,i,0))
    return pl.pallas_call(proj_body,
        out_shape=(S((3,n,384),bf16),S((3,n,384),bf16),S((n,768),bf16),S((16,768),f32)),
        grid_spec=pltpu.PrefetchScalarGridSpec(num_scalar_prefetch=1,grid=(n//rb,),
            in_specs=[pl.BlockSpec((1,rb,768),lambda i,me:(me[0],i%per,0)),pl.BlockSpec((rb,768),lambda i,me:(i%per,0))]+
              [WHOLE(w.shape) for w in qa]+[WHOLE((w.shape[0],768)) for w in qb]+
              [pl.BlockSpec((3,rb,128),lambda i,me:(0,(2*(i//per)+me[1])*per+i%per,0))],
            out_specs=(out,out,pl.BlockSpec((rb,768),lambda i,me:(i,0)),pl.BlockSpec((16,768),lambda i,me:(0,0))),
            scratch_shapes=[pltpu.VMEM((768,2304),bf16),pltpu.VMEM((768,EXTRA),f32)]),
        compiler_params=pltpu.CompilerParams(vmem_limit_bytes=56<<20),
        name="project",
        cost_estimate=pl.CostEstimate(flops=2*n*768*2304,transcendentals=n,bytes_accessed=n*768*10+768*3072*2),
    )(me,mine,other,*qa,*qb,tab)

def upst_body(me, a, b, *refs):
    qb,(keep,send,u,ws)=refs[:4],refs[4:]
    i=pl.program_id(0)
    @pl.when(i==0)
    def _():
        for n in range(4): ws[rows_of(me,n,qb[n].shape[0]),:]=qb[n][...]
    x=jnp.where(i//2==me[0],a[0],b[...])
    u[...]=x
    split(me[1],dot_nt(x,ws[...]).astype(bf16),keep,send,384)

def upstream_heads(me,mine,other,qb,rb=256):
    n=2*other.shape[0]; per=n//2//rb
    S=jax.ShapeDtypeStruct
    out=pl.BlockSpec((rb,384),lambda i,me:(i,0))
    return pl.pallas_call(upst_body,
        out_shape=(S((n,384),bf16),S((n,384),bf16),S((n,768),bf16)),
        grid_spec=pltpu.PrefetchScalarGridSpec(num_scalar_prefetch=1,grid=(n//rb,),
            in_specs=[pl.BlockSpec((1,rb,768),lambda i,me:(me[0],i%per,0)),pl.BlockSpec((rb,768),lambda i,me:(i%per,0))]+
              [pl.BlockSpec((w.shape[0],768),lambda i,me:(0,1),pipeline_mode=pl.Buffered(1)) for w in qb],
            out_specs=(out,out,pl.BlockSpec((rb,768),lambda i,me:(i,0))),
            scratch_shapes=[pltpu.VMEM((768,768),bf16)]),
        name="upstream",
        cost_estimate=pl.CostEstimate(flops=2*n*768*768,transcendentals=0,bytes_accessed=n*768*6+768*768*2),
    )(me,mine,other,*qb)

def outl_body(me, *refs):
    ka,ra,qb=refs[:3],refs[3:6],refs[6:10]
    mid,out,wos=refs[10:]
    @pl.when(pl.program_id(0)==0)
    def _():
        for n in range(4): wos[rows_of(me,n,qb[n].shape[0]),:]=qb[n][...]
    acc=mid[...]
    for g,a in ((0,ka),(1,ra)):
        rows=pl.ds(pl.multiple_of((me[1]^g)*384,384),384)
        acc=acc+dot(jnp.concatenate([r[0] for r in a],1),wos[rows,:])
    out[...]=acc.astype(bf16)

def layer_output(me,keep,recv,qb,mid,rb=256):
    n=mid.shape[0]
    a=pl.BlockSpec((1,rb,128),lambda i,me:(0,i,0))
    return pl.pallas_call(outl_body,
        out_shape=jax.ShapeDtypeStruct((n,768),bf16),
        grid_spec=pltpu.PrefetchScalarGridSpec(num_scalar_prefetch=1,grid=(n//rb,),
            in_specs=[a]*6+[pl.BlockSpec((w.shape[0],768),lambda i,me:(0,1),pipeline_mode=pl.Buffered(1)) for w in qb]+
              [pl.BlockSpec((rb,768),lambda i,me:(i,0))],
            out_specs=pl.BlockSpec((rb,768),lambda i,me:(i,0)),
            scratch_shapes=[pltpu.VMEM((768,768),bf16)]),
        name="layer_output",
        cost_estimate=pl.CostEstimate(flops=2*n*768*768,transcendentals=0,bytes_accessed=n*768*8+768*768*2),
    )(me,*keep,*recv,*qb,mid)

def back_body(me, *refs):
    ka,ra=refs[:3],refs[3:6]
    u,t,low=refs[6:9]
    qa,qb=refs[9:13],refs[13:17]
    vec,eb,sums_two,keepA,sendA,keepB,sendB,ig,ws,b1T,acc,gs,os,ex=refs[17:]
    g=pl.program_id(0)
    gc=me[1]^g
    @pl.when(g==0)
    def _():
        for i in range(4):
            rows=rows_of(me,i,qa[i].shape[0])
            for h in range(2):
                for j in range(2): ws[h,rows,j*384:(j+1)*384]=qa[i][:,(2*j+h)*384:(2*j+h+1)*384]
                ws[h,rows,768:1152]=qb[i][:,h*384:(h+1)*384]
        acc[...]=jnp.zeros_like(acc)
        ex[...]=jnp.zeros_like(ex)
        ex[4:5,:]=jnp.sum(u[...].astype(f32),axis=0,keepdims=True)
        ex[2:4,:]=sums_two[0:2,:]
        ex[8:12,:]=eb[...]
        normed,_=norm_of(t[...])
        b1T[...]=(normed*vec[0:1,:]+vec[1:2,:]).astype(bf16).T
    def one(a):
        p=jnp.concatenate([r[j] for j in (1,2,3) for r in a],1)
        acc[...]+=dot_nt(p,ws[gc])
        gs[...]=dot(b1T[...],p).astype(bf16)
        os[pl.ds(pl.multiple_of(gc*384,384),384),:]=dot_tn(jnp.concatenate([r[0] for r in a],1),u[...]).astype(bf16)
        s=jnp.sum(p.astype(f32),axis=0,keepdims=True)
        for h in range(2):
            @pl.when(gc==h)
            def _():
                for j in range(3): ex[5+j:6+j,h*384:(h+1)*384]=s[:,j*384:(j+1)*384]
    @pl.when(g==0)
    def _(): one(ka)
    @pl.when(g==1)
    def _(): one(ra)
    for h in range(2):
        @pl.when(gc==h)
        def _():
            for i in range(4):
                A,B=((keepA,keepB),(sendA,sendB))[i%2]
                r=gs[rows_of(me,i,192),:]
                for j in range(2): A[i//2,:,(2*j+h)*384:(2*j+h+1)*384]=r[:,j*384:(j+1)*384]
                B[i//2,:,h*384:(h+1)*384]=r[:,768:]
    @pl.when(g==1)
    def _():
        normed,inv=norm_of(t[...])
        b=acc[...]
        ex[0:1,:]=jnp.sum(b*normed,axis=0,keepdims=True)
        ex[1:2,:]=jnp.sum(b,axis=0,keepdims=True)
        ig[...]=(low[...]+norm_back(b,normed,inv,vec[0:1,:])).astype(bf16)
        acc[0:768,0:EXTRA]=ex[...].T
        for i in range(4):
            A,B=((keepA,keepB),(sendA,sendB))[i%2]
            rows=rows_of(me,i,192)
            B[i//2,:,768:]=os[rows,:]
            A[i//2,:,1536:]=acc[rows,0:EXTRA].astype(bf16)

def back(me,keep,recv,u,t,low,qa,qb,vec,eb,sums_two):
    n=t.shape[0]
    S=jax.ShapeDtypeStruct; V=pltpu.VMEM
    A,B=(2,192,1536+EXTRA),(2,192,1536)
    return pl.pallas_call(back_body,
        out_shape=(S(A,bf16),S(A,bf16),S(B,bf16),S(B,bf16),S((n,768),bf16)),
        grid_spec=pltpu.PrefetchScalarGridSpec(num_scalar_prefetch=1,grid=(2,),
            in_specs=[WHOLE((4,n,128))]*6+[WHOLE((n,768))]*3+
              [WHOLE(w.shape) for w in qa]+[WHOLE((w.shape[0],768)) for w in qb]+[WHOLE((16,768)),WHOLE((4,768)),WHOLE((8,768))],
            out_specs=[WHOLE(A),WHOLE(A),WHOLE(B),WHOLE(B),WHOLE((n,768))],
            scratch_shapes=[V((2,768,1152),bf16),V((768,n),bf16),V((n,768),f32),V((768,1152),bf16),V((768,768),bf16),V((EXTRA,768),f32)]),
        compiler_params=pltpu.CompilerParams(vmem_limit_bytes=58<<20),
        name="back",
        cost_estimate=pl.CostEstimate(flops=2*n*768*768*7,transcendentals=n,bytes_accessed=n*768*24+768*3072*6),
    )(me,*keep,*recv,u,t,low,*qa,*qb,vec,eb,sums_two)

def feed_body(me, t,u,e0,e1,e2,e3,r0,r1,r2,r3,be,vec, keepR,sendR,keepE,sendE,eb,mid,low,sums, b2,b2T,we,wr,act,hg,am,ab,egs, *, rb):
    s=pl.program_id(0)
    n=t.shape[0]; fb=we.shape[1]
    @pl.when(s==0)
    def _():
        def one(i,_):
            rows=pl.ds(pl.multiple_of(i*rb,rb),rb)
            normed,_=norm_of(t[rows,:])
            b=(normed*vec[2:3,:]+vec[3:4,:]).astype(bf16)
            b2[rows,:]=b
            b2T[i]=b.T
            am[rows,:]=t[rows,:].astype(f32)+(vec[4:5,:]+vec[5:6,:])
            ab[rows,:]=jnp.zeros((rb,768),f32)
            return 0
        lax.fori_loop(0,n//rb,one,0)
    for i,e in enumerate((e0,e1,e2,e3)): we[rows_of(me,i,192),:]=e[...]
    for i,r in enumerate((r0,r1,r2,r3)):
        @pl.when(s==i)
        def _(): wr[...]=r[...]
    w_e=we[...]; w_r=wr[...]
    def one(i,bs):
        rows=pl.ds(pl.multiple_of(i*rb,rb),rb)
        h=dot(b2[rows,:],w_e)+be[0]
        ag=dot_nt(u[rows,:],w_r)
        cdf=0.5+0.5*lax.erf(h*0.7071067811865476)
        a=(h*cdf).astype(bf16)
        d=(ag*(cdf+h*(0.3989422804014327*jnp.exp(h*h*-0.5)))).astype(bf16)
        act[rows,:]=a; hg[rows,:]=d
        am[rows,:]+=dot(a,w_r)
        ab[rows,:]+=dot_nt(d,w_e)
        return bs+jnp.sum(d.astype(f32).reshape(rb//8,8,fb),axis=0)
    bs=lax.fori_loop(0,n//rb,one,jnp.zeros((8,fb),f32))
    eb[0]=jnp.sum(bs,axis=0,keepdims=True)
    g=dot_tn(act[...],u[...]).astype(bf16)
    @pl.when(s%2==0)
    def _(): keepR[0]=g
    @pl.when(s%2==1)
    def _(): sendR[0]=g
    x=dot(b2T[0],hg[0:rb,:])
    for i in range(1,n//rb): x=x+dot(b2T[i],hg[i*rb:(i+1)*rb,:])
    egs[...]=x.astype(bf16)
    for i in range(4): (keepE,sendE)[i%2][i//2]=egs[rows_of(me,i,192),:]
    @pl.when(s==3)
    def _():
        def fin(i,c):
            rows=pl.ds(pl.multiple_of(i*rb,rb),rb)
            mid[rows,:]=am[rows,:]
            normed,inv=norm_of(t[rows,:])
            b=ab[rows,:]
            low[rows,:]=u[rows,:].astype(f32)+norm_back(b,normed,inv,vec[2:3,:])
            return c[0]+jnp.sum(b*normed,axis=0,keepdims=True),c[1]+jnp.sum(b,axis=0,keepdims=True)
        z=jnp.zeros((1,768),f32)
        p,q=lax.fori_loop(0,n//rb,fin,(z,z))
        sums[...]=jnp.zeros_like(sums)
        sums[0:1,:]=p; sums[1:2,:]=q

def feed(me,t,u,eq,rq,be,vec,rb=256):
    n=t.shape[0]; fb=768
    S=jax.ShapeDtypeStruct; V=pltpu.VMEM
    def qa(s,me): return (me[0]^(s//2))*2+(me[1]^(s%2))
    R=pl.BlockSpec((1,768,768),lambda s,me:(s//2,0,0))
    E=pl.BlockSpec((2,192,fb),lambda s,me:(0,0,qa(s,me)))
    return pl.pallas_call(functools.partial(feed_body,rb=rb),
        out_shape=[S((2,768,768),bf16)]*2+[S((2,192,4*fb),bf16)]*2+[S((4,1,fb),f32),S((n,768),f32),S((n,768),f32),S((8,768),f32)],
        grid_spec=pltpu.PrefetchScalarGridSpec(num_scalar_prefetch=1,grid=(4,),
            in_specs=[WHOLE((n,768))]*2+[pl.BlockSpec((192,fb),lambda s,me:(0,qa(s,me)))]*4+[WHOLE((768,768))]*4+
              [pl.BlockSpec((1,1,fb),lambda s,me:(qa(s,me),0,0)),WHOLE((16,768))],
            out_specs=[R,R,E,E,pl.BlockSpec((1,1,fb),lambda s,me:(qa(s,me),0,0))]+[WHOLE((n,768))]*2+[WHOLE((8,768))],
            scratch_shapes=[V((n,768),bf16),V((n//rb,768,rb),bf16),V((768,fb),bf16),V((fb,768),bf16),V((n,fb),bf16),V((n,fb),bf16),
                            V((n,768),f32),V((n,768),f32),V((768,fb),bf16)]),
        compiler_params=pltpu.CompilerParams(vmem_limit_bytes=60<<20),
        name="feed",
        cost_estimate=pl.CostEstimate(flops=6*2*n*768*4*fb,transcendentals=n*4*fb*2,bytes_accessed=n*768*20+768*fb*32),
    )(me,t,u,*eq,*rq,be,vec)

def finish_body(*refs):
    pieces,(packed,output,vecs)=refs[:-3],refs[-3:]
    total=pieces[0][...].astype(f32)
    for p in pieces[1:]: total=total+p[...].astype(f32)
    packed[:,:1536]=total[:,:1536]
    packed[:,1536:]=total[:,1536+EXTRA:2304+EXTRA]
    output[...]=total[:,2304+EXTRA:]
    vecs[...]=total[:,1536:1536+EXTRA].T

def finish(pieces):
    r=pieces[0].shape[0]
    S=jax.ShapeDtypeStruct
    return pl.pallas_call(finish_body,out_shape=(S((r,2304),f32),S((r,768),f32),S((EXTRA,r),f32)),name="finish")(*pieces)

def swap(a, axis):
    return lax.ppermute(a, axis, [(0, 1), (1, 0)])


def shift(a, axis, size, step):
    return lax.ppermute(a, axis, [(i, (i + step) % size) for i in range(size)])


def pick(index, here, there):
    place = lax.broadcasted_iota(jnp.int32, (2,) + (1,) * here.ndim, 0)
    return jnp.where(place == index, here[None], there[None])


def after(value, *others):
    return lax.optimization_barrier((value,) + others)[0]


def gather_line(shard, m):
    z = lax.axis_index("z")
    pieces = [shard] + [shift(shard, "z", m, step) for step in range(1, m)]
    back = (z - lax.broadcasted_iota(jnp.int32, (m,) + (1,) * shard.ndim, 0)) % m
    line = pieces[0][None]
    for step in range(1, m):
        line = jnp.where(back == step, pieces[step][None], line)
    return line


def join(y, near, far):
    return jnp.moveaxis(pick(y, near, far), 0, 1).reshape((-1,) + near.shape[2:])


def halve(a, y, m):
    a = a.reshape(a.shape[:-2] + (m, 2, -1) + a.shape[-1:])
    mine = lax.dynamic_index_in_dim(a, y, a.ndim - 3, keepdims=False)
    other = lax.dynamic_index_in_dim(a, 1 - y, a.ndim - 3, keepdims=False)
    return add(mine, swap(other, "y"), bf16)


def wide(a):
    a = a.reshape(a.shape[:-1] + (4, -1))
    return jnp.moveaxis(a, -2, -3).reshape(a.shape[:-3] + (-1, a.shape[-1]))


def narrow(a):
    a = a.reshape(a.shape[:-2] + (4, -1, a.shape[-1]))
    return jnp.moveaxis(a, -3, -2).reshape(a.shape[:-3] + (a.shape[-2], -1))


def add(a, b, dtype):
    return (a.astype(f32) + b.astype(f32)).astype(dtype)


def scatter_line(line, m):
    z = lax.axis_index("z")
    total = lax.dynamic_index_in_dim(line, z, 0, keepdims=False).astype(f32)
    for step in range(1, m):
        part = lax.dynamic_index_in_dim(line, (z + step) % m, 0, keepdims=False)
        total = total + shift(part, "z", m, step).astype(f32)
    return total


def rotary(length):
    half = ROT // 2
    frequency = rope_base ** (-(jnp.arange(half, dtype=f32) * 2.0 / ROT))
    lane = jnp.arange(128, dtype=jnp.int32) % HD
    angles = jnp.arange(length, dtype=jnp.int32).astype(f32)[:, None] * jnp.tile(frequency, 16)[None, :]
    co, si = jnp.cos(angles), jnp.sin(angles)
    return jnp.stack(
        [
            jnp.where(lane < ROT, co, 1.0),
            jnp.where(lane < half, -si, 0.0),
            jnp.where((lane >= half) & (lane < ROT), si, 0.0),
        ]
    )


def exchange(mine, x):
    other = swap(lax.dynamic_index_in_dim(mine, 1 - x, 0, keepdims=False), "x")
    place = lax.broadcasted_iota(jnp.int32, (2, 1, 1), 0)
    return jnp.where(place == x, mine, other[None])


def shards(
    inputs,
    first_gain,
    first_shift,
    second_gain,
    second_shift,
    packed_weight,
    packed_bias,
    output_weight,
    output_bias,
    expand_weight,
    expand_bias,
    reduce_weight,
    reduce_bias,
    cotangent,
    *,
    m,
):
    x, c, y = (lax.axis_index(a) for a in "xcy")
    me = jnp.stack([x, c]).astype(jnp.int32)
    block, width = inputs.shape[1:]
    r = first_gain.shape[0]
    first = 2 * width + EXTRA
    other_tokens = swap(lax.dynamic_index_in_dim(inputs, 1 - x, 0, keepdims=False), "x")
    vectors = [first_gain, first_shift, second_gain, second_shift, output_bias, reduce_bias]
    shard = pack(packed_weight, output_weight, vectors, packed_bias, expand_bias)
    table = rotary(4 * block)
    line = gather_line(shard, m)
    pair_r = jnp.stack([reduce_weight, swap(reduce_weight, "x")])
    line_a, line_b = line[:, :, :first], line[:, :, first:]
    far_b = swap(line_b, "x")
    near_a = join(y, line_a, swap(line_a, "y"))
    near_b = join(y, line_b, swap(line_b, "y"))
    far_a = swap(after(near_a, table), "x")
    far_b = join(y, far_b, swap(far_b, "y"))
    qa = [near_a, swap(near_a, "c"), far_a, swap(far_a, "c")]
    qb = [near_b, swap(near_b, "c"), far_b, swap(far_b, "c")]

    line_e = gather_line(expand_weight, m)
    line_r = gather_line(pair_r, m)
    other_grads = swap(lax.dynamic_index_in_dim(cotangent, 1 - x, 0, keepdims=False), "x")
    side_r = swap(line_r, "y")
    near_e = join(y, line_e, swap(line_e, "y"))

    own, send, t, vec = project(me, inputs, other_tokens, qa, qb, table)
    got = swap(send, "c")
    gown, gsend, u = upstream_heads(after(me, own), cotangent, other_grads, qb)
    ggot = swap(gsend, "c")
    core = me[1:]
    operands = (own, got, gown, ggot, table)
    keep0, give0 = attention(core, *operands, 0)

    near_r, far_r = (join(y, line_r[:, i], side_r[:, i]) for i in range(2))
    far_e = swap(near_e, "x")
    eq = [near_e, swap(near_e, "c"), far_e, swap(far_e, "c")]
    rq = [near_r, swap(near_r, "c"), far_r, swap(far_r, "c")]
    be = vec[9:13].reshape(4, -1, r).transpose(1, 0, 2).reshape(4, 1, -1)
    keep_r, send_r, keep_e, send_e, eb, mid, low, sums_two = feed(me, after(t, keep0), u, eq, rq, be, vec)
    eb = eb.reshape(-1, 4, r).transpose(1, 0, 2).reshape(4, width)
    keep1, give1 = attention(after(core, mid), *operands, 1)
    sum_r = add(keep_r, swap(send_r, "c"), bf16)
    sum_e = add(keep_e, swap(send_e, "c"), bf16)
    keep2, give2 = attention(after(core, keep1, sum_r, sum_e), *operands, 2)
    sum_r = add(sum_r[0], swap(sum_r[1], "x"), bf16)
    sum_e = halve(sum_e, y, m)
    keep = [keep0, keep1, keep2]
    recv = [swap(give0, "c"), swap(give1, "c"), swap(give2, "c")]
    layer_out = layer_output(after(me, sum_r, sum_e, keep2), keep, recv, qb, mid)
    sum_r = halve(sum_r, y, m)
    sum_e = add(sum_e[0], swap(sum_e[1], "x"), bf16)
    feed_line = jnp.stack([wide(sum_e), sum_r], 1)
    keep_a, send_a, keep_b, send_b, input_grad = back(
        after(me, layer_out, feed_line), keep, recv, u, t, low, qa, qb, vec, eb, sums_two
    )
    total = scatter_line(feed_line, m)
    expand_grad, reduce_grad = narrow(total[0]), total[1]
    layer_out = exchange(layer_out.reshape(inputs.shape), x)
    sum_a = add(keep_a, swap(send_a, "c"), bf16)
    sum_b = add(keep_b, swap(send_b, "c"), bf16)
    input_grad = exchange(input_grad.reshape(inputs.shape), x)
    line_a = halve(add(sum_a[0], swap(sum_a[1], "x"), bf16), y, m)
    sum_b = halve(sum_b, y, m)
    line_b = add(sum_b[0], swap(sum_b[1], "x"), bf16)
    line = jnp.concatenate([line_a, line_b], 2)
    z = lax.axis_index("z")
    pieces = [lax.dynamic_index_in_dim(line, (z + step) % m, 0, keepdims=False) for step in range(m)]
    pieces[1:] = [shift(p, "z", m, step + 1) for step, p in enumerate(pieces[1:])]
    packed_grad, output_grad, v = finish(pieces)
    return (
        layer_out,
        input_grad,
        v[0],
        v[1],
        v[2],
        v[3],
        packed_grad,
        v[5:8],
        output_grad,
        v[4],
        expand_grad,
        v[8:12].reshape(-1),
        reduce_grad,
        v[4],
    )


def solution(mesh):
    shard = mesh.shape["shard"]
    m = shard // 2
    fine = Mesh(mesh.devices.reshape(2, 2, m, 2), ("x", "c", "z", "y"))
    every = ("x", "c", "z", "y")
    tokens = P(("z", "y"), ("x", "c"), None)
    vec, mat = P(every), P(every, None)
    in_specs = (tokens, vec, vec, vec, vec, mat, P(None, every), mat, vec, mat, vec, mat, vec, tokens)
    out_specs = (tokens, tokens, vec, vec, vec, vec, mat, P(None, every), mat, vec, mat, vec, mat, vec)

    def body(*args):
        return shards(*args, m=m)

    return jax.shard_map(body, mesh=fine, in_specs=in_specs, out_specs=out_specs, check_vma=False)
```

profile of v0, /device:TPU:0, one launch (start us, length us, event | category | flops | bytes accessed | tf_op | source)
XLA Modules:
  0.0 448.4 jit_solution(17473666573493145284)
XLA Ops:
  2.4 5.1 %collective-permute-start.1 = (bf16[24,3200]{1,0:T(8,128)(2,1)}, bf16[24,3200]{1,0:T(8,128)(2,1)S(1)}, u32[]{:S(2)}, u32[]{:S(2)}) collective-permute-start(bf16[24,3200]{1,0:T(8,128)(2,1)} %pack.1), channel_id=1, source_target_pairs={{0,6},{2,0},{4,2},{6,4},{1,7},{3,1},{5,3},{7,5},{8,14},{10,8},{12,... | collective-permute-start | bytes 460808 | tf_op jit(solution)/shard_map/ppermute | solution.py:433
  8.7 3.8 fusion.9
  12.6 8.3 %collective-permute-done.2 = bf16[24,3200]{1,0:T(8,128)(2,1)} collective-permute-done((bf16[24,3200]{1,0:T(8,128)(2,1)}, bf16[24,3200]{1,0:T(8,128)(2,1)}, u32[]{:S(2)}, u32[]{:S(2)}) %collective-permute-start.2) | collective-permute-done | bytes 153632 | tf_op jit(solution)/shard_map/ppermute | solution.py:433
  26.6 5.5 %collective-permute-done.4 = bf16[4,24,1664]{2,1,0:T(8,128)(2,1)} collective-permute-done((bf16[4,24,1664]{2,1,0:T(8,128)(2,1)S(1)}, bf16[4,24,1664]{2,1,0:T(8,128)(2,1)}, u32[]{:S(2)}, u32[]{:S(2)}) %collective-permute-start.4) | collective-permute-done | bytes 319520 | tf_op jit(solution)/shard_map/ppermute | solution.py:429
  38.7 16.9 %collective-permute-done.10 = bf16[4,24,1536]{2,1,0:T(8,128)(2,1)S(1)} collective-permute-done((bf16[4,24,1536]{2,1,0:T(8,128)(2,1)S(1)}, bf16[4,24,1536]{2,1,0:T(8,128)(2,1)S(1)}, u32[]{:S(2)}, u32[]{:S(2)}) %collective-permute-start.10) | collective-permute-done | bytes 294944 | tf_op jit(solution)/shard_map/ppermute | solution.py:429
  62.5 15.9 %collective-permute-done.23 = bf16[96,768]{1,0:T(8,128)(2,1)S(1)} collective-permute-done((bf16[96,768]{1,0:T(8,128)(2,1)S(1)}, bf16[96,768]{1,0:T(8,128)(2,1)S(1)}, u32[]{:S(2)}, u32[]{:S(2)}) %collective-permute-start.23) | collective-permute-done | bytes 147488 | tf_op jit(solution)/shard_map/ppermute | solution.py:429
  86.8 15.0 %project.1 = (bf16[3,1024,384]{2,1,0:T(8,128)(2,1)}, bf16[3,1024,384]{2,1,0:T(8,128)(2,1)}, bf16[1024,768]{1,0:T(8,128)(2,1)}, f32[16,768]{1,0:T(8,128)}) custom-call(s32[2]{0:T(128)} %pad_add_fusion.me, bf16[2,512,768]{2,1,0:T(8,128)(2,1)} %a.4, bf16[512,768]{1,0:T(8,128)(2,1)} %collective-permute-done.b, ...), custom_call_target="tpu_custom_call" | custom-call | flops 3623878656 | bytes 12582912 | tf_op jit(solution)/shard_map/project/pallas_call | solution.py:202
  105.8 16.4 %collective-permute-done.25 = bf16[2,96,768]{2,1,0:T(8,128)(2,1)S(1)} collective-permute-done((bf16[2,96,768]{2,1,0:T(8,128)(2,1)S(1)}, bf16[2,96,768]{2,1,0:T(8,128)(2,1)S(1)}, u32[]{:S(2)}, u32[]{:S(2)}) %collective-permute-start.25) | collective-permute-done | bytes 294944 | tf_op jit(solution)/shard_map/ppermute | solution.py:433
  124.8 6.3 %upstream.1 = (bf16[1024,384]{1,0:T(8,128)(2,1)}, bf16[1024,384]{1,0:T(8,128)(2,1)}, bf16[1024,768]{1,0:T(8,128)(2,1)}) custom-call(s32[2]{0:T(128)} %pad_add_fusion.me, bf16[2,512,768]{2,1,0:T(8,128)(2,1)} %a.5, bf16[512,768]{1,0:T(8,128)(2,1)} %collective-permute-done.14.b, bf16[192,1536]{1,0:T(8,128)(2,1)} %copy-done.2, bf16[192,1536]{1,0:T(8,128)(2,1)} %copy-done.9, ...), custom_call_target="tpu_custom_call" | custom-call | flops 1207959552 | bytes 5898240 | tf_op jit(solution)/shard_map/upstream/pallas_call | solution.py:229
  131.9 18.4 %collective-permute-done.27 = bf16[4,2,96,768]{3,2,0,1:T(8,128)(2,1)S(1)} collective-permute-done((bf16[4,2,96,768]{3,2,0,1:T(8,128)(2,1)S(1)}, bf16[4,2,96,768]{3,2,0,1:T(8,128)(2,1)S(1)}, u32[]{:S(2)}, u32[]{:S(2)}) %collective-permute-start.27) | collective-permute-done | bytes 1179680 | tf_op jit(solution)/shard_map/ppermute | solution.py:429
  155.9 29.9 %attention.3 = (bf16[4,1024,128]{2,1,0:T(8,128)(2,1)}, bf16[4,1024,128]{2,1,0:T(8,128)(2,1)}) custom-call(s32[1]{0:T(128)} %bitcast.1.c_ref, bf16[3,1024,384]{2,1,0:T(8,128)(2,1)} %get-tuple-element.52.own, bf16[3,1024,384]{2,1,0:T(8,128)(2,1)} %collective-permute-done.13.par, bf16[1024,384]{1,0:T(8,128)(2,1)} %get-tuple-element.55.gown, ...), custom_call_target="tpu_custom_call" | custom-call | flops 12884901888 | bytes 4194304 | tf_op jit(solution)/shard_map/attention/pallas_call | solution.py:117
  187.9 59.4 %feed.1 = (bf16[2,768,768]{2,1,0:T(8,128)(2,1)}, bf16[2,768,768]{2,1,0:T(8,128)(2,1)}, bf16[2,192,3072]{2,1,0:T(8,128)(2,1)}, bf16[2,192,3072]{2,1,0:T(8,128)(2,...) custom-call(s32[2]{0:T(128)} %pad_add_fusion.me, ...), custom_call_target="tpu_custom_call" | custom-call | flops 28991029248 | bytes 34603008 | tf_op jit(solution)/shard_map/feed/pallas_call | solution.py:401
  247.9 30.5 %attention.4 = (bf16[4,1024,128]{2,1,0:T(8,128)(2,1)}, bf16[4,1024,128]{2,1,0:T(8,128)(2,1)}) custom-call(s32[1]{0:T(128)} %bitcast.1.c_ref, bf16[3,1024,384]{2,1,0:T(8,128)(2,1)} %get-tuple-element.52.own, bf16[3,1024,384]{2,1,0:T(8,128)(2,1)} %collective-permute-done.13.par, bf16[1024,384]{1,0:T(8,128)(2,1)} %get-tuple-element.55.gown, ...), custom_call_target="tpu_custom_call" | custom-call | flops 12884901888 | bytes 4194304 | tf_op jit(solution)/shard_map/attention/pallas_call | solution.py:117
  287.0 30.0 %attention.5 = (bf16[4,1024,128]{2,1,0:T(8,128)(2,1)}, bf16[4,1024,128]{2,1,0:T(8,128)(2,1)}) custom-call(s32[1]{0:T(128)} %bitcast.1.c_ref, bf16[3,1024,384]{2,1,0:T(8,128)(2,1)} %get-tuple-element.52.own, bf16[3,1024,384]{2,1,0:T(8,128)(2,1)} %collective-permute-done.13.par, bf16[1024,384]{1,0:T(8,128)(2,1)} %get-tuple-element.55.gown, ...), custom_call_target="tpu_custom_call" | custom-call | flops 12884901888 | bytes 4194304 | tf_op jit(solution)/shard_map/attention/pallas_call | solution.py:117
  323.1 6.5 %layer_output.1 = bf16[1024,768]{1,0:T(8,128)(2,1)} custom-call(s32[2]{0:T(128)} %pad_add_fusion.me, bf16[4,1024,128]{2,1,0:T(8,128)(2,1)} %get-tuple-element.57.refs_0_, bf16[4,1024,128]{2,1,0:T(8,128)(2,1)} %get-tuple-element.67.refs_1_, bf16[4,1024,128]{2,1,0:T(8,128)(2,1)} %get-tuple-element.69.refs_2_, ...), custom_call_target="tpu_custom_call" | custom-call | flops 1207959552 | bytes 7471104 | tf_op jit(solution)/shard_map/layer_output/pallas_call | solution.py:255
  329.6 22.8 %back.1 = (bf16[2,192,1664]{2,1,0:T(8,128)(2,1)}, bf16[2,192,1664]{2,1,0:T(8,128)(2,1)}, bf16[2,192,1536]{2,1,0:T(8,128)(2,1)}, bf16[2,192,1536]{2,1,0:T(8,128)(2,1)}, bf16[1024,768]{1,0:T(8,128)(2,1)}) custom-call(s32[2]{0:T(128)} %pad_add_fusion.me, bf16[4,1024,128]{2,1,0:T(8,128)(2,1)} %get-tuple-element.57.refs_0_, ...), custom_call_target="tpu_custom_call" | custom-call | flops 8455716864 | bytes 33030144 | tf_op jit(solution)/shard_map/back/pallas_call | solution.py:327
  358.0 5.7 %collective-permute-start.50 = (bf16[2,96,768]{2,1,0:T(8,128)(2,1)S(1)}, bf16[2,96,768]{2,1,0:T(8,128)(2,1)S(1)}, u32[]{:S(2)}, u32[]{:S(2)}) collective-permute-start(bf16[2,96,768]{2,1,0:T(8,128)(2,1)S(1)} %get-tuple-element.86), channel_id=1, source_target_pairs={{0,2},{2,4},{4,6},{6,0},{1,3},{3,5},{5,7},{7,1},{8,10},{10,12},{12... | collective-permute-start | bytes 884744 | tf_op jit(solution)/shard_map/ppermute | solution.py:433
  363.7 11.0 %collective-permute-done.40 = bf16[512,768]{1,0:T(8,128)(2,1)S(1)} collective-permute-done((bf16[512,768]{1,0:T(8,128)(2,1)S(1)}, bf16[512,768]{1,0:T(8,128)(2,1)S(1)}, u32[]{:S(2)}, u32[]{:S(2)}) %collective-permute-start.40) | collective-permute-done | bytes 786464 | tf_op jit(solution)/shard_map/ppermute | solution.py:429
  374.7 4.6 %collective-permute-start.51 = (bf16[2,96,768]{2,1,0:T(8,128)(2,1)S(1)}, bf16[2,96,768]{2,1,0:T(8,128)(2,1)S(1)}, u32[]{:S(2)}, u32[]{:S(2)}) collective-permute-start(bf16[2,96,768]{2,1,0:T(8,128)(2,1)S(1)} %get-tuple-element.87), channel_id=1, source_target_pairs={{0,4},{2,6},{4,0},{6,2},{1,5},{3,7},{5,1},{7,3},{8,12},{10,14},{12... | collective-permute-start | bytes 884744 | tf_op jit(solution)/shard_map/ppermute | solution.py:433
  379.3 11.4 %collective-permute-done.37 = bf16[512,768]{1,0:T(8,128)(2,1)S(1)} collective-permute-done((bf16[512,768]{1,0:T(8,128)(2,1)S(1)}, bf16[512,768]{1,0:T(8,128)(2,1)S(1)}, u32[]{:S(2)}, u32[]{:S(2)}) %collective-permute-start.37) | collective-permute-done | bytes 786464 | tf_op jit(solution)/shard_map/ppermute | solution.py:429
  392.7 10.0 %collective-permute-done.52 = bf16[2,96,768]{2,1,0:T(8,128)(2,1)S(1)} collective-permute-done((bf16[2,96,768]{2,1,0:T(8,128)(2,1)S(1)}, bf16[2,96,768]{2,1,0:T(8,128)(2,1)S(1)}, u32[]{:S(2)}, u32[]{:S(2)}) %collective-permute-start.52) | collective-permute-done | bytes 294944 | tf_op jit(solution)/shard_map/ppermute | solution.py:433
  405.2 12.0 %collective-permute-done.45 = bf16[2,4,24,1536]{3,2,1,0:T(8,128)(2,1)S(1)} collective-permute-done((bf16[2,4,24,1536]{3,2,1,0:T(8,128)(2,1)S(1)}, bf16[2,4,24,1536]{3,2,1,0:T(8,128)(2,1)S(1)}, u32[]{:S(2)}, u32[]{:S(2)}) %collective-permute-start.45) | collective-permute-done | bytes 589856 | tf_op jit(solution)/shard_map/ppermute | solution.py:429
  417.9 3.4 collective-permute-done.42
  436.6 4.4 collective-permute-done.48.refs_2_
  (217 shorter events, 93.7 us)
Async XLA Ops:
  34.1 26.3 %collective-permute-start.6 = (bf16[192,1664]{1,0:T(8,128)(2,1)}, bf16[192,1664]{1,0:T(8,128)(2,1)}, u32[]{:S(2)}, u32[]{:S(2)}) collective-permute-start(bf16[192,1664]{1,0:T(8,128)(2,1)} %bitcast_select_fusion.3.refs_0_.refs_9_), channel_id=1, source_target_pairs={{0,16},{16,0},{1,17},{17,1},{2,18},{18,2},{3,19},{19,3},{4,20},{20... | collective-permute-start | bytes 1916936 | tf_op jit(solution)/shard_map/ppermute | solution.py:429
  37.1 23.2 %collective-permute-start.8 = (bf16[4,24,1536]{2,1,0:T(8,128)(2,1)S(1)}, bf16[4,24,1536]{2,1,0:T(8,128)(2,1)S(1)}, u32[]{:S(2)}, u32[]{:S(2)}) collective-permute-start(bf16[4,24,1536]{2,1,0:T(8,128)(2,1)S(1)} %slice.98), channel_id=1, source_target_pairs={{0,1},{1,0},{2,3},{3,2},{4,5},{5,4},{6,7},{7,6},{8,9},{9,8},{10,11... | collective-permute-start | bytes 884744 | tf_op jit(solution)/shard_map/ppermute | solution.py:429
  60.4 26.4 %collective-permute-start.7 = (bf16[192,1664]{1,0:T(8,128)(2,1)}, bf16[192,1664]{1,0:T(8,128)(2,1)}, u32[]{:S(2)}, u32[]{:S(2)}) collective-permute-start(bf16[192,1664]{1,0:T(8,128)(2,1)} %collective-permute-done.6.refs_2_.refs_11_), channel_id=1, source_target_pairs={{0,8},{8,0},{1,9},{9,1},{2,10},{10,2},{3,11},{11,3},{4,12},{12,4},... | collective-permute-start | bytes 1916936 | tf_op jit(solution)/shard_map/ppermute | solution.py:429
  86.8 35.4 %collective-permute-start.25 = (bf16[2,96,768]{2,1,0:T(8,128)(2,1)S(1)}, bf16[2,96,768]{2,1,0:T(8,128)(2,1)S(1)}, u32[]{:S(2)}, u32[]{:S(2)}) collective-permute-start(bf16[2,96,768]{2,1,0:T(8,128)(2,1)S(1)} %pad_maximum_fusion.2), channel_id=1, source_target_pairs={{0,4},{2,6},{4,0},{6,2},{1,5},{3,7},{5,1},{7,3},{8,12},{10,14},{12... | collective-permute-start | bytes 884744 | tf_op jit(solution)/shard_map/ppermute | solution.py:433
  103.4 52.5 %collective-permute-start.13 = (bf16[3,1024,384]{2,1,0:T(8,128)(2,1)}, bf16[3,1024,384]{2,1,0:T(8,128)(2,1)}, u32[]{:S(2)}, u32[]{:S(2)}) collective-permute-start(bf16[3,1024,384]{2,1,0:T(8,128)(2,1)} %get-tuple-element.53), channel_id=1, source_target_pairs={{0,8},{8,0},{1,9},{9,1},{2,10},{10,2},{3,11},{11,3},{4,12},{12,4},... | collective-permute-start | bytes 7077896 | tf_op jit(solution)/shard_map/ppermute | solution.py:429
  122.5 27.9 %collective-permute-start.27 = (bf16[4,2,96,768]{3,2,0,1:T(8,128)(2,1)S(1)}, bf16[4,2,96,768]{3,2,0,1:T(8,128)(2,1)S(1)}, u32[]{:S(2)}, u32[]{:S(2)}) collective-permute-start(bf16[4,2,96,768]{3,2,0,1:T(8,128)(2,1)S(1)} %select_select_fusion), channel_id=1, source_target_pairs={{0,1},{1,0},{2,3},{3,2},{4,5},{5,4},{6,7},{7,6},{8,9},{9,8},{10,11... | collective-permute-start | bytes 3538952 | tf_op jit(solution)/shard_map/ppermute | solution.py:429
  123.2 32.2 %collective-permute-start.21 = (bf16[192,3072]{1,0:T(8,128)(2,1)S(1)}, bf16[192,3072]{1,0:T(8,128)(2,1)}, u32[]{:S(2)}, u32[]{:S(2)}) collective-permute-start(bf16[192,3072]{1,0:T(8,128)(2,1)S(1)} %bitcast_select_fusion.2.e0), channel_id=1, source_target_pairs={{0,16},{16,0},{1,17},{17,1},{2,18},{18,2},{3,19},{19,3},{4,20},{20... | collective-permute-start | bytes 3538952 | tf_op jit(solution)/shard_map/ppermute | solution.py:429
  131.1 24.8 %collective-permute-start.15 = (bf16[1024,384]{1,0:T(8,128)(2,1)}, bf16[1024,384]{1,0:T(8,128)(2,1)}, u32[]{:S(2)}, u32[]{:S(2)}) collective-permute-start(bf16[1024,384]{1,0:T(8,128)(2,1)} %get-tuple-element.56), channel_id=1, source_target_pairs={{0,8},{8,0},{1,9},{9,1},{2,10},{10,2},{3,11},{11,3},{4,12},{12,4},... | collective-permute-start | bytes 2359304 | tf_op jit(solution)/shard_map/ppermute | solution.py:429
  131.3 54.5 %collective-permute-start.20 = (bf16[192,3072]{1,0:T(8,128)(2,1)S(1)}, bf16[192,3072]{1,0:T(8,128)(2,1)}, u32[]{:S(2)}, u32[]{:S(2)}) collective-permute-start(bf16[192,3072]{1,0:T(8,128)(2,1)S(1)} %bitcast_select_fusion.2.e0), channel_id=1, source_target_pairs={{0,8},{8,0},{1,9},{9,1},{2,10},{10,2},{3,11},{11,3},{4,12},{12,4},... | collective-permute-start | bytes 3538952 | tf_op jit(solution)/shard_map/ppermute | solution.py:429
  150.7 35.1 %collective-permute-start.28 = (bf16[768,768]{1,0:T(8,128)(2,1)S(1)}, bf16[768,768]{1,0:T(8,128)(2,1)}, u32[]{:S(2)}, u32[]{:S(2)}) collective-permute-start(bf16[768,768]{1,0:T(8,128)(2,1)S(1)} %get-tuple-element.108.r0), channel_id=1, source_target_pairs={{0,8},{8,0},{1,9},{9,1},{2,10},{10,2},{3,11},{11,3},{4,12},{12,4},... | collective-permute-start | bytes 3538952 | tf_op jit(solution)/shard_map/ppermute | solution.py:429
  155.4 30.5 %collective-permute-start.29 = (bf16[768,768]{1,0:T(8,128)(2,1)S(1)}, bf16[768,768]{1,0:T(8,128)(2,1)S(1)}, u32[]{:S(2)}, u32[]{:S(2)}) collective-permute-start(bf16[768,768]{1,0:T(8,128)(2,1)S(1)} %get-tuple-element.107.r2), channel_id=1, source_target_pairs={{0,8},{8,0},{1,9},{9,1},{2,10},{10,2},{3,11},{11,3},{4,12},{12,4},... | collective-permute-start | bytes 3538952 | tf_op jit(solution)/shard_map/ppermute | solution.py:429
  155.8 31.1 %collective-permute-start.22 = (bf16[192,3072]{1,0:T(8,128)(2,1)}, bf16[192,3072]{1,0:T(8,128)(2,1)S(1)}, u32[]{:S(2)}, u32[]{:S(2)}) collective-permute-start(bf16[192,3072]{1,0:T(8,128)(2,1)} %collective-permute-done.21.e2), channel_id=1, source_target_pairs={{0,8},{8,0},{1,9},{9,1},{2,10},{10,2},{3,11},{11,3},{4,12},{12,4},... | collective-permute-start | bytes 3538952 | tf_op jit(solution)/shard_map/ppermute | solution.py:429
  247.3 32.5 %collective-permute-start.30 = (bf16[2,768,768]{2,1,0:T(8,128)(2,1)}, bf16[2,768,768]{2,1,0:T(8,128)(2,1)}, u32[]{:S(2)}, u32[]{:S(2)}) collective-permute-start(bf16[2,768,768]{2,1,0:T(8,128)(2,1)} %get-tuple-element.62), channel_id=1, source_target_pairs={{0,8},{8,0},{1,9},{9,1},{2,10},{10,2},{3,11},{11,3},{4,12},{12,4},... | collective-permute-start | bytes 7077896 | tf_op jit(solution)/shard_map/ppermute | solution.py:429
  247.8 35.9 %collective-permute-start.32 = (bf16[2,192,3072]{2,1,0:T(8,128)(2,1)}, bf16[2,192,3072]{2,1,0:T(8,128)(2,1)}, u32[]{:S(2)}, u32[]{:S(2)}) collective-permute-start(bf16[2,192,3072]{2,1,0:T(8,128)(2,1)} %get-tuple-element.64), channel_id=1, source_target_pairs={{0,8},{8,0},{1,9},{9,1},{2,10},{10,2},{3,11},{11,3},{4,12},{12,4},... | collective-permute-start | bytes 7077896 | tf_op jit(solution)/shard_map/ppermute | solution.py:429
  278.4 44.7 %collective-permute-start.35 = (bf16[4,1024,128]{2,1,0:T(8,128)(2,1)}, bf16[4,1024,128]{2,1,0:T(8,128)(2,1)}, u32[]{:S(2)}, u32[]{:S(2)}) collective-permute-start(bf16[4,1024,128]{2,1,0:T(8,128)(2,1)} %get-tuple-element.72), channel_id=1, source_target_pairs={{0,8},{8,0},{1,9},{9,1},{2,10},{10,2},{3,11},{11,3},{4,12},{12,4},... | collective-permute-start | bytes 3145736 | tf_op jit(solution)/shard_map/ppermute | solution.py:429
  278.8 44.3 %collective-permute-start.34 = (bf16[4,1024,128]{2,1,0:T(8,128)(2,1)}, bf16[4,1024,128]{2,1,0:T(8,128)(2,1)}, u32[]{:S(2)}, u32[]{:S(2)}) collective-permute-start(bf16[4,1024,128]{2,1,0:T(8,128)(2,1)} %get-tuple-element.71), channel_id=1, source_target_pairs={{0,8},{8,0},{1,9},{9,1},{2,10},{10,2},{3,11},{11,3},{4,12},{12,4},... | collective-permute-start | bytes 3145736 | tf_op jit(solution)/shard_map/ppermute | solution.py:429
  282.2 35.0 %collective-permute-start.31 = (bf16[768,768]{1,0:T(8,128)(2,1)S(1)}, bf16[768,768]{1,0:T(8,128)(2,1)S(1)}, u32[]{:S(2)}, u32[]{:S(2)}) collective-permute-start(bf16[768,768]{1,0:T(8,128)(2,1)S(1)} %slice_bitcast_fusion), channel_id=1, source_target_pairs={{0,16},{16,0},{1,17},{17,1},{2,18},{18,2},{3,19},{19,3},{4,20},{20... | collective-permute-start | bytes 3538952 | tf_op jit(solution)/shard_map/ppermute | solution.py:429
  286.4 33.4 %collective-permute-start.33 = (bf16[2,4,24,3072]{3,2,1,0:T(8,128)(2,1)S(1)}, bf16[2,4,24,3072]{3,2,1,0:T(8,128)(2,1)}, u32[]{:S(2)}, u32[]{:S(2)}) collective-permute-start(bf16[2,4,24,3072]{3,2,1,0:T(8,128)(2,1)S(1)} %dynamic-slice_bitcast_fusion), channel_id=1, source_target_pairs={{0,1},{1,0},{2,3},{3,2},{4,5},{5,4},{6,7},{7,6},{8,9},{9,8},{10,11... | collective-permute-start | bytes 3538952 | tf_op jit(solution)/shard_map/ppermute | solution.py:429
  318.3 38.4 %collective-permute-start.39 = (bf16[4,96,768]{2,1,0:T(8,128)(2,1)}, bf16[4,96,768]{2,1,0:T(8,128)(2,1)}, u32[]{:S(2)}, u32[]{:S(2)}) collective-permute-start(bf16[4,96,768]{2,1,0:T(8,128)(2,1)} %dynamic-slice_bitcast_fusion.6), channel_id=1, source_target_pairs={{0,1},{1,0},{2,3},{3,2},{4,5},{5,4},{6,7},{7,6},{8,9},{9,8},{10,11... | collective-permute-start | bytes 1769480 | tf_op jit(solution)/shard_map/ppermute | solution.py:429
  321.5 33.4 %collective-permute-start.38 = (bf16[4,24,3072]{2,1,0:T(8,128)(2,1)S(1)}, bf16[4,24,3072]{2,1,0:T(8,128)(2,1)S(1)}, u32[]{:S(2)}, u32[]{:S(2)}) collective-permute-start(bf16[4,24,3072]{2,1,0:T(8,128)(2,1)S(1)} %slice_bitcast_fusion.4), channel_id=1, source_target_pairs={{0,16},{16,0},{1,17},{17,1},{2,18},{18,2},{3,19},{19,3},{4,20},{20... | collective-permute-start | bytes 1769480 | tf_op jit(solution)/shard_map/ppermute | solution.py:429
  352.5 50.4 %collective-permute-start.44 = (bf16[2,192,1536]{2,1,0:T(8,128)(2,1)}, bf16[2,192,1536]{2,1,0:T(8,128)(2,1)S(1)}, u32[]{:S(2)}, u32[]{:S(2)}) collective-permute-start(bf16[2,192,1536]{2,1,0:T(8,128)(2,1)} %get-tuple-element.82), channel_id=1, source_target_pairs={{0,8},{8,0},{1,9},{9,1},{2,10},{10,2},{3,11},{11,3},{4,12},{12,4},... | collective-permute-start | bytes 3538952 | tf_op jit(solution)/shard_map/ppermute | solution.py:429
  352.5 51.3 %collective-permute-start.41 = (bf16[2,192,1664]{2,1,0:T(8,128)(2,1)}, bf16[2,192,1664]{2,1,0:T(8,128)(2,1)S(1)}, u32[]{:S(2)}, u32[]{:S(2)}) collective-permute-start(bf16[2,192,1664]{2,1,0:T(8,128)(2,1)} %get-tuple-element.80), channel_id=1, source_target_pairs={{0,8},{8,0},{1,9},{9,1},{2,10},{10,2},{3,11},{11,3},{4,12},{12,4},... | collective-permute-start | bytes 3833864 | tf_op jit(solution)/shard_map/ppermute | solution.py:429
  354.9 35.8 %collective-permute-start.37 = (bf16[512,768]{1,0:T(8,128)(2,1)S(1)}, bf16[512,768]{1,0:T(8,128)(2,1)S(1)}, u32[]{:S(2)}, u32[]{:S(2)}) collective-permute-start(bf16[512,768]{1,0:T(8,128)(2,1)S(1)} %dynamic-slice_bitcast_fusion.2), channel_id=1, source_target_pairs={{0,16},{16,0},{1,17},{17,1},{2,18},{18,2},{3,19},{19,3},{4,20},{20... | collective-permute-start | bytes 2359304 | tf_op jit(solution)/shard_map/ppermute | solution.py:429
  358.0 34.7 %collective-permute-start.50 = (bf16[2,96,768]{2,1,0:T(8,128)(2,1)S(1)}, bf16[2,96,768]{2,1,0:T(8,128)(2,1)S(1)}, u32[]{:S(2)}, u32[]{:S(2)}) collective-permute-start(bf16[2,96,768]{2,1,0:T(8,128)(2,1)S(1)} %get-tuple-element.86), channel_id=1, source_target_pairs={{0,2},{2,4},{4,6},{6,0},{1,3},{3,5},{5,7},{7,1},{8,10},{10,12},{12... | collective-permute-start | bytes 884744 | tf_op jit(solution)/shard_map/ppermute | solution.py:433
  (55 other events, 767.3 us)
where the time goes:
time: 457 us; the launch traced here: 448 us
  Pallas kernels  204 us (45%)
  waiting for transfers between devices  142 us (31%)
  starting transfers between devices  55.2 us (12%)
  other arithmetic  23.8 us (5%)
  local copies, waits for them, and re-layouts  21.4 us (5%)
    ppermute x38, waiting for transfers between devices, swap(): return lax.ppermute(a, axis, [(0, 1), (1, 0)])  102 us
    pallas_call x3, Pallas kernels, attention(): pl.pallas_call(functools.partial(attn_body, blk=blk, length=length), out_...  90.4 us
    pallas_call x1, Pallas kernels, feed(): pl.pallas_call(functools.partial(feed_body, rb=rb), out_shape=[S((2, 768,...  59.4 us
    ppermute x15, waiting for transfers between devices, shift(): return lax.ppermute(a, axis, [(i, (i + step) % size) for i in range(size)])  40.7 us
    ppermute x15, starting transfers between devices, shift(): return lax.ppermute(a, axis, [(i, (i + step) % size) for i in range(size)])  28.1 us
    ppermute x38, starting transfers between devices, swap(): return lax.ppermute(a, axis, [(0, 1), (1, 0)])  27 us
    pallas_call x1, Pallas kernels, back(): pl.pallas_call(back_body, out_shape=(S(A, bf16), S(A, bf16), S(B, bf16),...  22.8 us
    pallas_call x1, Pallas kernels, project(): pl.pallas_call(proj_body, out_shape=(S((3, n, 384), bf16), S((3, n, 384),...  15 us
  transfers between devices with their start and end apart: 53, of which 16 were waited for; matrix products, arithmetic and copies ran while one was open for 7% of the time, Pallas kernels for 31%

commit v1 on v0

--- a/solution.py
+++ b/solution.py
@@ -15,7 +15,7 @@
     sgn=-1.0 if back else 1.0
     return v*tab[0]+sgn*(pltpu.roll(v,120,1)*tab[1]+pltpu.roll(v,8,1)*tab[2])
 
-def attn_body(c_ref, own, par, gown, gpar, tab, keep, send, qs, ks, gs, vs, qT, gT, kT, vT, es, oT, dqT, dk, dv, *, blk, length):
+def attn_body(c_ref, own, par, gown, gpar, tab, keep, send, qs, ks, gs, vs, qT, gT, kT, vT, es0, es1, eb, dss, mx0, mx1, oT, dqT, dk, dv, *, blk, length, ch):
     c=c_ref[0]
     nb=length//blk
     lane=lax.broadcasted_iota(jnp.int32,(1,128),1)
@@ -31,72 +31,89 @@
             dT[2*h+1-c]=b.T
     dk[...]=jnp.zeros_like(dk); dv[...]=jnp.zeros_like(dv)
     kk=HD**-0.5*1.4426950408889634
-    rowi=lax.broadcasted_iota(jnp.int32,(blk,blk),0)
-    coli=lax.broadcasted_iota(jnp.int32,(blk,blk),1)
-    allowed=rowi<=coli
     zero64=jnp.zeros((HD,blk),bf16)
-
-    def block(i,_):
-        qt=qT[i]; gt=gT[i]
-        qh=[jnp.concatenate([qt[:HD],zero64],0),jnp.concatenate([zero64,qt[HD:]],0)]
-        gh=[jnp.concatenate([gt[:HD],zero64],0),jnp.concatenate([zero64,gt[HD:]],0)]
+    nc=blk//ch
+
+    def masked(x): return [jnp.concatenate([x[:HD],zero64],0),jnp.concatenate([zero64,x[HD:]],0)]
+    def top(x): return jnp.max(x.reshape(x.shape[0]//8,8,blk),axis=0)
+
+    def score_diag(i,qh,es,mx):
+        coli=lax.broadcasted_iota(jnp.int32,(ch,blk),1)
+        rowi=lax.broadcasted_iota(jnp.int32,(ch,blk),0)
+        for a in range(nc):
+            rows=pl.ds(pl.multiple_of(i*blk+a*ch,ch),ch)
+            k=ks[rows,:]
+            for h in range(2):
+                s=jnp.where(rowi+a*ch<=coli,dot(k,qh[h]),-1e30)
+                es[h,rows,:]=s
+                mx[h]=jnp.maximum(mx[h],top(s))
+
+    mx0[...]=jnp.full_like(mx0,-1e30)
+    score_diag(0,masked(qT[0]),es0,mx0)
+
+    def block(i,es,mx,es_next,mx_next):
+        i1=jnp.minimum(i+1,nb-1)
         rows=pl.ds(pl.multiple_of(i*blk,blk),blk)
-        q=qs[rows,:]; g=gs[rows,:]
+        q1=masked(qT[i1])
+        mk=[jnp.max(mx[h],axis=0,keepdims=True)*kk for h in range(2)]
+        mx_next[...]=jnp.full((2,8,blk),-1e30,f32)
+        oT[...]=jnp.zeros_like(oT)
+        def sB(j,l):
+            out=list(l)
+            for a in range(nc):
+                kr=pl.ds(pl.multiple_of(j*blk+a*ch,ch),ch)
+                k=ks[kr,:]
+                for h in range(2):
+                    s=dot(k,q1[h])
+                    es_next[h,kr,:]=s
+                    mx_next[h]=jnp.maximum(mx_next[h],top(s))
+                    e=jnp.exp2(es[h,kr,:]*kk-mk[h])
+                    es[h,kr,:]=e
+                    eb[h,kr,:]=e.astype(bf16)
+                    out[h]=out[h]+jnp.sum(e.reshape(ch//8,8,blk),axis=0)
+            jr=pl.ds(pl.multiple_of(j*blk,blk),blk)
+            for h in range(2):
+                hs=slice(h*HD,(h+1)*HD)
+                oT[hs,:]+=dot(vT[j,hs,:],eb[h,jr,:])
+            return tuple(out)
+        z=jnp.zeros((8,blk),f32)
+        l=lax.fori_loop(0,i+1,sB,(z,z))
+        @pl.when(i<nb-1)
+        def _(): score_diag(i1,q1,es_next,mx_next)
+        r=[1.0/jnp.sum(t,axis=0,keepdims=True) for t in l]
+        gt=gT[i]
+        sc=jnp.concatenate([(gt[h*HD:(h+1)*HD].astype(f32)*r[h]) for h in range(2)],0).astype(bf16)
+        gh=masked(sc)
+        o=[oT[h*HD:(h+1)*HD,:]*r[h] for h in range(2)]
+        D=[jnp.sum(o[h]*sc[h*HD:(h+1)*HD].astype(f32),axis=0,keepdims=True) for h in range(2)]
+        oT[...]=jnp.concatenate(o,0)
+        g=sc.T
+        q=qs[rows,:]
         zq=jnp.zeros_like(q)
         qm=[jnp.where(first,q,zq),jnp.where(first,zq,q)]
         gm=[jnp.where(first,g,zq),jnp.where(first,zq,g)]
-        def sA(j,m):
-            kr=pl.ds(pl.multiple_of(j*blk,blk),blk)
-            k=ks[kr,:]
-            out=[]
-            for h in range(2):
-                s=dot(k,qh[h])
-                es[h,kr,:]=s
-                out.append(jnp.maximum(m[h],jnp.max(s.reshape(blk//8,8,blk),axis=0)))
-            return tuple(out)
-        m0=jnp.full((8,blk),-1e30,f32)
-        k=ks[rows,:]
-        m=[]
-        for h in range(2):
-            s=jnp.where(allowed,dot(k,qh[h]),-1e30)
-            es[h,rows,:]=s
-            m.append(jnp.max(s.reshape(blk//8,8,blk),axis=0))
-        m=lax.fori_loop(0,i,sA,tuple(m))
-        mk=[jnp.max(t,axis=0,keepdims=True)*kk for t in m]
-        oT[...]=jnp.zeros_like(oT)
-        def sB(j,l):
-            kr=pl.ds(pl.multiple_of(j*blk,blk),blk)
-            out=[]
-            for h in range(2):
-                e=jnp.exp2(es[h,kr,:]*kk-mk[h])
-                es[h,kr,:]=e
-                out.append(l[h]+jnp.sum(e.reshape(blk//8,8,blk),axis=0))
-                oT[h*HD:(h+1)*HD,:]+=dot(vT[j,h*HD:(h+1)*HD,:],e.astype(bf16))
-            return tuple(out)
-        z=jnp.zeros((8,blk),f32)
-        l=lax.fori_loop(0,i+1,sB,(z,z))
-        r=[1.0/jnp.sum(t,axis=0,keepdims=True) for t in l]
-        o=[oT[h*HD:(h+1)*HD,:]*r[h] for h in range(2)]
-        D=[jnp.sum(o[h]*gt[h*HD:(h+1)*HD].astype(f32),axis=0,keepdims=True) for h in range(2)]
-        oT[...]=jnp.concatenate(o,0)
         dqT[...]=jnp.zeros_like(dqT)
         def sC(j,_):
-            kr=pl.ds(pl.multiple_of(j*blk,blk),blk)
-            v=vs[kr,:]
-            pb=[];db=[]
+            for a in range(nc):
+                kr=pl.ds(pl.multiple_of(j*blk+a*ch,ch),ch)
+                v=vs[kr,:]
+                ds=[(es[h,kr,:]*(dot(v,gh[h])-D[h])).astype(bf16) for h in range(2)]
+                for h in range(2): dss[h,a*ch:(a+1)*ch,:]=ds[h]
+                dv[kr,:]+=dot(eb[0,kr,:],gm[0])+dot(eb[1,kr,:],gm[1])
+                dk[kr,:]+=dot(ds[0],qm[0])+dot(ds[1],qm[1])
             for h in range(2):
-                p=es[h,kr,:]*r[h]
-                ds=(p*(dot(v,gh[h])-D[h])).astype(bf16)
-                pb.append(p.astype(bf16)); db.append(ds)
-                dqT[h*HD:(h+1)*HD,:]+=dot(kT[j,h*HD:(h+1)*HD,:],ds)
-            dv[kr,:]+=dot(pb[0],gm[0])+dot(pb[1],gm[1])
-            dk[kr,:]+=dot(db[0],qm[0])+dot(db[1],qm[1])
+                hs=slice(h*HD,(h+1)*HD)
+                dqT[hs,:]+=dot(kT[j,hs,:],dss[h])
             return 0
         lax.fori_loop(0,i+1,sC,0)
         qs[rows,:]=(dqT[...].T*HD**-0.5).astype(bf16)
         gs[rows,:]=oT[...].T.astype(bf16)
+
+    def two(i,_):
+        block(2*i,es0,mx0,es1,mx1)
+        block(2*i+1,es1,mx1,es0,mx0)
         return 0
-    lax.fori_loop(0,nb,block,0)
+    lax.fori_loop(0,nb//2,two,0)
     for h in range(nb//2):
         for who,ref in ((c,keep),(1-c,send)):
             rows=pl.ds(pl.multiple_of((2*h+who)*blk,blk),blk)
@@ -107,7 +124,7 @@
             ref[2,dst,:]=turn((dk[rows,:]*HD**-0.5).astype(bf16).astype(f32),t,True).astype(bf16)
             ref[3,dst,:]=dv[rows,:].astype(bf16)
 
-def attention(c, own, par, gown, gpar, tab, pair, npair=1, blk=512):
+def attention(c, own, par, gown, gpar, tab, pair, npair=1, blk=512, ch=512):
     rows=own.shape[1]; length=2*rows
     nb=length//blk
     spec=pl.BlockSpec((3,rows,128),lambda p,c:(0,0,p+pair))
@@ -115,14 +132,15 @@
     ospec=pl.BlockSpec((4,rows,128),lambda p,c:(0,0,p))
     V=pltpu.VMEM
     return pl.pallas_call(
-        functools.partial(attn_body,blk=blk,length=length),
+        functools.partial(attn_body,blk=blk,length=length,ch=ch),
         out_shape=(jax.ShapeDtypeStruct((4,rows,128*npair),bf16),)*2,
         grid_spec=pltpu.PrefetchScalarGridSpec(num_scalar_prefetch=1,grid=(npair,),
             in_specs=[spec,spec,gspec,gspec,pl.BlockSpec((3,length,128),lambda p,c:(0,0,0),pipeline_mode=pl.Buffered(1))],
             out_specs=[ospec,ospec],
             scratch_shapes=[V((length,128),bf16)]*4+[V((nb,128,blk),bf16)]*4+
-              [V((2,length,blk),f32),V((128,blk),f32),V((128,blk),f32),V((length,128),f32),V((length,128),f32)]),
-        compiler_params=pltpu.CompilerParams(vmem_limit_bytes=56<<20),
+              [V((2,length,blk),f32),V((2,length,blk),f32),V((2,length,blk),bf16),V((2,blk,blk),bf16),V((2,8,blk),f32),V((2,8,blk),f32),
+               V((128,blk),f32),V((128,blk),f32),V((length,128),f32),V((length,128),f32)]),
+        compiler_params=pltpu.CompilerParams(vmem_limit_bytes=58<<20),
         name="attention",
         cost_estimate=pl.CostEstimate(flops=int(6*2*length*length//2*HD*2*npair*4),transcendentals=length*length*npair,bytes_accessed=16*rows*128*2*npair),
     )(c,own,par,gown,gpar,tab)
@@ -175,7 +193,7 @@
 
 def proj_body(me, a, b, *refs):
     qa,qb=refs[:4],refs[4:8]
-    tab,keep,send,t,vec,ws,ex=refs[8:]
+    tab,keep,send,t,vec,ws,ex,st=refs[8:]
     i=pl.program_id(0)
     @pl.when(i==0)
     def _():
@@ -185,18 +203,26 @@
             ws[rows,1536:]=qb[n][...]
             ex[rows,:]=qa[n][:,1536:].astype(f32)
         vec[...]=ex[...].T[:16,:]
-    x=jnp.where(i//2==me[0],a[0],b[...])
+    x=jnp.where(i==me[0],a[0],b[...])
     t[...]=x
     normed,_=norm_of(x)
     b1=(normed*vec[0:1,:]+vec[1:2,:]).astype(bf16)
-    tb=[tab[n] for n in range(3)]
-    for j in range(3):
-        v=dot(b1,ws[:,j*768:(j+1)*768])+vec[6+j:7+j,:]
-        if j<2: v=jnp.concatenate([turn(v[:,g*128:(g+1)*128],tb,False) for g in range(6)],1)
-        split(me[1],v.astype(bf16),keep.at[j],send.at[j],384)
-
-def project(me,mine,other,qa,qb,tab,rb=256):
-    n=2*other.shape[0]; per=n//2//rb
+    half=x.shape[0]//2
+    rows=[slice(r*half,(r+1)*half) for r in range(2)]
+    vs=[[dot(b1[r,:],ws[:,j*768:(j+1)*768])+vec[6+j:7+j,:] for r in rows] for j in range(3)]
+    for r in range(2):
+        tb=[tab[n,rows[r],:] for n in range(3)]
+        for j in range(2):
+            for g in range(6): st[j,rows[r],g*128:(g+1)*128]=turn(vs[j][r][:,g*128:(g+1)*128],tb,False).astype(bf16)
+        st[2,rows[r],:]=vs[2][r].astype(bf16)
+    for k in range(2):
+        @pl.when(me[1]==k)
+        def _():
+            keep[...]=st[:,:,k*384:(k+1)*384]
+            send[...]=st[:,:,(1-k)*384:(2-k)*384]
+
+def project(me,mine,other,qa,qb,tab):
+    n=2*other.shape[0]; rb=n//2; per=1
     S=jax.ShapeDtypeStruct
     out=pl.BlockSpec((3,rb,384),lambda i,me:(0,i,0))
     return pl.pallas_call(proj_body,
@@ -206,7 +232,7 @@
               [WHOLE(w.shape) for w in qa]+[WHOLE((w.shape[0],768)) for w in qb]+
               [pl.BlockSpec((3,rb,128),lambda i,me:(0,(2*(i//per)+me[1])*per+i%per,0))],
             out_specs=(out,out,pl.BlockSpec((rb,768),lambda i,me:(i,0)),pl.BlockSpec((16,768),lambda i,me:(0,0))),
-            scratch_shapes=[pltpu.VMEM((768,2304),bf16),pltpu.VMEM((768,EXTRA),f32)]),
+            scratch_shapes=[pltpu.VMEM((768,2304),bf16),pltpu.VMEM((768,EXTRA),f32),pltpu.VMEM((3,rb,768),bf16)]),
         compiler_params=pltpu.CompilerParams(vmem_limit_bytes=56<<20),
         name="project",
         cost_estimate=pl.CostEstimate(flops=2*n*768*2304,transcendentals=n,bytes_accessed=n*768*10+768*3072*2),
@@ -218,12 +244,13 @@
     @pl.when(i==0)
     def _():
         for n in range(4): ws[rows_of(me,n,qb[n].shape[0]),:]=qb[n][...]
-    x=jnp.where(i//2==me[0],a[0],b[...])
+    x=jnp.where(i==me[0],a[0],b[...])
     u[...]=x
-    split(me[1],dot_nt(x,ws[...]).astype(bf16),keep,send,384)
-
-def upstream_heads(me,mine,other,qb,rb=256):
-    n=2*other.shape[0]; per=n//2//rb
+    half=x.shape[0]//2
+    split(me[1],jnp.concatenate([dot_nt(x[:half],ws[...]),dot_nt(x[half:],ws[...])],0).astype(bf16),keep,send,384)
+
+def upstream_heads(me,mine,other,qb):
+    n=2*other.shape[0]; rb=n//2; per=1
     S=jax.ShapeDtypeStruct
     out=pl.BlockSpec((rb,384),lambda i,me:(i,0))
     return pl.pallas_call(upst_body,
@@ -243,13 +270,15 @@
     @pl.when(pl.program_id(0)==0)
     def _():
         for n in range(4): wos[rows_of(me,n,qb[n].shape[0]),:]=qb[n][...]
-    acc=mid[...]
-    for g,a in ((0,ka),(1,ra)):
-        rows=pl.ds(pl.multiple_of((me[1]^g)*384,384),384)
-        acc=acc+dot(jnp.concatenate([r[0] for r in a],1),wos[rows,:])
-    out[...]=acc.astype(bf16)
-
-def layer_output(me,keep,recv,qb,mid,rb=256):
+    half=mid.shape[0]//2
+    for r in (slice(0,half),slice(half,2*half)):
+        acc=mid[r,:]
+        for g,a in ((0,ka),(1,ra)):
+            rows=pl.ds(pl.multiple_of((me[1]^g)*384,384),384)
+            acc=acc+dot(jnp.concatenate([p[0,r,:] for p in a],1),wos[rows,:])
+        out[r,:]=acc.astype(bf16)
+
+def layer_output(me,keep,recv,qb,mid,rb=512):
     n=mid.shape[0]
     a=pl.BlockSpec((1,rb,128),lambda i,me:(0,i,0))
     return pl.pallas_call(outl_body,
@@ -336,7 +365,7 @@
         cost_estimate=pl.CostEstimate(flops=2*n*768*768*7,transcendentals=n,bytes_accessed=n*768*24+768*3072*6),
     )(me,*keep,*recv,u,t,low,*qa,*qb,vec,eb,sums_two)
 
-def feed_body(me, t,u,e0,e1,e2,e3,r0,r1,r2,r3,be,vec, keepR,sendR,keepE,sendE,eb,mid,low,sums, b2,b2T,we,wr,act,hg,am,ab,egs, *, rb):
+def feed_body(me, t,u,e0,e1,e2,e3,r0,r1,r2,r3,be,vec, keepR,sendR,keepE,sendE,eb,mid,low,sums, b2,b2T,we,wr,act,hg,am,ab,egs,rgs, *, rb):
     s=pl.program_id(0)
     n=t.shape[0]; fb=we.shape[1]
     @pl.when(s==0)
@@ -355,28 +384,27 @@
     for i,r in enumerate((r0,r1,r2,r3)):
         @pl.when(s==i)
         def _(): wr[...]=r[...]
-    w_e=we[...]; w_r=wr[...]
     def one(i,bs):
         rows=pl.ds(pl.multiple_of(i*rb,rb),rb)
-        h=dot(b2[rows,:],w_e)+be[0]
-        ag=dot_nt(u[rows,:],w_r)
+        h=dot(b2[rows,:],we[...])+be[0]
+        ag=dot_nt(u[rows,:],wr[...])
         cdf=0.5+0.5*lax.erf(h*0.7071067811865476)
         a=(h*cdf).astype(bf16)
         d=(ag*(cdf+h*(0.3989422804014327*jnp.exp(h*h*-0.5)))).astype(bf16)
         act[rows,:]=a; hg[rows,:]=d
-        am[rows,:]+=dot(a,w_r)
-        ab[rows,:]+=dot_nt(d,w_e)
+        am[rows,:]+=dot(act[rows,:],wr[...])
+        ab[rows,:]+=dot_nt(hg[rows,:],we[...])
         return bs+jnp.sum(d.astype(f32).reshape(rb//8,8,fb),axis=0)
     bs=lax.fori_loop(0,n//rb,one,jnp.zeros((8,fb),f32))
     eb[0]=jnp.sum(bs,axis=0,keepdims=True)
-    g=dot_tn(act[...],u[...]).astype(bf16)
-    @pl.when(s%2==0)
-    def _(): keepR[0]=g
-    @pl.when(s%2==1)
-    def _(): sendR[0]=g
+    rgs[...]=dot_tn(act[...],u[...]).astype(bf16)
     x=dot(b2T[0],hg[0:rb,:])
     for i in range(1,n//rb): x=x+dot(b2T[i],hg[i*rb:(i+1)*rb,:])
     egs[...]=x.astype(bf16)
+    @pl.when(s%2==0)
+    def _(): keepR[0]=rgs[...]
+    @pl.when(s%2==1)
+    def _(): sendR[0]=rgs[...]
     for i in range(4): (keepE,sendE)[i%2][i//2]=egs[rows_of(me,i,192),:]
     @pl.when(s==3)
     def _():
@@ -392,7 +420,7 @@
         sums[...]=jnp.zeros_like(sums)
         sums[0:1,:]=p; sums[1:2,:]=q
 
-def feed(me,t,u,eq,rq,be,vec,rb=256):
+def feed(me,t,u,eq,rq,be,vec,rb=512):
     n=t.shape[0]; fb=768
     S=jax.ShapeDtypeStruct; V=pltpu.VMEM
     def qa(s,me): return (me[0]^(s//2))*2+(me[1]^(s%2))
@@ -405,25 +433,39 @@
               [pl.BlockSpec((1,1,fb),lambda s,me:(qa(s,me),0,0)),WHOLE((16,768))],
             out_specs=[R,R,E,E,pl.BlockSpec((1,1,fb),lambda s,me:(qa(s,me),0,0))]+[WHOLE((n,768))]*2+[WHOLE((8,768))],
             scratch_shapes=[V((n,768),bf16),V((n//rb,768,rb),bf16),V((768,fb),bf16),V((fb,768),bf16),V((n,fb),bf16),V((n,fb),bf16),
-                            V((n,768),f32),V((n,768),f32),V((768,fb),bf16)]),
+                            V((n,768),f32),V((n,768),f32),V((768,fb),bf16),V((fb,768),bf16)]),
         compiler_params=pltpu.CompilerParams(vmem_limit_bytes=60<<20),
         name="feed",
         cost_estimate=pl.CostEstimate(flops=6*2*n*768*4*fb,transcendentals=n*4*fb*2,bytes_accessed=n*768*20+768*fb*32),
     )(me,t,u,*eq,*rq,be,vec)
 
 def finish_body(*refs):
-    pieces,(packed,output,vecs)=refs[:-3],refs[-3:]
-    total=pieces[0][...].astype(f32)
-    for p in pieces[1:]: total=total+p[...].astype(f32)
-    packed[:,:1536]=total[:,:1536]
-    packed[:,1536:]=total[:,1536+EXTRA:2304+EXTRA]
-    output[...]=total[:,2304+EXTRA:]
-    vecs[...]=total[:,1536:1536+EXTRA].T
-
-def finish(pieces):
+    pieces,(packed,output,expand,reduce_,*vecs)=refs[:-11],refs[-11:]
+    count=len(pieces)//2
+    r=packed.shape[0]
+    def total(ps,*at):
+        s=ps[0][at].astype(f32)
+        for p in ps[1:]: s=s+p[at].astype(f32)
+        return s
+    s=total(pieces[:count],Ellipsis)
+    packed[:,:1536]=s[:,:1536]
+    packed[:,1536:]=s[:,1536+EXTRA:2304+EXTRA]
+    output[...]=s[:,2304+EXTRA:]
+    v=s[:,1536:1536+EXTRA].T
+    for i in range(5): vecs[i][...]=v[i,:]
+    vecs[5][...]=v[5:8,:]
+    vecs[6][...]=jnp.concatenate([v[8+i:9+i,:] for i in range(4)],1)[0,:]
+    e=total(pieces[count:],0)
+    for i in range(4): expand[:,i*768:(i+1)*768]=e[i*r:(i+1)*r,:]
+    reduce_[...]=total(pieces[count:],1)
+
+def finish(pieces,feed_pieces):
     r=pieces[0].shape[0]
     S=jax.ShapeDtypeStruct
-    return pl.pallas_call(finish_body,out_shape=(S((r,2304),f32),S((r,768),f32),S((EXTRA,r),f32)),name="finish")(*pieces)
+    o=pl.pallas_call(finish_body,out_shape=[S((r,2304),f32),S((r,768),f32),S((r,3072),f32),S((4*r,768),f32)]+[S((r,),f32)]*5+
+        [S((3,r),f32),S((4*r,),f32)],name="finish")(*pieces,*feed_pieces)
+    return o[:4],o[4:9],o[9],o[10]
+
 
 def swap(a, axis):
     return lax.ppermute(a, axis, [(0, 1), (1, 0)])
@@ -468,22 +510,14 @@
     return jnp.moveaxis(a, -2, -3).reshape(a.shape[:-3] + (-1, a.shape[-1]))
 
 
-def narrow(a):
-    a = a.reshape(a.shape[:-2] + (4, -1, a.shape[-1]))
-    return jnp.moveaxis(a, -3, -2).reshape(a.shape[:-3] + (a.shape[-2], -1))
-
-
 def add(a, b, dtype):
     return (a.astype(f32) + b.astype(f32)).astype(dtype)
 
 
-def scatter_line(line, m):
+def line_pieces(line, m):
     z = lax.axis_index("z")
-    total = lax.dynamic_index_in_dim(line, z, 0, keepdims=False).astype(f32)
-    for step in range(1, m):
-        part = lax.dynamic_index_in_dim(line, (z + step) % m, 0, keepdims=False)
-        total = total + shift(part, "z", m, step).astype(f32)
-    return total
+    pieces = [lax.dynamic_index_in_dim(line, (z + step) % m, 0, keepdims=False) for step in range(m)]
+    return pieces[:1] + [shift(p, "z", m, step + 1) for step, p in enumerate(pieces[1:])]
 
 
 def rotary(length):
@@ -579,22 +613,19 @@
     sum_e = add(sum_e[0], swap(sum_e[1], "x"), bf16)
     feed_line = jnp.stack([wide(sum_e), sum_r], 1)
     keep_a, send_a, keep_b, send_b, input_grad = back(
-        after(me, layer_out, feed_line), keep, recv, u, t, low, qa, qb, vec, eb, sums_two
+        after(me, layer_out), keep, recv, u, t, low, qa, qb, vec, eb, sums_two
     )
-    total = scatter_line(feed_line, m)
-    expand_grad, reduce_grad = narrow(total[0]), total[1]
+    feed_pieces = line_pieces(feed_line, m)
     layer_out = exchange(layer_out.reshape(inputs.shape), x)
     sum_a = add(keep_a, swap(send_a, "c"), bf16)
     sum_b = add(keep_b, swap(send_b, "c"), bf16)
-    input_grad = exchange(input_grad.reshape(inputs.shape), x)
     line_a = halve(add(sum_a[0], swap(sum_a[1], "x"), bf16), y, m)
     sum_b = halve(sum_b, y, m)
     line_b = add(sum_b[0], swap(sum_b[1], "x"), bf16)
+    input_grad = exchange(after(input_grad, layer_out).reshape(inputs.shape), x)
     line = jnp.concatenate([line_a, line_b], 2)
-    z = lax.axis_index("z")
-    pieces = [lax.dynamic_index_in_dim(line, (z + step) % m, 0, keepdims=False) for step in range(m)]
-    pieces[1:] = [shift(p, "z", m, step + 1) for step, p in enumerate(pieces[1:])]
-    packed_grad, output_grad, v = finish(pieces)
+    mats, v, packed_vec, expand_vec = finish(line_pieces(line, m), feed_pieces)
+    packed_grad, output_grad, expand_grad, reduce_grad = mats
     return (
         layer_out,
         input_grad,
@@ -603,11 +634,11 @@
         v[2],
         v[3],
         packed_grad,
-        v[5:8],
+        packed_vec,
         output_grad,
         v[4],
         expand_grad,
-        v[8:12].reshape(-1),
+        expand_vec,
         reduce_grad,
         v[4],
     )

time: 457 us -> 431 us (0.943)
  Pallas kernels: 204 us -> 179 us
    pallas_call x1, Pallas kernels: 59.4 us -> 47.2 us  [feed(): pl.pallas_call(functools.partial(feed_body, rb=rb), out_shape=[S((2, 768,...]
    ppermute x38, waiting for transfers between devices: 102 us -> 111 us  [swap(): return lax.ppermute(a, axis, [(0, 1), (1, 0)])]
    pallas_call x4, Pallas kernels: 92.4 us -> 84.8 us  [the longest x3 82.3 us: attention(): pl.pallas_call(functools.partial(attn_body, blk=blk, length=length, ch=ch...]
    ppermute x15, waiting for transfers between devices: 40.7 us -> 33.6 us  [shift(): return lax.ppermute(a, axis, [(i, (i + step) % size) for i in range(size)])]
  transfers between devices with their start and end apart: 53 -> 53, of which waited for: 16 -> 13; matrix products, arithmetic and copies ran while one was open for 7% -> 8% of each run, Pallas kernels for 31% -> 30%
where the time goes in v1:
time: 431 us; the launch traced here: 423 us
  Pallas kernels  179 us (42%)
  waiting for transfers between devices  145 us (34%)
  starting transfers between devices  53.6 us (12%)
  other arithmetic  26.4 us (6%)
  local copies, waits for them, and re-layouts  17.3 us (4%)
    ppermute x38, waiting for transfers between devices, swap(): return lax.ppermute(a, axis, [(0, 1), (1, 0)])  111 us
    pallas_call x3, Pallas kernels, attention(): pl.pallas_call(functools.partial(attn_body, blk=blk, length=length, ch=ch...  82.3 us
    pallas_call x1, Pallas kernels, feed(): pl.pallas_call(functools.partial(feed_body, rb=rb), out_shape=[S((2, 768,...  47.2 us
    ppermute x15, waiting for transfers between devices, shift(): return lax.ppermute(a, axis, [(i, (i + step) % size) for i in range(size)])  33.6 us
    ppermute x15, starting transfers between devices, shift(): return lax.ppermute(a, axis, [(i, (i + step) % size) for i in range(size)])  28 us
    ppermute x38, starting transfers between devices, swap(): return lax.ppermute(a, axis, [(0, 1), (1, 0)])  25.5 us
    pallas_call x1, Pallas kernels, back(): pl.pallas_call(back_body, out_shape=(S(A, bf16), S(A, bf16), S(B, bf16),...  23.2 us
    pallas_call x1, Pallas kernels, project(): pl.pallas_call(proj_body, out_shape=(S((3, n, 384), bf16), S((3, n, 384),...  11 us
  transfers between devices with their start and end apart: 53, of which 13 were waited for; matrix products, arithmetic and copies ran while one was open for 8% of the time, Pallas kernels for 30%

profile of v1, /device:TPU:0, one launch (start us, length us, event | category | flops | bytes accessed | tf_op | source)
XLA Modules:
  0.0 423.0 jit_solution(17362213598982792318)
XLA Ops:
  2.4 5.1 %collective-permute-start.1 = (bf16[24,3200]{1,0:T(8,128)(2,1)}, bf16[24,3200]{1,0:T(8,128)(2,1)S(1)}, u32[]{:S(2)}, u32[]{:S(2)}) collective-permute-start(bf16[24,3200]{1,0:T(8,128)(2,1)} %pack.1), channel_id=1, source_target_pairs={{0,6},{2,0},{4,2},{6,4},{1,7},{3,1},{5,3},{7,5},{8,14},{10,8},{12,... | collective-permute-start | bytes 460808 | tf_op jit(solution)/shard_map/ppermute | solution.py:475
  8.7 3.8 fusion.9
  12.6 8.3 %collective-permute-done.2 = bf16[24,3200]{1,0:T(8,128)(2,1)} collective-permute-done((bf16[24,3200]{1,0:T(8,128)(2,1)}, bf16[24,3200]{1,0:T(8,128)(2,1)}, u32[]{:S(2)}, u32[]{:S(2)}) %collective-permute-start.2) | collective-permute-done | bytes 153632 | tf_op jit(solution)/shard_map/ppermute | solution.py:475
  26.6 5.5 %collective-permute-done.4 = bf16[4,24,1664]{2,1,0:T(8,128)(2,1)} collective-permute-done((bf16[4,24,1664]{2,1,0:T(8,128)(2,1)S(1)}, bf16[4,24,1664]{2,1,0:T(8,128)(2,1)}, u32[]{:S(2)}, u32[]{:S(2)}) %collective-permute-start.4) | collective-permute-done | bytes 319520 | tf_op jit(solution)/shard_map/ppermute | solution.py:471
  38.7 16.9 %collective-permute-done.10 = bf16[4,24,1536]{2,1,0:T(8,128)(2,1)S(1)} collective-permute-done((bf16[4,24,1536]{2,1,0:T(8,128)(2,1)S(1)}, bf16[4,24,1536]{2,1,0:T(8,128)(2,1)S(1)}, u32[]{:S(2)}, u32[]{:S(2)}) %collective-permute-start.10) | collective-permute-done | bytes 294944 | tf_op jit(solution)/shard_map/ppermute | solution.py:471
  63.5 14.8 %collective-permute-done.23 = bf16[96,768]{1,0:T(8,128)(2,1)S(1)} collective-permute-done((bf16[96,768]{1,0:T(8,128)(2,1)S(1)}, bf16[96,768]{1,0:T(8,128)(2,1)S(1)}, u32[]{:S(2)}, u32[]{:S(2)}) %collective-permute-start.23) | collective-permute-done | bytes 147488 | tf_op jit(solution)/shard_map/ppermute | solution.py:471
  85.1 11.0 %project.1 = (bf16[3,1024,384]{2,1,0:T(8,128)(2,1)}, bf16[3,1024,384]{2,1,0:T(8,128)(2,1)}, bf16[1024,768]{1,0:T(8,128)(2,1)}, f32[16,768]{1,0:T(8,128)}) custom-call(s32[2]{0:T(128)} %pad_add_fusion.me, bf16[2,512,768]{2,1,0:T(8,128)(2,1)} %a.4, bf16[512,768]{1,0:T(8,128)(2,1)} %collective-permute-done.b, ...), custom_call_target="tpu_custom_call" | custom-call | flops 3623878656 | bytes 12582912 | tf_op jit(solution)/shard_map/project/pallas_call | solution.py:228
  99.7 20.8 %collective-permute-done.25 = bf16[2,96,768]{2,1,0:T(8,128)(2,1)S(1)} collective-permute-done((bf16[2,96,768]{2,1,0:T(8,128)(2,1)S(1)}, bf16[2,96,768]{2,1,0:T(8,128)(2,1)S(1)}, u32[]{:S(2)}, u32[]{:S(2)}) %collective-permute-start.25) | collective-permute-done | bytes 294944 | tf_op jit(solution)/shard_map/ppermute | solution.py:475
  123.1 5.5 %upstream.1 = (bf16[1024,384]{1,0:T(8,128)(2,1)}, bf16[1024,384]{1,0:T(8,128)(2,1)}, bf16[1024,768]{1,0:T(8,128)(2,1)}) custom-call(s32[2]{0:T(128)} %pad_add_fusion.me, bf16[2,512,768]{2,1,0:T(8,128)(2,1)} %a.5, bf16[512,768]{1,0:T(8,128)(2,1)} %collective-permute-done.14.b, bf16[192,1536]{1,0:T(8,128)(2,1)} %copy-done.2, bf16[192,1536]{1,0:T(8,128)(2,1)} %copy-done.11, ...), custom_call_target="tpu_custom_call" | custom-call | flops 1207959552 | bytes 5898240 | tf_op jit(solution)/shard_map/upstream/pallas_call | solution.py:256
  129.4 19.3 %collective-permute-done.27 = bf16[4,2,96,768]{3,2,0,1:T(8,128)(2,1)S(1)} collective-permute-done((bf16[4,2,96,768]{3,2,0,1:T(8,128)(2,1)S(1)}, bf16[4,2,96,768]{3,2,0,1:T(8,128)(2,1)S(1)}, u32[]{:S(2)}, u32[]{:S(2)}) %collective-permute-start.27) | collective-permute-done | bytes 1179680 | tf_op jit(solution)/shard_map/ppermute | solution.py:471
  154.2 27.2 %attention.3 = (bf16[4,1024,128]{2,1,0:T(8,128)(2,1)}, bf16[4,1024,128]{2,1,0:T(8,128)(2,1)}) custom-call(s32[1]{0:T(128)} %bitcast.1.c_ref, bf16[3,1024,384]{2,1,0:T(8,128)(2,1)} %get-tuple-element.61.own, bf16[3,1024,384]{2,1,0:T(8,128)(2,1)} %collective-permute-done.13.par, bf16[1024,384]{1,0:T(8,128)(2,1)} %get-tuple-element.64.gown, ...), custom_call_target="tpu_custom_call" | custom-call | flops 12884901888 | bytes 4194304 | tf_op jit(solution)/shard_map/attention/pallas_call | solution.py:134
  183.5 47.2 %feed.1 = (bf16[2,768,768]{2,1,0:T(8,128)(2,1)}, bf16[2,768,768]{2,1,0:T(8,128)(2,1)}, bf16[2,192,3072]{2,1,0:T(8,128)(2,1)}, bf16[2,192,3072]{2,1,0:T(8,128)(2,...) custom-call(s32[2]{0:T(128)} %pad_add_fusion.me, ...), custom_call_target="tpu_custom_call" | custom-call | flops 28991029248 | bytes 34603008 | tf_op jit(solution)/shard_map/feed/pallas_call | solution.py:429
  231.3 27.5 %attention.4 = (bf16[4,1024,128]{2,1,0:T(8,128)(2,1)}, bf16[4,1024,128]{2,1,0:T(8,128)(2,1)}) custom-call(s32[1]{0:T(128)} %bitcast.1.c_ref, bf16[3,1024,384]{2,1,0:T(8,128)(2,1)} %get-tuple-element.61.own, bf16[3,1024,384]{2,1,0:T(8,128)(2,1)} %collective-permute-done.13.par, bf16[1024,384]{1,0:T(8,128)(2,1)} %get-tuple-element.64.gown, ...), custom_call_target="tpu_custom_call" | custom-call | flops 12884901888 | bytes 4194304 | tf_op jit(solution)/shard_map/attention/pallas_call | solution.py:134
  268.4 27.5 %attention.5 = (bf16[4,1024,128]{2,1,0:T(8,128)(2,1)}, bf16[4,1024,128]{2,1,0:T(8,128)(2,1)}) custom-call(s32[1]{0:T(128)} %bitcast.1.c_ref, bf16[3,1024,384]{2,1,0:T(8,128)(2,1)} %get-tuple-element.61.own, bf16[3,1024,384]{2,1,0:T(8,128)(2,1)} %collective-permute-done.13.par, bf16[1024,384]{1,0:T(8,128)(2,1)} %get-tuple-element.64.gown, ...), custom_call_target="tpu_custom_call" | custom-call | flops 12884901888 | bytes 4194304 | tf_op jit(solution)/shard_map/attention/pallas_call | solution.py:134
  304.3 5.9 %layer_output.1 = bf16[1024,768]{1,0:T(8,128)(2,1)} custom-call(s32[2]{0:T(128)} %pad_add_fusion.me, bf16[4,1024,128]{2,1,0:T(8,128)(2,1)} %get-tuple-element.66.refs_0_, bf16[4,1024,128]{2,1,0:T(8,128)(2,1)} %get-tuple-element.76.refs_1_, bf16[4,1024,128]{2,1,0:T(8,128)(2,1)} %get-tuple-element.78.refs_2_, ...), custom_call_target="tpu_custom_call" | custom-call | flops 1207959552 | bytes 7471104 | tf_op jit(solution)/shard_map/layer_output/pallas_call | solution.py:284
  310.1 23.2 %back.1 = (bf16[2,192,1664]{2,1,0:T(8,128)(2,1)}, bf16[2,192,1664]{2,1,0:T(8,128)(2,1)}, bf16[2,192,1536]{2,1,0:T(8,128)(2,1)}, bf16[2,192,1536]{2,1,0:T(8,128)(2,1)}, bf16[1024,768]{1,0:T(8,128)(2,1)}) custom-call(s32[2]{0:T(128)} %pad_add_fusion.me, bf16[4,1024,128]{2,1,0:T(8,128)(2,1)} %get-tuple-element.66.refs_0_, ...), custom_call_target="tpu_custom_call" | custom-call | flops 8455716864 | bytes 33030144 | tf_op jit(solution)/shard_map/back/pallas_call | solution.py:356
  336.9 5.6 %collective-permute-start.50 = (bf16[2,96,768]{2,1,0:T(8,128)(2,1)S(1)}, bf16[2,96,768]{2,1,0:T(8,128)(2,1)S(1)}, u32[]{:S(2)}, u32[]{:S(2)}) collective-permute-start(bf16[2,96,768]{2,1,0:T(8,128)(2,1)S(1)} %get-tuple-element.106), channel_id=1, source_target_pairs={{0,2},{2,4},{4,6},{6,0},{1,3},{3,5},{5,7},{7,1},{8,10},{10,12},{12... | collective-permute-start | bytes 884744 | tf_op jit(solution)/shard_map/ppermute | solution.py:475
  342.5 11.1 %collective-permute-done.37 = bf16[512,768]{1,0:T(8,128)(2,1)S(1)} collective-permute-done((bf16[512,768]{1,0:T(8,128)(2,1)S(1)}, bf16[512,768]{1,0:T(8,128)(2,1)S(1)}, u32[]{:S(2)}, u32[]{:S(2)}) %collective-permute-start.37) | collective-permute-done | bytes 786464 | tf_op jit(solution)/shard_map/ppermute | solution.py:471
  358.1 13.2 %collective-permute-done.43 = bf16[2,4,24,1536]{3,2,1,0:T(8,128)(2,1)S(1)} collective-permute-done((bf16[2,4,24,1536]{3,2,1,0:T(8,128)(2,1)S(1)}, bf16[2,4,24,1536]{3,2,1,0:T(8,128)(2,1)S(1)}, u32[]{:S(2)}, u32[]{:S(2)}) %collective-permute-start.43) | collective-permute-done | bytes 589856 | tf_op jit(solution)/shard_map/ppermute | solution.py:471
  372.4 15.6 %collective-permute-done.40 = bf16[192,1664]{1,0:T(8,128)(2,1)S(1)} collective-permute-done((bf16[192,1664]{1,0:T(8,128)(2,1)S(1)}, bf16[192,1664]{1,0:T(8,128)(2,1)S(1)}, u32[]{:S(2)}, u32[]{:S(2)}) %collective-permute-start.40) | collective-permute-done | bytes 639008 | tf_op jit(solution)/shard_map/ppermute | solution.py:471
  388.7 6.5 %collective-permute-done.44 = bf16[4,24,1536]{2,1,0:T(8,128)(2,1)S(1)} collective-permute-done((bf16[4,24,1536]{2,1,0:T(8,128)(2,1)S(1)}, bf16[4,24,1536]{2,1,0:T(8,128)(2,1)S(1)}, u32[]{:S(2)}, u32[]{:S(2)}) %collective-permute-start.44) | collective-permute-done | bytes 294944 | tf_op jit(solution)/shard_map/ppermute | solution.py:471
  395.8 6.4 %collective-permute-done.41 = bf16[4,24,1664]{2,1,0:T(8,128)(2,1)S(1)} collective-permute-done((bf16[4,24,1664]{2,1,0:T(8,128)(2,1)S(1)}, bf16[4,24,1664]{2,1,0:T(8,128)(2,1)S(1)}, u32[]{:S(2)}, u32[]{:S(2)}) %collective-permute-start.41) | collective-permute-done | bytes 319520 | tf_op jit(solution)/shard_map/ppermute | solution.py:471
  403.0 5.6 %collective-permute-start.45 = (bf16[24,3200]{1,0:T(8,128)(2,1)S(1)}, bf16[24,3200]{1,0:T(8,128)(2,1)S(1)}, u32[]{:S(2)}, u32[]{:S(2)}) collective-permute-start(bf16[24,3200]{1,0:T(8,128)(2,1)S(1)} %get-tuple-element.114), channel_id=1, source_target_pairs={{0,2},{2,4},{4,6},{6,0},{1,3},{3,5},{5,7},{7,1},{8,10},{10,12},{12... | collective-permute-start | bytes 460808 | tf_op jit(solution)/shard_map/ppermute | solution.py:475
  413.5 4.5 %collective-permute-done.46.refs_2_ = bf16[24,3200]{1,0:T(8,128)(2,1)S(1)} collective-permute-done((bf16[24,3200]{1,0:T(8,128)(2,1)S(1)}, bf16[24,3200]{1,0:T(8,128)(2,1)S(1)}, u32[]{:S(2)}, u32[]{:S(2)}) %collective-permute-start.46) | collective-permute-done | bytes 153632 | tf_op jit(solution)/shard_map/ppermute | solution.py:475
  (219 shorter events, 83.3 us)
Async XLA Ops:
  34.1 26.0 %collective-permute-start.6 = (bf16[192,1664]{1,0:T(8,128)(2,1)}, bf16[192,1664]{1,0:T(8,128)(2,1)}, u32[]{:S(2)}, u32[]{:S(2)}) collective-permute-start(bf16[192,1664]{1,0:T(8,128)(2,1)} %bitcast_select_fusion.3.refs_0_.refs_9_), channel_id=1, source_target_pairs={{0,16},{16,0},{1,17},{17,1},{2,18},{18,2},{3,19},{19,3},{4,20},{20... | collective-permute-start | bytes 1916936 | tf_op jit(solution)/shard_map/ppermute | solution.py:471
  60.0 25.1 %collective-permute-start.7 = (bf16[192,1664]{1,0:T(8,128)(2,1)}, bf16[192,1664]{1,0:T(8,128)(2,1)}, u32[]{:S(2)}, u32[]{:S(2)}) collective-permute-start(bf16[192,1664]{1,0:T(8,128)(2,1)} %collective-permute-done.6.refs_2_.refs_11_), channel_id=1, source_target_pairs={{0,8},{8,0},{1,9},{9,1},{2,10},{10,2},{3,11},{11,3},{4,12},{12,4},... | collective-permute-start | bytes 1916936 | tf_op jit(solution)/shard_map/ppermute | solution.py:471
  85.1 35.4 %collective-permute-start.25 = (bf16[2,96,768]{2,1,0:T(8,128)(2,1)S(1)}, bf16[2,96,768]{2,1,0:T(8,128)(2,1)S(1)}, u32[]{:S(2)}, u32[]{:S(2)}) collective-permute-start(bf16[2,96,768]{2,1,0:T(8,128)(2,1)S(1)} %pad_maximum_fusion.1), channel_id=1, source_target_pairs={{0,4},{2,6},{4,0},{6,2},{1,5},{3,7},{5,1},{7,3},{8,12},{10,14},{12... | collective-permute-start | bytes 884744 | tf_op jit(solution)/shard_map/ppermute | solution.py:475
  97.3 56.9 %collective-permute-start.13 = (bf16[3,1024,384]{2,1,0:T(8,128)(2,1)}, bf16[3,1024,384]{2,1,0:T(8,128)(2,1)}, u32[]{:S(2)}, u32[]{:S(2)}) collective-permute-start(bf16[3,1024,384]{2,1,0:T(8,128)(2,1)} %get-tuple-element.62), channel_id=1, source_target_pairs={{0,8},{8,0},{1,9},{9,1},{2,10},{10,2},{3,11},{11,3},{4,12},{12,4},... | collective-permute-start | bytes 7077896 | tf_op jit(solution)/shard_map/ppermute | solution.py:471
  98.2 24.9 %collective-permute-start.14 = (bf16[512,768]{1,0:T(8,128)(2,1)S(1)}, bf16[512,768]{1,0:T(8,128)(2,1)}, u32[]{:S(2)}, u32[]{:S(2)}) collective-permute-start(bf16[512,768]{1,0:T(8,128)(2,1)S(1)} %dynamic-slice_bitcast_fusion.3), channel_id=1, source_target_pairs={{0,16},{16,0},{1,17},{17,1},{2,18},{18,2},{3,19},{19,3},{4,20},{20... | collective-permute-start | bytes 2359304 | tf_op jit(solution)/shard_map/ppermute | solution.py:471
  120.8 27.9 %collective-permute-start.27 = (bf16[4,2,96,768]{3,2,0,1:T(8,128)(2,1)S(1)}, bf16[4,2,96,768]{3,2,0,1:T(8,128)(2,1)S(1)}, u32[]{:S(2)}, u32[]{:S(2)}) collective-permute-start(bf16[4,2,96,768]{3,2,0,1:T(8,128)(2,1)S(1)} %select_select_fusion), channel_id=1, source_target_pairs={{0,1},{1,0},{2,3},{3,2},{4,5},{5,4},{6,7},{7,6},{8,9},{9,8},{10,11... | collective-permute-start | bytes 3538952 | tf_op jit(solution)/shard_map/ppermute | solution.py:471
  121.5 32.2 %collective-permute-start.21 = (bf16[192,3072]{1,0:T(8,128)(2,1)S(1)}, bf16[192,3072]{1,0:T(8,128)(2,1)}, u32[]{:S(2)}, u32[]{:S(2)}) collective-permute-start(bf16[192,3072]{1,0:T(8,128)(2,1)S(1)} %bitcast_select_fusion.2.e0), channel_id=1, source_target_pairs={{0,16},{16,0},{1,17},{17,1},{2,18},{18,2},{3,19},{19,3},{4,20},{20... | collective-permute-start | bytes 3538952 | tf_op jit(solution)/shard_map/ppermute | solution.py:471
  128.6 25.6 %collective-permute-start.15 = (bf16[1024,384]{1,0:T(8,128)(2,1)}, bf16[1024,384]{1,0:T(8,128)(2,1)}, u32[]{:S(2)}, u32[]{:S(2)}) collective-permute-start(bf16[1024,384]{1,0:T(8,128)(2,1)} %get-tuple-element.65), channel_id=1, source_target_pairs={{0,8},{8,0},{1,9},{9,1},{2,10},{10,2},{3,11},{11,3},{4,12},{12,4},... | collective-permute-start | bytes 2359304 | tf_op jit(solution)/shard_map/ppermute | solution.py:471
  128.8 52.6 %collective-permute-start.20 = (bf16[192,3072]{1,0:T(8,128)(2,1)S(1)}, bf16[192,3072]{1,0:T(8,128)(2,1)}, u32[]{:S(2)}, u32[]{:S(2)}) collective-permute-start(bf16[192,3072]{1,0:T(8,128)(2,1)S(1)} %bitcast_select_fusion.2.e0), channel_id=1, source_target_pairs={{0,8},{8,0},{1,9},{9,1},{2,10},{10,2},{3,11},{11,3},{4,12},{12,4},... | collective-permute-start | bytes 3538952 | tf_op jit(solution)/shard_map/ppermute | solution.py:471
  149.0 32.4 %collective-permute-start.28 = (bf16[768,768]{1,0:T(8,128)(2,1)S(1)}, bf16[768,768]{1,0:T(8,128)(2,1)}, u32[]{:S(2)}, u32[]{:S(2)}) collective-permute-start(bf16[768,768]{1,0:T(8,128)(2,1)S(1)} %get-tuple-element.120.r0), channel_id=1, source_target_pairs={{0,8},{8,0},{1,9},{9,1},{2,10},{10,2},{3,11},{11,3},{4,12},{12,4},... | collective-permute-start | bytes 3538952 | tf_op jit(solution)/shard_map/ppermute | solution.py:471
  153.7 27.8 %collective-permute-start.29 = (bf16[768,768]{1,0:T(8,128)(2,1)S(1)}, bf16[768,768]{1,0:T(8,128)(2,1)S(1)}, u32[]{:S(2)}, u32[]{:S(2)}) collective-permute-start(bf16[768,768]{1,0:T(8,128)(2,1)S(1)} %get-tuple-element.119.r2), channel_id=1, source_target_pairs={{0,8},{8,0},{1,9},{9,1},{2,10},{10,2},{3,11},{11,3},{4,12},{12,4},... | collective-permute-start | bytes 3538952 | tf_op jit(solution)/shard_map/ppermute | solution.py:471
  154.2 28.3 %collective-permute-start.22 = (bf16[192,3072]{1,0:T(8,128)(2,1)}, bf16[192,3072]{1,0:T(8,128)(2,1)S(1)}, u32[]{:S(2)}, u32[]{:S(2)}) collective-permute-start(bf16[192,3072]{1,0:T(8,128)(2,1)} %collective-permute-done.21.e2), channel_id=1, source_target_pairs={{0,8},{8,0},{1,9},{9,1},{2,10},{10,2},{3,11},{11,3},{4,12},{12,4},... | collective-permute-start | bytes 3538952 | tf_op jit(solution)/shard_map/ppermute | solution.py:471
  230.7 29.6 %collective-permute-start.30 = (bf16[2,768,768]{2,1,0:T(8,128)(2,1)}, bf16[2,768,768]{2,1,0:T(8,128)(2,1)}, u32[]{:S(2)}, u32[]{:S(2)}) collective-permute-start(bf16[2,768,768]{2,1,0:T(8,128)(2,1)} %get-tuple-element.71), channel_id=1, source_target_pairs={{0,8},{8,0},{1,9},{9,1},{2,10},{10,2},{3,11},{11,3},{4,12},{12,4},... | collective-permute-start | bytes 7077896 | tf_op jit(solution)/shard_map/ppermute | solution.py:471
  231.2 32.9 %collective-permute-start.32 = (bf16[2,192,3072]{2,1,0:T(8,128)(2,1)}, bf16[2,192,3072]{2,1,0:T(8,128)(2,1)}, u32[]{:S(2)}, u32[]{:S(2)}) collective-permute-start(bf16[2,192,3072]{2,1,0:T(8,128)(2,1)} %get-tuple-element.73), channel_id=1, source_target_pairs={{0,8},{8,0},{1,9},{9,1},{2,10},{10,2},{3,11},{11,3},{4,12},{12,4},... | collective-permute-start | bytes 7077896 | tf_op jit(solution)/shard_map/ppermute | solution.py:471
  258.9 45.4 %collective-permute-start.35 = (bf16[4,1024,128]{2,1,0:T(8,128)(2,1)}, bf16[4,1024,128]{2,1,0:T(8,128)(2,1)}, u32[]{:S(2)}, u32[]{:S(2)}) collective-permute-start(bf16[4,1024,128]{2,1,0:T(8,128)(2,1)} %get-tuple-element.81), channel_id=1, source_target_pairs={{0,8},{8,0},{1,9},{9,1},{2,10},{10,2},{3,11},{11,3},{4,12},{12,4},... | collective-permute-start | bytes 3145736 | tf_op jit(solution)/shard_map/ppermute | solution.py:471
  259.3 45.0 %collective-permute-start.34 = (bf16[4,1024,128]{2,1,0:T(8,128)(2,1)}, bf16[4,1024,128]{2,1,0:T(8,128)(2,1)}, u32[]{:S(2)}, u32[]{:S(2)}) collective-permute-start(bf16[4,1024,128]{2,1,0:T(8,128)(2,1)} %get-tuple-element.80), channel_id=1, source_target_pairs={{0,8},{8,0},{1,9},{9,1},{2,10},{10,2},{3,11},{11,3},{4,12},{12,4},... | collective-permute-start | bytes 3145736 | tf_op jit(solution)/shard_map/ppermute | solution.py:471
  262.6 33.4 %collective-permute-start.31 = (bf16[768,768]{1,0:T(8,128)(2,1)S(1)}, bf16[768,768]{1,0:T(8,128)(2,1)}, u32[]{:S(2)}, u32[]{:S(2)}) collective-permute-start(bf16[768,768]{1,0:T(8,128)(2,1)S(1)} %slice_bitcast_fusion), channel_id=1, source_target_pairs={{0,16},{16,0},{1,17},{17,1},{2,18},{18,2},{3,19},{19,3},{4,20},{20... | collective-permute-start | bytes 3538952 | tf_op jit(solution)/shard_map/ppermute | solution.py:471
  267.9 32.1 %collective-permute-start.33 = (bf16[2,4,24,3072]{3,2,1,0:T(8,128)(2,1)}, bf16[2,4,24,3072]{3,2,1,0:T(8,128)(2,1)}, u32[]{:S(2)}, u32[]{:S(2)}) collective-permute-start(bf16[2,4,24,3072]{3,2,1,0:T(8,128)(2,1)} %dynamic-slice_bitcast_fusion), channel_id=1, source_target_pairs={{0,1},{1,0},{2,3},{3,2},{4,5},{5,4},{6,7},{7,6},{8,9},{9,8},{10,11... | collective-permute-start | bytes 3538952 | tf_op jit(solution)/shard_map/ppermute | solution.py:471
  298.5 36.4 %collective-permute-start.49 = (bf16[4,96,768]{2,1,0:T(8,128)(2,1)}, bf16[4,96,768]{2,1,0:T(8,128)(2,1)}, u32[]{:S(2)}, u32[]{:S(2)}) collective-permute-start(bf16[4,96,768]{2,1,0:T(8,128)(2,1)} %dynamic-slice_bitcast_fusion.5), channel_id=1, source_target_pairs={{0,1},{1,0},{2,3},{3,2},{4,5},{5,4},{6,7},{7,6},{8,9},{9,8},{10,11... | collective-permute-start | bytes 1769480 | tf_op jit(solution)/shard_map/ppermute | solution.py:471
  302.7 31.9 %collective-permute-start.48 = (bf16[4,24,3072]{2,1,0:T(8,128)(2,1)S(1)}, bf16[4,24,3072]{2,1,0:T(8,128)(2,1)S(1)}, u32[]{:S(2)}, u32[]{:S(2)}) collective-permute-start(bf16[4,24,3072]{2,1,0:T(8,128)(2,1)S(1)} %slice_bitcast_fusion.4), channel_id=1, source_target_pairs={{0,16},{16,0},{1,17},{17,1},{2,18},{18,2},{3,19},{19,3},{4,20},{20... | collective-permute-start | bytes 1769480 | tf_op jit(solution)/shard_map/ppermute | solution.py:471
  336.9 71.8 %collective-permute-start.50 = (bf16[2,96,768]{2,1,0:T(8,128)(2,1)S(1)}, bf16[2,96,768]{2,1,0:T(8,128)(2,1)S(1)}, u32[]{:S(2)}, u32[]{:S(2)}) collective-permute-start(bf16[2,96,768]{2,1,0:T(8,128)(2,1)S(1)} %get-tuple-element.106), channel_id=1, source_target_pairs={{0,2},{2,4},{4,6},{6,0},{1,3},{3,5},{5,7},{7,1},{8,10},{10,12},{12... | collective-permute-start | bytes 884744 | tf_op jit(solution)/shard_map/ppermute | solution.py:475
  342.5 70.9 %collective-permute-start.51 = (bf16[2,96,768]{2,1,0:T(8,128)(2,1)S(1)}, bf16[2,96,768]{2,1,0:T(8,128)(2,1)S(1)}, u32[]{:S(2)}, u32[]{:S(2)}) collective-permute-start(bf16[2,96,768]{2,1,0:T(8,128)(2,1)S(1)} %get-tuple-element.107), channel_id=1, source_target_pairs={{0,4},{2,6},{4,0},{6,2},{1,5},{3,7},{5,1},{7,3},{8,12},{10,14},{12... | collective-permute-start | bytes 884744 | tf_op jit(solution)/shard_map/ppermute | solution.py:475
  353.6 59.9 %collective-permute-start.52 = (bf16[2,96,768]{2,1,0:T(8,128)(2,1)S(1)}, bf16[2,96,768]{2,1,0:T(8,128)(2,1)S(1)}, u32[]{:S(2)}, u32[]{:S(2)}) collective-permute-start(bf16[2,96,768]{2,1,0:T(8,128)(2,1)S(1)} %get-tuple-element.104), channel_id=1, source_target_pairs={{0,6},{2,0},{4,2},{6,4},{1,7},{3,1},{5,3},{7,5},{8,14},{10,8},{12,... | collective-permute-start | bytes 884744 | tf_op jit(solution)/shard_map/ppermute | solution.py:475
  355.5 53.7 %collective-permute-start.38 = (bf16[512,768]{1,0:T(8,128)(2,1)S(1)}, bf16[512,768]{1,0:T(8,128)(2,1)S(1)}, u32[]{:S(2)}, u32[]{:S(2)}) collective-permute-start(bf16[512,768]{1,0:T(8,128)(2,1)S(1)} %dynamic-slice_bitcast_fusion.1), channel_id=1, source_target_pairs={{0,16},{16,0},{1,17},{17,1},{2,18},{18,2},{3,19},{19,3},{4,20},{20... | collective-permute-start | bytes 2359304 | tf_op jit(solution)/shard_map/ppermute | solution.py:471
  (59 other events, 773.7 us)

commit v2 on v1

--- a/solution.py
+++ b/solution.py
@@ -147,6 +147,7 @@
 eps_norm = 1e-05
 rope_base = 10000.0
 EXTRA = 128
+BIAS = 32
 
 def dot_nt(a,b): return lax.dot_general(a,b,(((1,),(1,)),((),())),preferred_element_type=f32)
 def dot_tn(a,b): return lax.dot_general(a,b,(((0,),(0,)),((),())),preferred_element_type=f32)
@@ -168,10 +169,10 @@
     s[...]=jnp.zeros_like(s)
     for k,v in enumerate((a,b,c,d,e,f)): s[k:k+1,0:r]=v[...].astype(f32)[None,:]
     s[6:9,0:r]=pb[...].astype(f32)
-    ebv=eb[...].astype(f32)[None,:]
-    for k in range(4): s[9+k:10+k,0:r]=ebv[:,k*r:(k+1)*r]
     out[:,:1536]=pk[:,:1536]
-    out[:,1536:1536+EXTRA]=s[...].T[0:r,:].astype(bf16)
+    s[...]=s[...].T
+    s[0:1,BIAS:BIAS+4*r]=eb[...].astype(f32)[None,:]
+    out[:,1536:1536+EXTRA]=s[0:r,:].astype(bf16)
     out[:,1536+EXTRA:2304+EXTRA]=pk[:,1536:]
     out[:,2304+EXTRA:]=ow[...]
 def pack(pk,ow,vecs,pb,eb):
@@ -191,9 +192,9 @@
             keep[...]=value[:,k*half:(k+1)*half]
             send[...]=value[:,(1-k)*half:(2-k)*half]
 
-def proj_body(me, a, b, *refs):
+def proj_body(me, a, b, *refs, r_of):
     qa,qb=refs[:4],refs[4:8]
-    tab,keep,send,t,vec,ws,ex,st=refs[8:]
+    tab,keep,send,t,vec,be,ws,ex,st=refs[8:]
     i=pl.program_id(0)
     @pl.when(i==0)
     def _():
@@ -203,6 +204,10 @@
             ws[rows,1536:]=qb[n][...]
             ex[rows,:]=qa[n][:,1536:].astype(f32)
         vec[...]=ex[...].T[:16,:]
+        per=4*r_of
+        for d in range(3072//per):
+            q,o=divmod(d*per,768)
+            be[q,:,o:o+per]=ex[d*r_of:d*r_of+1,BIAS:BIAS+per]
     x=jnp.where(i==me[0],a[0],b[...])
     t[...]=x
     normed,_=norm_of(x)
@@ -221,17 +226,17 @@
             keep[...]=st[:,:,k*384:(k+1)*384]
             send[...]=st[:,:,(1-k)*384:(2-k)*384]
 
-def project(me,mine,other,qa,qb,tab):
+def project(me,mine,other,qa,qb,tab,r):
     n=2*other.shape[0]; rb=n//2; per=1
     S=jax.ShapeDtypeStruct
     out=pl.BlockSpec((3,rb,384),lambda i,me:(0,i,0))
-    return pl.pallas_call(proj_body,
-        out_shape=(S((3,n,384),bf16),S((3,n,384),bf16),S((n,768),bf16),S((16,768),f32)),
+    return pl.pallas_call(functools.partial(proj_body,r_of=r),
+        out_shape=(S((3,n,384),bf16),S((3,n,384),bf16),S((n,768),bf16),S((16,768),f32),S((4,1,768),f32)),
         grid_spec=pltpu.PrefetchScalarGridSpec(num_scalar_prefetch=1,grid=(n//rb,),
             in_specs=[pl.BlockSpec((1,rb,768),lambda i,me:(me[0],i%per,0)),pl.BlockSpec((rb,768),lambda i,me:(i%per,0))]+
               [WHOLE(w.shape) for w in qa]+[WHOLE((w.shape[0],768)) for w in qb]+
               [pl.BlockSpec((3,rb,128),lambda i,me:(0,(2*(i//per)+me[1])*per+i%per,0))],
-            out_specs=(out,out,pl.BlockSpec((rb,768),lambda i,me:(i,0)),pl.BlockSpec((16,768),lambda i,me:(0,0))),
+            out_specs=(out,out,pl.BlockSpec((rb,768),lambda i,me:(i,0)),pl.BlockSpec((16,768),lambda i,me:(0,0)),pl.BlockSpec((4,1,768),lambda i,me:(0,0,0))),
             scratch_shapes=[pltpu.VMEM((768,2304),bf16),pltpu.VMEM((768,EXTRA),f32),pltpu.VMEM((3,rb,768),bf16)]),
         compiler_params=pltpu.CompilerParams(vmem_limit_bytes=56<<20),
         name="project",
@@ -266,39 +271,48 @@
 
 def outl_body(me, *refs):
     ka,ra,qb=refs[:3],refs[3:6],refs[6:10]
-    mid,out,wos=refs[10:]
-    @pl.when(pl.program_id(0)==0)
+    mid,mine,other,wos=refs[10:]
+    i=pl.program_id(0)
+    @pl.when(i==0)
     def _():
         for n in range(4): wos[rows_of(me,n,qb[n].shape[0]),:]=qb[n][...]
     half=mid.shape[0]//2
+    outs=[]
     for r in (slice(0,half),slice(half,2*half)):
         acc=mid[r,:]
         for g,a in ((0,ka),(1,ra)):
             rows=pl.ds(pl.multiple_of((me[1]^g)*384,384),384)
             acc=acc+dot(jnp.concatenate([p[0,r,:] for p in a],1),wos[rows,:])
-        out[r,:]=acc.astype(bf16)
-
-def layer_output(me,keep,recv,qb,mid,rb=512):
-    n=mid.shape[0]
+        outs.append(acc.astype(bf16))
+    out=jnp.concatenate(outs,0)
+    @pl.when(i==me[0])
+    def _(): mine[...]=out
+    @pl.when(i!=me[0])
+    def _(): other[...]=out
+
+def layer_output(me,keep,recv,qb,mid):
+    n=mid.shape[0]; rb=n//2
     a=pl.BlockSpec((1,rb,128),lambda i,me:(0,i,0))
+    o=pl.BlockSpec((rb,768),lambda i,me:(0,0))
     return pl.pallas_call(outl_body,
-        out_shape=jax.ShapeDtypeStruct((n,768),bf16),
-        grid_spec=pltpu.PrefetchScalarGridSpec(num_scalar_prefetch=1,grid=(n//rb,),
+        out_shape=(jax.ShapeDtypeStruct((rb,768),bf16),)*2,
+        grid_spec=pltpu.PrefetchScalarGridSpec(num_scalar_prefetch=1,grid=(2,),
             in_specs=[a]*6+[pl.BlockSpec((w.shape[0],768),lambda i,me:(0,1),pipeline_mode=pl.Buffered(1)) for w in qb]+
               [pl.BlockSpec((rb,768),lambda i,me:(i,0))],
-            out_specs=pl.BlockSpec((rb,768),lambda i,me:(i,0)),
+            out_specs=(o,o),
             scratch_shapes=[pltpu.VMEM((768,768),bf16)]),
         name="layer_output",
         cost_estimate=pl.CostEstimate(flops=2*n*768*768,transcendentals=0,bytes_accessed=n*768*8+768*768*2),
     )(me,*keep,*recv,*qb,mid)
 
-def back_body(me, *refs):
+def back_body(me, *refs, r_of):
     ka,ra=refs[:3],refs[3:6]
     u,t,low=refs[6:9]
     qa,qb=refs[9:13],refs[13:17]
-    vec,eb,sums_two,keepA,sendA,keepB,sendB,ig,ws,b1T,acc,gs,os,ex=refs[17:]
+    vec,eb,sums_two,keepA,sendA,keepB,sendB,ig_mine,ig_other,ws,b1T,acc,gs,os,ex=refs[17:]
     g=pl.program_id(0)
     gc=me[1]^g
+    n=t.shape[0]
     @pl.when(g==0)
     def _():
         for i in range(4):
@@ -310,7 +324,6 @@
         ex[...]=jnp.zeros_like(ex)
         ex[4:5,:]=jnp.sum(u[...].astype(f32),axis=0,keepdims=True)
         ex[2:4,:]=sums_two[0:2,:]
-        ex[8:12,:]=eb[...]
         normed,_=norm_of(t[...])
         b1T[...]=(normed*vec[0:1,:]+vec[1:2,:]).astype(bf16).T
     def one(a):
@@ -341,24 +354,33 @@
         b=acc[...]
         ex[0:1,:]=jnp.sum(b*normed,axis=0,keepdims=True)
         ex[1:2,:]=jnp.sum(b,axis=0,keepdims=True)
-        ig[...]=(low[...]+norm_back(b,normed,inv,vec[0:1,:])).astype(bf16)
+        v=(low[...]+norm_back(b,normed,inv,vec[0:1,:])).astype(bf16)
+        for h in range(2):
+            @pl.when(me[0]==h)
+            def _():
+                ig_mine[...]=v[h*(n//2):(h+1)*(n//2)]
+                ig_other[...]=v[(1-h)*(n//2):(2-h)*(n//2)]
         acc[0:768,0:EXTRA]=ex[...].T
+        per=4*r_of
+        for d in range(3072//per):
+            q,o=divmod(d*per,768)
+            acc[d*r_of:d*r_of+1,BIAS:BIAS+per]=eb[q,:,o:o+per]
         for i in range(4):
             A,B=((keepA,keepB),(sendA,sendB))[i%2]
             rows=rows_of(me,i,192)
             B[i//2,:,768:]=os[rows,:]
             A[i//2,:,1536:]=acc[rows,0:EXTRA].astype(bf16)
 
-def back(me,keep,recv,u,t,low,qa,qb,vec,eb,sums_two):
+def back(me,keep,recv,u,t,low,qa,qb,vec,eb,sums_two,r):
     n=t.shape[0]
     S=jax.ShapeDtypeStruct; V=pltpu.VMEM
     A,B=(2,192,1536+EXTRA),(2,192,1536)
-    return pl.pallas_call(back_body,
-        out_shape=(S(A,bf16),S(A,bf16),S(B,bf16),S(B,bf16),S((n,768),bf16)),
+    return pl.pallas_call(functools.partial(back_body,r_of=r),
+        out_shape=(S(A,bf16),S(A,bf16),S(B,bf16),S(B,bf16),S((n//2,768),bf16),S((n//2,768),bf16)),
         grid_spec=pltpu.PrefetchScalarGridSpec(num_scalar_prefetch=1,grid=(2,),
             in_specs=[WHOLE((4,n,128))]*6+[WHOLE((n,768))]*3+
-              [WHOLE(w.shape) for w in qa]+[WHOLE((w.shape[0],768)) for w in qb]+[WHOLE((16,768)),WHOLE((4,768)),WHOLE((8,768))],
-            out_specs=[WHOLE(A),WHOLE(A),WHOLE(B),WHOLE(B),WHOLE((n,768))],
+              [WHOLE(w.shape) for w in qa]+[WHOLE((w.shape[0],768)) for w in qb]+[WHOLE((16,768)),WHOLE((4,1,768)),WHOLE((8,768))],
+            out_specs=[WHOLE(A),WHOLE(A),WHOLE(B),WHOLE(B),WHOLE((n//2,768)),WHOLE((n//2,768))],
             scratch_shapes=[V((2,768,1152),bf16),V((768,n),bf16),V((n,768),f32),V((768,1152),bf16),V((768,768),bf16),V((EXTRA,768),f32)]),
         compiler_params=pltpu.CompilerParams(vmem_limit_bytes=58<<20),
         name="back",
@@ -454,7 +476,7 @@
     v=s[:,1536:1536+EXTRA].T
     for i in range(5): vecs[i][...]=v[i,:]
     vecs[5][...]=v[5:8,:]
-    vecs[6][...]=jnp.concatenate([v[8+i:9+i,:] for i in range(4)],1)[0,:]
+    vecs[6][...]=s[0:1,1536+BIAS:1536+BIAS+4*r][0,:]
     e=total(pieces[count:],0)
     for i in range(4): expand[:,i*768:(i+1)*768]=e[i*r:(i+1)*r,:]
     reduce_[...]=total(pieces[count:],1)
@@ -524,8 +546,13 @@
     half = ROT // 2
     frequency = rope_base ** (-(jnp.arange(half, dtype=f32) * 2.0 / ROT))
     lane = jnp.arange(128, dtype=jnp.int32) % HD
-    angles = jnp.arange(length, dtype=jnp.int32).astype(f32)[:, None] * jnp.tile(frequency, 16)[None, :]
-    co, si = jnp.cos(angles), jnp.sin(angles)
+    frequency = jnp.tile(frequency, 16)[None, :]
+    fine = jnp.arange(64, dtype=jnp.int32).astype(f32)[:, None] * frequency
+    coarse = jnp.arange(0, length, 64, dtype=jnp.int32).astype(f32)[:, None] * frequency
+    cf, sf = jnp.cos(fine)[None], jnp.sin(fine)[None]
+    cc, sc = jnp.cos(coarse)[:, None], jnp.sin(coarse)[:, None]
+    co = (cc * cf - sc * sf).reshape(length, 128)
+    si = (sc * cf + cc * sf).reshape(length, 128)
     return jnp.stack(
         [
             jnp.where(lane < ROT, co, 1.0),
@@ -535,10 +562,8 @@
     )
 
 
-def exchange(mine, x):
-    other = swap(lax.dynamic_index_in_dim(mine, 1 - x, 0, keepdims=False), "x")
-    place = lax.broadcasted_iota(jnp.int32, (2, 1, 1), 0)
-    return jnp.where(place == x, mine, other[None])
+def exchange(mine, other, x):
+    return pick(x, mine, swap(other, "x"))
 
 
 def shards(
@@ -585,7 +610,7 @@
     side_r = swap(line_r, "y")
     near_e = join(y, line_e, swap(line_e, "y"))
 
-    own, send, t, vec = project(me, inputs, other_tokens, qa, qb, table)
+    own, send, t, vec, be = project(me, inputs, other_tokens, qa, qb, table, r)
     got = swap(send, "c")
     gown, gsend, u = upstream_heads(after(me, own), cotangent, other_grads, qb)
     ggot = swap(gsend, "c")
@@ -597,9 +622,7 @@
     far_e = swap(near_e, "x")
     eq = [near_e, swap(near_e, "c"), far_e, swap(far_e, "c")]
     rq = [near_r, swap(near_r, "c"), far_r, swap(far_r, "c")]
-    be = vec[9:13].reshape(4, -1, r).transpose(1, 0, 2).reshape(4, 1, -1)
     keep_r, send_r, keep_e, send_e, eb, mid, low, sums_two = feed(me, after(t, keep0), u, eq, rq, be, vec)
-    eb = eb.reshape(-1, 4, r).transpose(1, 0, 2).reshape(4, width)
     keep1, give1 = attention(after(core, mid), *operands, 1)
     sum_r = add(keep_r, swap(send_r, "c"), bf16)
     sum_e = add(keep_e, swap(send_e, "c"), bf16)
@@ -608,21 +631,21 @@
     sum_e = halve(sum_e, y, m)
     keep = [keep0, keep1, keep2]
     recv = [swap(give0, "c"), swap(give1, "c"), swap(give2, "c")]
-    layer_out = layer_output(after(me, sum_r, sum_e, keep2), keep, recv, qb, mid)
+    out_mine, out_other = layer_output(after(me, sum_r, sum_e, keep2), keep, recv, qb, mid)
     sum_r = halve(sum_r, y, m)
     sum_e = add(sum_e[0], swap(sum_e[1], "x"), bf16)
     feed_line = jnp.stack([wide(sum_e), sum_r], 1)
-    keep_a, send_a, keep_b, send_b, input_grad = back(
-        after(me, layer_out), keep, recv, u, t, low, qa, qb, vec, eb, sums_two
+    keep_a, send_a, keep_b, send_b, grad_mine, grad_other = back(
+        after(me, out_mine), keep, recv, u, t, low, qa, qb, vec, eb, sums_two, r
     )
     feed_pieces = line_pieces(feed_line, m)
-    layer_out = exchange(layer_out.reshape(inputs.shape), x)
+    layer_out = exchange(out_mine, out_other, x)
     sum_a = add(keep_a, swap(send_a, "c"), bf16)
     sum_b = add(keep_b, swap(send_b, "c"), bf16)
     line_a = halve(add(sum_a[0], swap(sum_a[1], "x"), bf16), y, m)
     sum_b = halve(sum_b, y, m)
     line_b = add(sum_b[0], swap(sum_b[1], "x"), bf16)
-    input_grad = exchange(after(input_grad, layer_out).reshape(inputs.shape), x)
+    input_grad = exchange(grad_mine, after(grad_other, layer_out), x)
     line = jnp.concatenate([line_a, line_b], 2)
     mats, v, packed_vec, expand_vec = finish(line_pieces(line, m), feed_pieces)
     packed_grad, output_grad, expand_grad, reduce_grad = mats

time: 431 us -> 427 us (level)
  starting transfers between devices: 53.6 us -> 60.1 us
  local copies, waits for them, and re-layouts: 17.3 us -> 11.8 us
    ppermute x15, starting transfers between devices: 28 us -> 34.8 us  [shift(): return lax.ppermute(a, axis, [(i, (i + step) % size) for i in range(size)])]
  transfers between devices with their start and end apart: 53 -> 53, of which waited for: 13 -> 14; matrix products, arithmetic and copies ran while one was open for 8% -> 6% of each run, Pallas kernels for 30% -> 31%
where the time goes in v2:
time: 427 us; the launch traced here: 421 us
  Pallas kernels  180 us (42%)
  waiting for transfers between devices  144 us (34%)
  starting transfers between devices  60.1 us (14%)
  other arithmetic  23.4 us (5%)
  local copies, waits for them, and re-layouts  11.8 us (3%)
    ppermute x38, waiting for transfers between devices, swap(): return lax.ppermute(a, axis, [(0, 1), (1, 0)])  108 us
    pallas_call x3, Pallas kernels, attention(): pl.pallas_call(functools.partial(attn_body, blk=blk, length=length, ch=ch...  82.6 us
    pallas_call x1, Pallas kernels, feed(): pl.pallas_call(functools.partial(feed_body, rb=rb), out_shape=[S((2, 768,...  47 us
    ppermute x15, waiting for transfers between devices, shift(): return lax.ppermute(a, axis, [(i, (i + step) % size) for i in range(size)])  36.2 us
    ppermute x15, starting transfers between devices, shift(): return lax.ppermute(a, axis, [(i, (i + step) % size) for i in range(size)])  34.8 us
    ppermute x38, starting transfers between devices, swap(): return lax.ppermute(a, axis, [(0, 1), (1, 0)])  25.3 us
    pallas_call x1, Pallas kernels, back(): pl.pallas_call(functools.partial(back_body, r_of=r), out_shape=(S(A, bf16...  23.4 us
    pallas_call x1, Pallas kernels, project(): pl.pallas_call(functools.partial(proj_body, r_of=r), out_shape=(S((3, n,...  11.1 us
  transfers between devices with their start and end apart: 53, of which 14 were waited for; matrix products, arithmetic and copies ran while one was open for 6% of the time, Pallas kernels for 31%

profile of v2, /device:TPU:0, one launch (start us, length us, event | category | flops | bytes accessed | tf_op | source)
XLA Modules:
  0.0 421.1 jit_solution(14019013627314401113)
XLA Ops:
  2.4 5.1 %collective-permute-start.1 = (bf16[24,3200]{1,0:T(8,128)(2,1)}, bf16[24,3200]{1,0:T(8,128)(2,1)S(1)}, u32[]{:S(2)}, u32[]{:S(2)}) collective-permute-start(bf16[24,3200]{1,0:T(8,128)(2,1)} %pack.1), channel_id=1, source_target_pairs={{0,6},{2,0},{4,2},{6,4},{1,7},{3,1},{5,3},{7,5},{8,14},{10,8},{12,... | collective-permute-start | bytes 460808 | tf_op jit(solution)/shard_map/ppermute | solution.py:497
  12.2 8.6 %collective-permute-done.2 = bf16[24,3200]{1,0:T(8,128)(2,1)} collective-permute-done((bf16[24,3200]{1,0:T(8,128)(2,1)}, bf16[24,3200]{1,0:T(8,128)(2,1)}, u32[]{:S(2)}, u32[]{:S(2)}) %collective-permute-start.2) | collective-permute-done | bytes 153632 | tf_op jit(solution)/shard_map/ppermute | solution.py:497
  26.5 5.5 %collective-permute-done.4 = bf16[4,24,1664]{2,1,0:T(8,128)(2,1)} collective-permute-done((bf16[4,24,1664]{2,1,0:T(8,128)(2,1)S(1)}, bf16[4,24,1664]{2,1,0:T(8,128)(2,1)}, u32[]{:S(2)}, u32[]{:S(2)}) %collective-permute-start.4) | collective-permute-done | bytes 319520 | tf_op jit(solution)/shard_map/ppermute | solution.py:493
  38.6 16.9 %collective-permute-done.10 = bf16[4,24,1536]{2,1,0:T(8,128)(2,1)S(1)} collective-permute-done((bf16[4,24,1536]{2,1,0:T(8,128)(2,1)S(1)}, bf16[4,24,1536]{2,1,0:T(8,128)(2,1)S(1)}, u32[]{:S(2)}, u32[]{:S(2)}) %collective-permute-start.10) | collective-permute-done | bytes 294944 | tf_op jit(solution)/shard_map/ppermute | solution.py:493
  63.5 14.8 %collective-permute-done.23 = bf16[96,768]{1,0:T(8,128)(2,1)S(1)} collective-permute-done((bf16[96,768]{1,0:T(8,128)(2,1)S(1)}, bf16[96,768]{1,0:T(8,128)(2,1)S(1)}, u32[]{:S(2)}, u32[]{:S(2)}) %collective-permute-start.23) | collective-permute-done | bytes 147488 | tf_op jit(solution)/shard_map/ppermute | solution.py:493
  85.1 11.1 %project.1 = (bf16[3,1024,384]{2,1,0:T(8,128)(2,1)}, bf16[3,1024,384]{2,1,0:T(8,128)(2,1)}, bf16[1024,768]{1,0:T(8,128)(2,1)}, f32[16,768]{1,0:T(8,128)}, f32[4,1,768]{2,1,0:T(1,128)}) custom-call(s32[2]{0:T(128)} %pad_add_fusion.me, bf16[2,512,768]{2,1,0:T(8,128)(2,1)} %a.4, bf16[512,768]{1,0:T(8,128)(2,1)} %collective-permute-done.b, ...), custom_call_target="tpu_custom_call" | custom-call | flops 3623878656 | bytes 12582912 | tf_op jit(solution)/shard_map/project/pallas_call | solution.py:233
  99.7 20.7 %collective-permute-done.25 = bf16[2,96,768]{2,1,0:T(8,128)(2,1)S(1)} collective-permute-done((bf16[2,96,768]{2,1,0:T(8,128)(2,1)S(1)}, bf16[2,96,768]{2,1,0:T(8,128)(2,1)S(1)}, u32[]{:S(2)}, u32[]{:S(2)}) %collective-permute-start.25) | collective-permute-done | bytes 294944 | tf_op jit(solution)/shard_map/ppermute | solution.py:497
  123.0 5.5 %upstream.1 = (bf16[1024,384]{1,0:T(8,128)(2,1)}, bf16[1024,384]{1,0:T(8,128)(2,1)}, bf16[1024,768]{1,0:T(8,128)(2,1)}) custom-call(s32[2]{0:T(128)} %pad_add_fusion.me, bf16[2,512,768]{2,1,0:T(8,128)(2,1)} %a.5, bf16[512,768]{1,0:T(8,128)(2,1)} %collective-permute-done.14.b, bf16[192,1536]{1,0:T(8,128)(2,1)} %copy-done.1, bf16[192,1536]{1,0:T(8,128)(2,1)} %copy-done.7, ...), custom_call_target="tpu_custom_call" | custom-call | flops 1207959552 | bytes 5898240 | tf_op jit(solution)/shard_map/upstream/pallas_call | solution.py:261
  129.3 19.4 %collective-permute-done.27 = bf16[4,2,96,768]{3,2,0,1:T(8,128)(2,1)} collective-permute-done((bf16[4,2,96,768]{3,2,0,1:T(8,128)(2,1)S(1)}, bf16[4,2,96,768]{3,2,0,1:T(8,128)(2,1)}, u32[]{:S(2)}, u32[]{:S(2)}) %collective-permute-start.27) | collective-permute-done | bytes 1179680 | tf_op jit(solution)/shard_map/ppermute | solution.py:493
  151.0 27.3 %attention.3 = (bf16[4,1024,128]{2,1,0:T(8,128)(2,1)}, bf16[4,1024,128]{2,1,0:T(8,128)(2,1)}) custom-call(s32[1]{0:T(128)} %bitcast.1.c_ref, bf16[3,1024,384]{2,1,0:T(8,128)(2,1)} %get-tuple-element.65.own, bf16[3,1024,384]{2,1,0:T(8,128)(2,1)} %collective-permute-done.13.par, bf16[1024,384]{1,0:T(8,128)(2,1)} %get-tuple-element.68.gown, ...), custom_call_target="tpu_custom_call" | custom-call | flops 12884901888 | bytes 4194304 | tf_op jit(solution)/shard_map/attention/pallas_call | solution.py:134
  179.7 47.0 %feed.1 = (bf16[2,768,768]{2,1,0:T(8,128)(2,1)}, bf16[2,768,768]{2,1,0:T(8,128)(2,1)}, bf16[2,192,3072]{2,1,0:T(8,128)(2,1)}, bf16[2,192,3072]{2,1,0:T(8,128)(2,...) custom-call(s32[2]{0:T(128)} %pad_add_fusion.me, ...), custom_call_target="tpu_custom_call" | custom-call | flops 28991029248 | bytes 34603008 | tf_op jit(solution)/shard_map/feed/pallas_call | solution.py:451
  227.3 27.6 %attention.4 = (bf16[4,1024,128]{2,1,0:T(8,128)(2,1)}, bf16[4,1024,128]{2,1,0:T(8,128)(2,1)}) custom-call(s32[1]{0:T(128)} %bitcast.1.c_ref, bf16[3,1024,384]{2,1,0:T(8,128)(2,1)} %get-tuple-element.65.own, bf16[3,1024,384]{2,1,0:T(8,128)(2,1)} %collective-permute-done.13.par, bf16[1024,384]{1,0:T(8,128)(2,1)} %get-tuple-element.68.gown, ...), custom_call_target="tpu_custom_call" | custom-call | flops 12884901888 | bytes 4194304 | tf_op jit(solution)/shard_map/attention/pallas_call | solution.py:134
  263.6 27.7 %attention.5 = (bf16[4,1024,128]{2,1,0:T(8,128)(2,1)}, bf16[4,1024,128]{2,1,0:T(8,128)(2,1)}) custom-call(s32[1]{0:T(128)} %bitcast.1.c_ref, bf16[3,1024,384]{2,1,0:T(8,128)(2,1)} %get-tuple-element.65.own, bf16[3,1024,384]{2,1,0:T(8,128)(2,1)} %collective-permute-done.13.par, bf16[1024,384]{1,0:T(8,128)(2,1)} %get-tuple-element.68.gown, ...), custom_call_target="tpu_custom_call" | custom-call | flops 12884901888 | bytes 4194304 | tf_op jit(solution)/shard_map/attention/pallas_call | solution.py:134
  299.6 6.3 %layer_output.1 = (bf16[512,768]{1,0:T(8,128)(2,1)}, bf16[512,768]{1,0:T(8,128)(2,1)}) custom-call(s32[2]{0:T(128)} %pad_add_fusion.me, bf16[4,1024,128]{2,1,0:T(8,128)(2,1)} %get-tuple-element.70.refs_0_, bf16[4,1024,128]{2,1,0:T(8,128)(2,1)} %get-tuple-element.81.refs_1_, bf16[4,1024,128]{2,1,0:T(8,128)(2,1)} %get-tuple-element.83.refs_2_, ...), custom_call_target="tpu_custom_call" | custom-call | flops 1207959552 | bytes 7471104 | tf_op jit(solution)/shard_map/layer_output/pallas_call | solution.py:297
  305.9 23.4 %back.1 = (bf16[2,192,1664]{2,1,0:T(8,128)(2,1)}, bf16[2,192,1664]{2,1,0:T(8,128)(2,1)}, bf16[2,192,1536]{2,1,0:T(8,128)(2,1)}, bf16[2,192,1536]{2,1,0:T(8,128)(...) custom-call(s32[2]{0:T(128)} %pad_add_fusion.me, bf16[4,1024,128]{2,1,0:T(8,128)(2,1)} %get-tuple-element.70.refs_0_, ...), custom_call_target="tpu_custom_call" | custom-call | flops 8455716864 | bytes 33030144 | tf_op jit(solution)/shard_map/back/pallas_call | solution.py:378
  332.7 8.8 %collective-permute-start.50 = (bf16[2,96,768]{2,1,0:T(8,128)(2,1)S(1)}, bf16[2,96,768]{2,1,0:T(8,128)(2,1)S(1)}, u32[]{:S(2)}, u32[]{:S(2)}) collective-permute-start(bf16[2,96,768]{2,1,0:T(8,128)(2,1)S(1)} %get-tuple-element.114), channel_id=1, source_target_pairs={{0,2},{2,4},{4,6},{6,0},{1,3},{3,5},{5,7},{7,1},{8,10},{10,12},{12... | collective-permute-start | bytes 884744 | tf_op jit(solution)/shard_map/ppermute | solution.py:497
  341.5 7.9 %collective-permute-done.37 = bf16[512,768]{1,0:T(8,128)(2,1)S(1)} collective-permute-done((bf16[512,768]{1,0:T(8,128)(2,1)S(1)}, bf16[512,768]{1,0:T(8,128)(2,1)S(1)}, u32[]{:S(2)}, u32[]{:S(2)}) %collective-permute-start.37) | collective-permute-done | bytes 786464 | tf_op jit(solution)/shard_map/ppermute | solution.py:493
  353.1 13.2 %collective-permute-done.43 = bf16[2,4,24,1536]{3,2,1,0:T(8,128)(2,1)S(1)} collective-permute-done((bf16[2,4,24,1536]{3,2,1,0:T(8,128)(2,1)S(1)}, bf16[2,4,24,1536]{3,2,1,0:T(8,128)(2,1)S(1)}, u32[]{:S(2)}, u32[]{:S(2)}) %collective-permute-start.43) | collective-permute-done | bytes 589856 | tf_op jit(solution)/shard_map/ppermute | solution.py:493
  367.5 15.6 %collective-permute-done.40 = bf16[192,1664]{1,0:T(8,128)(2,1)S(1)} collective-permute-done((bf16[192,1664]{1,0:T(8,128)(2,1)S(1)}, bf16[192,1664]{1,0:T(8,128)(2,1)S(1)}, u32[]{:S(2)}, u32[]{:S(2)}) %collective-permute-start.40) | collective-permute-done | bytes 639008 | tf_op jit(solution)/shard_map/ppermute | solution.py:493
  383.8 6.6 %collective-permute-done.44 = bf16[4,24,1536]{2,1,0:T(8,128)(2,1)S(1)} collective-permute-done((bf16[4,24,1536]{2,1,0:T(8,128)(2,1)S(1)}, bf16[4,24,1536]{2,1,0:T(8,128)(2,1)S(1)}, u32[]{:S(2)}, u32[]{:S(2)}) %collective-permute-start.44) | collective-permute-done | bytes 294944 | tf_op jit(solution)/shard_map/ppermute | solution.py:493
  391.0 6.4 %collective-permute-done.41 = bf16[4,24,1664]{2,1,0:T(8,128)(2,1)S(1)} collective-permute-done((bf16[4,24,1664]{2,1,0:T(8,128)(2,1)S(1)}, bf16[4,24,1664]{2,1,0:T(8,128)(2,1)S(1)}, u32[]{:S(2)}, u32[]{:S(2)}) %collective-permute-start.41) | collective-permute-done | bytes 319520 | tf_op jit(solution)/shard_map/ppermute | solution.py:493
  398.2 8.8 %collective-permute-start.45 = (bf16[24,3200]{1,0:T(8,128)(2,1)S(1)}, bf16[24,3200]{1,0:T(8,128)(2,1)S(1)}, u32[]{:S(2)}, u32[]{:S(2)}) collective-permute-start(bf16[24,3200]{1,0:T(8,128)(2,1)S(1)} %get-tuple-element.124), channel_id=1, source_target_pairs={{0,2},{2,4},{4,6},{6,0},{1,3},{3,5},{5,7},{7,1},{8,10},{10,12},{12... | collective-permute-start | bytes 460808 | tf_op jit(solution)/shard_map/ppermute | solution.py:497
  408.0 2.9 collective-permute-start.47
  412.2 4.2 %collective-permute-done.46.refs_2_ = bf16[24,3200]{1,0:T(8,128)(2,1)S(1)} collective-permute-done((bf16[24,3200]{1,0:T(8,128)(2,1)S(1)}, bf16[24,3200]{1,0:T(8,128)(2,1)S(1)}, u32[]{:S(2)}, u32[]{:S(2)}) %collective-permute-start.46) | collective-permute-done | bytes 153632 | tf_op jit(solution)/shard_map/ppermute | solution.py:497
  (216 shorter events, 78.4 us)
Async XLA Ops:
  34.0 26.0 %collective-permute-start.6 = (bf16[192,1664]{1,0:T(8,128)(2,1)}, bf16[192,1664]{1,0:T(8,128)(2,1)}, u32[]{:S(2)}, u32[]{:S(2)}) collective-permute-start(bf16[192,1664]{1,0:T(8,128)(2,1)} %bitcast_select_fusion.5.refs_0_.refs_9_), channel_id=1, source_target_pairs={{0,16},{16,0},{1,17},{17,1},{2,18},{18,2},{3,19},{19,3},{4,20},{20... | collective-permute-start | bytes 1916936 | tf_op jit(solution)/shard_map/ppermute | solution.py:493
  60.0 25.1 %collective-permute-start.7 = (bf16[192,1664]{1,0:T(8,128)(2,1)}, bf16[192,1664]{1,0:T(8,128)(2,1)}, u32[]{:S(2)}, u32[]{:S(2)}) collective-permute-start(bf16[192,1664]{1,0:T(8,128)(2,1)} %collective-permute-done.6.refs_2_.refs_11_), channel_id=1, source_target_pairs={{0,8},{8,0},{1,9},{9,1},{2,10},{10,2},{3,11},{11,3},{4,12},{12,4},... | collective-permute-start | bytes 1916936 | tf_op jit(solution)/shard_map/ppermute | solution.py:493
  85.0 35.4 %collective-permute-start.25 = (bf16[2,96,768]{2,1,0:T(8,128)(2,1)S(1)}, bf16[2,96,768]{2,1,0:T(8,128)(2,1)S(1)}, u32[]{:S(2)}, u32[]{:S(2)}) collective-permute-start(bf16[2,96,768]{2,1,0:T(8,128)(2,1)S(1)} %pad_maximum_fusion.1), channel_id=1, source_target_pairs={{0,4},{2,6},{4,0},{6,2},{1,5},{3,7},{5,1},{7,3},{8,12},{10,14},{12... | collective-permute-start | bytes 884744 | tf_op jit(solution)/shard_map/ppermute | solution.py:497
  96.2 24.2 %collective-permute-start.26 = (bf16[2,96,768]{2,1,0:T(8,128)(2,1)S(1)}, bf16[2,96,768]{2,1,0:T(8,128)(2,1)S(1)}, u32[]{:S(2)}, u32[]{:S(2)}) collective-permute-start(bf16[2,96,768]{2,1,0:T(8,128)(2,1)S(1)} %pad_maximum_fusion.1), channel_id=1, source_target_pairs={{0,2},{2,4},{4,6},{6,0},{1,3},{3,5},{5,7},{7,1},{8,10},{10,12},{12... | collective-permute-start | bytes 884744 | tf_op jit(solution)/shard_map/ppermute | solution.py:497
  97.3 53.7 %collective-permute-start.13 = (bf16[3,1024,384]{2,1,0:T(8,128)(2,1)}, bf16[3,1024,384]{2,1,0:T(8,128)(2,1)}, u32[]{:S(2)}, u32[]{:S(2)}) collective-permute-start(bf16[3,1024,384]{2,1,0:T(8,128)(2,1)} %get-tuple-element.66), channel_id=1, source_target_pairs={{0,8},{8,0},{1,9},{9,1},{2,10},{10,2},{3,11},{11,3},{4,12},{12,4},... | collective-permute-start | bytes 7077896 | tf_op jit(solution)/shard_map/ppermute | solution.py:493
  98.2 24.9 %collective-permute-start.14 = (bf16[512,768]{1,0:T(8,128)(2,1)S(1)}, bf16[512,768]{1,0:T(8,128)(2,1)}, u32[]{:S(2)}, u32[]{:S(2)}) collective-permute-start(bf16[512,768]{1,0:T(8,128)(2,1)S(1)} %dynamic-slice_bitcast_fusion.1), channel_id=1, source_target_pairs={{0,16},{16,0},{1,17},{17,1},{2,18},{18,2},{3,19},{19,3},{4,20},{20... | collective-permute-start | bytes 2359304 | tf_op jit(solution)/shard_map/ppermute | solution.py:493
  120.7 28.0 %collective-permute-start.27 = (bf16[4,2,96,768]{3,2,0,1:T(8,128)(2,1)S(1)}, bf16[4,2,96,768]{3,2,0,1:T(8,128)(2,1)}, u32[]{:S(2)}, u32[]{:S(2)}) collective-permute-start(bf16[4,2,96,768]{3,2,0,1:T(8,128)(2,1)S(1)} %select_select_fusion), channel_id=1, source_target_pairs={{0,1},{1,0},{2,3},{3,2},{4,5},{5,4},{6,7},{7,6},{8,9},{9,8},{10,11... | collective-permute-start | bytes 3538952 | tf_op jit(solution)/shard_map/ppermute | solution.py:493
  121.5 28.9 %collective-permute-start.21 = (bf16[192,3072]{1,0:T(8,128)(2,1)S(1)}, bf16[192,3072]{1,0:T(8,128)(2,1)}, u32[]{:S(2)}, u32[]{:S(2)}) collective-permute-start(bf16[192,3072]{1,0:T(8,128)(2,1)S(1)} %bitcast_select_fusion.2.e0), channel_id=1, source_target_pairs={{0,16},{16,0},{1,17},{17,1},{2,18},{18,2},{3,19},{19,3},{4,20},{20... | collective-permute-start | bytes 3538952 | tf_op jit(solution)/shard_map/ppermute | solution.py:493
  128.8 49.6 %collective-permute-start.20 = (bf16[192,3072]{1,0:T(8,128)(2,1)S(1)}, bf16[192,3072]{1,0:T(8,128)(2,1)S(1)}, u32[]{:S(2)}, u32[]{:S(2)}) collective-permute-start(bf16[192,3072]{1,0:T(8,128)(2,1)S(1)} %bitcast_select_fusion.2.e0), channel_id=1, source_target_pairs={{0,8},{8,0},{1,9},{9,1},{2,10},{10,2},{3,11},{11,3},{4,12},{12,4},... | collective-permute-start | bytes 3538952 | tf_op jit(solution)/shard_map/ppermute | solution.py:493
  150.3 28.0 %collective-permute-start.28 = (bf16[768,768]{1,0:T(8,128)(2,1)S(1)}, bf16[768,768]{1,0:T(8,128)(2,1)S(1)}, u32[]{:S(2)}, u32[]{:S(2)}) collective-permute-start(bf16[768,768]{1,0:T(8,128)(2,1)S(1)} %get-tuple-element.129.r0), channel_id=1, source_target_pairs={{0,8},{8,0},{1,9},{9,1},{2,10},{10,2},{3,11},{11,3},{4,12},{12,4},... | collective-permute-start | bytes 3538952 | tf_op jit(solution)/shard_map/ppermute | solution.py:493
  150.4 27.9 %collective-permute-start.29 = (bf16[768,768]{1,0:T(8,128)(2,1)S(1)}, bf16[768,768]{1,0:T(8,128)(2,1)}, u32[]{:S(2)}, u32[]{:S(2)}) collective-permute-start(bf16[768,768]{1,0:T(8,128)(2,1)S(1)} %get-tuple-element.128.r2), channel_id=1, source_target_pairs={{0,8},{8,0},{1,9},{9,1},{2,10},{10,2},{3,11},{11,3},{4,12},{12,4},... | collective-permute-start | bytes 3538952 | tf_op jit(solution)/shard_map/ppermute | solution.py:493
  150.9 27.5 %collective-permute-start.22 = (bf16[192,3072]{1,0:T(8,128)(2,1)}, bf16[192,3072]{1,0:T(8,128)(2,1)}, u32[]{:S(2)}, u32[]{:S(2)}) collective-permute-start(bf16[192,3072]{1,0:T(8,128)(2,1)} %collective-permute-done.21.e2), channel_id=1, source_target_pairs={{0,8},{8,0},{1,9},{9,1},{2,10},{10,2},{3,11},{11,3},{4,12},{12,4},... | collective-permute-start | bytes 3538952 | tf_op jit(solution)/shard_map/ppermute | solution.py:493
  226.7 28.7 %collective-permute-start.30 = (bf16[2,768,768]{2,1,0:T(8,128)(2,1)}, bf16[2,768,768]{2,1,0:T(8,128)(2,1)}, u32[]{:S(2)}, u32[]{:S(2)}) collective-permute-start(bf16[2,768,768]{2,1,0:T(8,128)(2,1)} %get-tuple-element.76), channel_id=1, source_target_pairs={{0,8},{8,0},{1,9},{9,1},{2,10},{10,2},{3,11},{11,3},{4,12},{12,4},... | collective-permute-start | bytes 7077896 | tf_op jit(solution)/shard_map/ppermute | solution.py:493
  227.1 32.2 %collective-permute-start.32 = (bf16[2,192,3072]{2,1,0:T(8,128)(2,1)}, bf16[2,192,3072]{2,1,0:T(8,128)(2,1)}, u32[]{:S(2)}, u32[]{:S(2)}) collective-permute-start(bf16[2,192,3072]{2,1,0:T(8,128)(2,1)} %get-tuple-element.78), channel_id=1, source_target_pairs={{0,8},{8,0},{1,9},{9,1},{2,10},{10,2},{3,11},{11,3},{4,12},{12,4},... | collective-permute-start | bytes 7077896 | tf_op jit(solution)/shard_map/ppermute | solution.py:493
  255.0 44.6 %collective-permute-start.35 = (bf16[4,1024,128]{2,1,0:T(8,128)(2,1)}, bf16[4,1024,128]{2,1,0:T(8,128)(2,1)}, u32[]{:S(2)}, u32[]{:S(2)}) collective-permute-start(bf16[4,1024,128]{2,1,0:T(8,128)(2,1)} %get-tuple-element.86), channel_id=1, source_target_pairs={{0,8},{8,0},{1,9},{9,1},{2,10},{10,2},{3,11},{11,3},{4,12},{12,4},... | collective-permute-start | bytes 3145736 | tf_op jit(solution)/shard_map/ppermute | solution.py:493
  255.3 44.3 %collective-permute-start.34 = (bf16[4,1024,128]{2,1,0:T(8,128)(2,1)}, bf16[4,1024,128]{2,1,0:T(8,128)(2,1)}, u32[]{:S(2)}, u32[]{:S(2)}) collective-permute-start(bf16[4,1024,128]{2,1,0:T(8,128)(2,1)} %get-tuple-element.85), channel_id=1, source_target_pairs={{0,8},{8,0},{1,9},{9,1},{2,10},{10,2},{3,11},{11,3},{4,12},{12,4},... | collective-permute-start | bytes 3145736 | tf_op jit(solution)/shard_map/ppermute | solution.py:493
  257.8 33.5 %collective-permute-start.31 = (bf16[768,768]{1,0:T(8,128)(2,1)S(1)}, bf16[768,768]{1,0:T(8,128)(2,1)}, u32[]{:S(2)}, u32[]{:S(2)}) collective-permute-start(bf16[768,768]{1,0:T(8,128)(2,1)S(1)} %slice_bitcast_fusion), channel_id=1, source_target_pairs={{0,16},{16,0},{1,17},{17,1},{2,18},{18,2},{3,19},{19,3},{4,20},{20... | collective-permute-start | bytes 3538952 | tf_op jit(solution)/shard_map/ppermute | solution.py:493
  263.1 32.2 %collective-permute-start.33 = (bf16[2,4,24,3072]{3,2,1,0:T(8,128)(2,1)}, bf16[2,4,24,3072]{3,2,1,0:T(8,128)(2,1)}, u32[]{:S(2)}, u32[]{:S(2)}) collective-permute-start(bf16[2,4,24,3072]{3,2,1,0:T(8,128)(2,1)} %dynamic-slice_bitcast_fusion), channel_id=1, source_target_pairs={{0,1},{1,0},{2,3},{3,2},{4,5},{5,4},{6,7},{7,6},{8,9},{9,8},{10,11... | collective-permute-start | bytes 3538952 | tf_op jit(solution)/shard_map/ppermute | solution.py:493
  293.7 36.8 %collective-permute-start.49 = (bf16[4,96,768]{2,1,0:T(8,128)(2,1)}, bf16[4,96,768]{2,1,0:T(8,128)(2,1)}, u32[]{:S(2)}, u32[]{:S(2)}) collective-permute-start(bf16[4,96,768]{2,1,0:T(8,128)(2,1)} %dynamic-slice_bitcast_fusion.3), channel_id=1, source_target_pairs={{0,1},{1,0},{2,3},{3,2},{4,5},{5,4},{6,7},{7,6},{8,9},{9,8},{10,11... | collective-permute-start | bytes 1769480 | tf_op jit(solution)/shard_map/ppermute | solution.py:493
  298.0 32.4 %collective-permute-start.48 = (bf16[4,24,3072]{2,1,0:T(8,128)(2,1)S(1)}, bf16[4,24,3072]{2,1,0:T(8,128)(2,1)S(1)}, u32[]{:S(2)}, u32[]{:S(2)}) collective-permute-start(bf16[4,24,3072]{2,1,0:T(8,128)(2,1)S(1)} %slice_bitcast_fusion.4), channel_id=1, source_target_pairs={{0,16},{16,0},{1,17},{17,1},{2,18},{18,2},{3,19},{19,3},{4,20},{20... | collective-permute-start | bytes 1769480 | tf_op jit(solution)/shard_map/ppermute | solution.py:493
  332.7 74.3 %collective-permute-start.50 = (bf16[2,96,768]{2,1,0:T(8,128)(2,1)S(1)}, bf16[2,96,768]{2,1,0:T(8,128)(2,1)S(1)}, u32[]{:S(2)}, u32[]{:S(2)}) collective-permute-start(bf16[2,96,768]{2,1,0:T(8,128)(2,1)S(1)} %get-tuple-element.114), channel_id=1, source_target_pairs={{0,2},{2,4},{4,6},{6,0},{1,3},{3,5},{5,7},{7,1},{8,10},{10,12},{12... | collective-permute-start | bytes 884744 | tf_op jit(solution)/shard_map/ppermute | solution.py:497
  341.5 70.7 %collective-permute-start.51 = (bf16[2,96,768]{2,1,0:T(8,128)(2,1)S(1)}, bf16[2,96,768]{2,1,0:T(8,128)(2,1)S(1)}, u32[]{:S(2)}, u32[]{:S(2)}) collective-permute-start(bf16[2,96,768]{2,1,0:T(8,128)(2,1)S(1)} %get-tuple-element.115), channel_id=1, source_target_pairs={{0,4},{2,6},{4,0},{6,2},{1,5},{3,7},{5,1},{7,3},{8,12},{10,14},{12... | collective-permute-start | bytes 884744 | tf_op jit(solution)/shard_map/ppermute | solution.py:497
  349.4 62.8 %collective-permute-start.52 = (bf16[2,96,768]{2,1,0:T(8,128)(2,1)S(1)}, bf16[2,96,768]{2,1,0:T(8,128)(2,1)S(1)}, u32[]{:S(2)}, u32[]{:S(2)}) collective-permute-start(bf16[2,96,768]{2,1,0:T(8,128)(2,1)S(1)} %get-tuple-element.112), channel_id=1, source_target_pairs={{0,6},{2,0},{4,2},{6,4},{1,7},{3,1},{5,3},{7,5},{8,14},{10,8},{12,... | collective-permute-start | bytes 884744 | tf_op jit(solution)/shard_map/ppermute | solution.py:497
  350.7 57.2 %collective-permute-start.38 = (bf16[512,768]{1,0:T(8,128)(2,1)S(1)}, bf16[512,768]{1,0:T(8,128)(2,1)S(1)}, u32[]{:S(2)}, u32[]{:S(2)}) collective-permute-start(bf16[512,768]{1,0:T(8,128)(2,1)S(1)} %copy-done.29), channel_id=1, source_target_pairs={{0,16},{16,0},{1,17},{17,1},{2,18},{18,2},{3,19},{19,3},{4,20},{20... | collective-permute-start | bytes 2359304 | tf_op jit(solution)/shard_map/ppermute | solution.py:493
  (60 other events, 795.8 us)

commit v3 on v2

--- a/solution.py
+++ b/solution.py
@@ -520,11 +520,17 @@
     return jnp.moveaxis(pick(y, near, far), 0, 1).reshape((-1,) + near.shape[2:])
 
 
+def add3(a, b, c):
+    return (a.astype(f32) + b.astype(f32) + c.astype(f32)).astype(bf16)
+
+
+def part(a, y, m):
+    a = a.reshape(a.shape[:-2] + (m, 2, -1) + a.shape[-1:])
+    return lax.dynamic_index_in_dim(a, y, a.ndim - 3, keepdims=False)
+
+
 def halve(a, y, m):
-    a = a.reshape(a.shape[:-2] + (m, 2, -1) + a.shape[-1:])
-    mine = lax.dynamic_index_in_dim(a, y, a.ndim - 3, keepdims=False)
-    other = lax.dynamic_index_in_dim(a, 1 - y, a.ndim - 3, keepdims=False)
-    return add(mine, swap(other, "y"), bf16)
+    return add(part(a, y, m), swap(part(a, 1 - y, m), "y"), bf16)
 
 
 def wide(a):
@@ -624,11 +630,12 @@
     rq = [near_r, swap(near_r, "c"), far_r, swap(far_r, "c")]
     keep_r, send_r, keep_e, send_e, eb, mid, low, sums_two = feed(me, after(t, keep0), u, eq, rq, be, vec)
     keep1, give1 = attention(after(core, mid), *operands, 1)
-    sum_r = add(keep_r, swap(send_r, "c"), bf16)
-    sum_e = add(keep_e, swap(send_e, "c"), bf16)
-    keep2, give2 = attention(after(core, keep1, sum_r, sum_e), *operands, 2)
-    sum_r = add(sum_r[0], swap(sum_r[1], "x"), bf16)
-    sum_e = halve(sum_e, y, m)
+    got_r, got_e = swap(send_r, "c"), swap(send_e, "c")
+    far_r = add(keep_r[1], got_r[1], bf16)
+    far_e = add(part(keep_e, 1 - y, m), part(got_e, 1 - y, m), bf16)
+    keep2, give2 = attention(after(core, keep1, far_r, far_e), *operands, 2)
+    sum_r = add3(keep_r[0], got_r[0], swap(far_r, "x"))
+    sum_e = add3(part(keep_e, y, m), part(got_e, y, m), swap(far_e, "y"))
     keep = [keep0, keep1, keep2]
     recv = [swap(give0, "c"), swap(give1, "c"), swap(give2, "c")]
     out_mine, out_other = layer_output(after(me, sum_r, sum_e, keep2), keep, recv, qb, mid)
@@ -640,10 +647,11 @@
     )
     feed_pieces = line_pieces(feed_line, m)
     layer_out = exchange(out_mine, out_other, x)
-    sum_a = add(keep_a, swap(send_a, "c"), bf16)
-    sum_b = add(keep_b, swap(send_b, "c"), bf16)
-    line_a = halve(add(sum_a[0], swap(sum_a[1], "x"), bf16), y, m)
-    sum_b = halve(sum_b, y, m)
+    got_a, got_b = swap(send_a, "c"), swap(send_b, "c")
+    far_a = add(keep_a[1], got_a[1], bf16)
+    far_b = add(part(keep_b, 1 - y, m), part(got_b, 1 - y, m), bf16)
+    line_a = halve(add3(keep_a[0], got_a[0], swap(far_a, "x")), y, m)
+    sum_b = add3(part(keep_b, y, m), part(got_b, y, m), swap(far_b, "y"))
     line_b = add(sum_b[0], swap(sum_b[1], "x"), bf16)
     input_grad = exchange(grad_mine, after(grad_other, layer_out), x)
     line = jnp.concatenate([line_a, line_b], 2)

time: 427 us -> 427 us (level)
  waiting for transfers between devices: 144 us -> 149 us
    ppermute x15, starting transfers between devices: 34.8 us -> 29.9 us  [shift(): return lax.ppermute(a, axis, [(i, (i + step) % size) for i in range(size)])]
    convert_element_type x0 -> x4, other arithmetic: none -> 4.55 us  [add3(): return (a.astype(f32) + b.astype(f32) + c.astype(f32)).astype(bf16)]
    convert_element_type x11 -> x7, other arithmetic: 9.2 us -> 5.02 us  [add(): return (a.astype(f32) + b.astype(f32)).astype(dtype)]
  transfers between devices with their start and end apart: 53 -> 53, of which waited for: 14 -> 16; matrix products, arithmetic and copies ran while one was open for 6% -> 6% of each run, Pallas kernels for 31% -> 30%
where the time goes in v3:
time: 427 us; the launch traced here: 421 us
  Pallas kernels  180 us (42%)
  waiting for transfers between devices  149 us (35%)
  starting transfers between devices  58.2 us (14%)
  other arithmetic  22.6 us (5%)
  local copies, waits for them, and re-layouts  9.83 us (2%)
    ppermute x38, waiting for transfers between devices, swap(): return lax.ppermute(a, axis, [(0, 1), (1, 0)])  112 us
    pallas_call x3, Pallas kernels, attention(): pl.pallas_call(functools.partial(attn_body, blk=blk, length=length, ch=ch...  82 us
    pallas_call x1, Pallas kernels, feed(): pl.pallas_call(functools.partial(feed_body, rb=rb), out_shape=[S((2, 768,...  47.2 us
    ppermute x15, waiting for transfers between devices, shift(): return lax.ppermute(a, axis, [(i, (i + step) % size) for i in range(size)])  37.5 us
    ppermute x15, starting transfers between devices, shift(): return lax.ppermute(a, axis, [(i, (i + step) % size) for i in range(size)])  29.9 us
    ppermute x38, starting transfers between devices, swap(): return lax.ppermute(a, axis, [(0, 1), (1, 0)])  28.3 us
    pallas_call x1, Pallas kernels, back(): pl.pallas_call(functools.partial(back_body, r_of=r), out_shape=(S(A, bf16...  23.2 us
    pallas_call x1, Pallas kernels, project(): pl.pallas_call(functools.partial(proj_body, r_of=r), out_shape=(S((3, n,...  11.1 us
  transfers between devices with their start and end apart: 53, of which 16 were waited for; matrix products, arithmetic and copies ran while one was open for 6% of the time, Pallas kernels for 30%

profile of v3, /device:TPU:0, one launch (start us, length us, event | category | flops | bytes accessed | tf_op | source)
XLA Modules:
  0.0 421.2 jit_solution(1788617930856018702)
XLA Ops:
  2.4 5.1 %collective-permute-start.1 = (bf16[24,3200]{1,0:T(8,128)(2,1)}, bf16[24,3200]{1,0:T(8,128)(2,1)S(1)}, u32[]{:S(2)}, u32[]{:S(2)}) collective-permute-start(bf16[24,3200]{1,0:T(8,128)(2,1)} %pack.1), channel_id=1, source_target_pairs={{0,6},{2,0},{4,2},{6,4},{1,7},{3,1},{5,3},{7,5},{8,14},{10,8},{12,... | collective-permute-start | bytes 460808 | tf_op jit(solution)/shard_map/ppermute | solution.py:497
  12.2 8.6 %collective-permute-done.2 = bf16[24,3200]{1,0:T(8,128)(2,1)} collective-permute-done((bf16[24,3200]{1,0:T(8,128)(2,1)}, bf16[24,3200]{1,0:T(8,128)(2,1)}, u32[]{:S(2)}, u32[]{:S(2)}) %collective-permute-start.2) | collective-permute-done | bytes 153632 | tf_op jit(solution)/shard_map/ppermute | solution.py:497
  26.5 5.5 %collective-permute-done.4 = bf16[4,24,1664]{2,1,0:T(8,128)(2,1)} collective-permute-done((bf16[4,24,1664]{2,1,0:T(8,128)(2,1)S(1)}, bf16[4,24,1664]{2,1,0:T(8,128)(2,1)}, u32[]{:S(2)}, u32[]{:S(2)}) %collective-permute-start.4) | collective-permute-done | bytes 319520 | tf_op jit(solution)/shard_map/ppermute | solution.py:493
  38.7 16.9 %collective-permute-done.10 = bf16[4,24,1536]{2,1,0:T(8,128)(2,1)S(1)} collective-permute-done((bf16[4,24,1536]{2,1,0:T(8,128)(2,1)S(1)}, bf16[4,24,1536]{2,1,0:T(8,128)(2,1)S(1)}, u32[]{:S(2)}, u32[]{:S(2)}) %collective-permute-start.10) | collective-permute-done | bytes 294944 | tf_op jit(solution)/shard_map/ppermute | solution.py:493
  62.5 16.0 %collective-permute-done.23 = bf16[96,768]{1,0:T(8,128)(2,1)} collective-permute-done((bf16[96,768]{1,0:T(8,128)(2,1)S(1)}, bf16[96,768]{1,0:T(8,128)(2,1)}, u32[]{:S(2)}, u32[]{:S(2)}) %collective-permute-start.23) | collective-permute-done | bytes 147488 | tf_op jit(solution)/shard_map/ppermute | solution.py:493
  86.3 11.1 %project.1 = (bf16[3,1024,384]{2,1,0:T(8,128)(2,1)}, bf16[3,1024,384]{2,1,0:T(8,128)(2,1)}, bf16[1024,768]{1,0:T(8,128)(2,1)}, f32[16,768]{1,0:T(8,128)}, f32[4,1,768]{2,1,0:T(1,128)}) custom-call(s32[2]{0:T(128)} %pad_add_fusion.me, bf16[2,512,768]{2,1,0:T(8,128)(2,1)} %a.4, bf16[512,768]{1,0:T(8,128)(2,1)} %collective-permute-done.b, ...), custom_call_target="tpu_custom_call" | custom-call | flops 3623878656 | bytes 12582912 | tf_op jit(solution)/shard_map/project/pallas_call | solution.py:233
  101.4 20.2 %collective-permute-done.25 = bf16[2,96,768]{2,1,0:T(8,128)(2,1)S(1)} collective-permute-done((bf16[2,96,768]{2,1,0:T(8,128)(2,1)S(1)}, bf16[2,96,768]{2,1,0:T(8,128)(2,1)S(1)}, u32[]{:S(2)}, u32[]{:S(2)}) %collective-permute-start.25) | collective-permute-done | bytes 294944 | tf_op jit(solution)/shard_map/ppermute | solution.py:497
  124.2 5.5 %upstream.1 = (bf16[1024,384]{1,0:T(8,128)(2,1)}, bf16[1024,384]{1,0:T(8,128)(2,1)}, bf16[1024,768]{1,0:T(8,128)(2,1)}) custom-call(s32[2]{0:T(128)} %pad_add_fusion.me, bf16[2,512,768]{2,1,0:T(8,128)(2,1)} %a.5, bf16[512,768]{1,0:T(8,128)(2,1)} %collective-permute-done.14.b, bf16[192,1536]{1,0:T(8,128)(2,1)} %copy-done.1, bf16[192,1536]{1,0:T(8,128)(2,1)} %copy-done.5, ...), custom_call_target="tpu_custom_call" | custom-call | flops 1207959552 | bytes 5898240 | tf_op jit(solution)/shard_map/upstream/pallas_call | solution.py:261
  130.5 19.4 %collective-permute-done.27 = bf16[4,2,96,768]{3,2,0,1:T(8,128)(2,1)} collective-permute-done((bf16[4,2,96,768]{3,2,0,1:T(8,128)(2,1)S(1)}, bf16[4,2,96,768]{3,2,0,1:T(8,128)(2,1)}, u32[]{:S(2)}, u32[]{:S(2)}) %collective-permute-start.27) | collective-permute-done | bytes 1179680 | tf_op jit(solution)/shard_map/ppermute | solution.py:493
  152.2 27.3 %attention.3 = (bf16[4,1024,128]{2,1,0:T(8,128)(2,1)}, bf16[4,1024,128]{2,1,0:T(8,128)(2,1)}) custom-call(s32[1]{0:T(128)} %bitcast.1.c_ref, bf16[3,1024,384]{2,1,0:T(8,128)(2,1)} %get-tuple-element.65.own, bf16[3,1024,384]{2,1,0:T(8,128)(2,1)} %collective-permute-done.13.par, bf16[1024,384]{1,0:T(8,128)(2,1)} %get-tuple-element.68.gown, ...), custom_call_target="tpu_custom_call" | custom-call | flops 12884901888 | bytes 4194304 | tf_op jit(solution)/shard_map/attention/pallas_call | solution.py:134
  180.8 47.2 %feed.1 = (bf16[2,768,768]{2,1,0:T(8,128)(2,1)}, bf16[2,768,768]{2,1,0:T(8,128)(2,1)}, bf16[2,192,3072]{2,1,0:T(8,128)(2,1)}, bf16[2,192,3072]{2,1,0:T(8,128)(2,...) custom-call(s32[2]{0:T(128)} %pad_add_fusion.me, ...), custom_call_target="tpu_custom_call" | custom-call | flops 28991029248 | bytes 34603008 | tf_op jit(solution)/shard_map/feed/pallas_call | solution.py:451
  228.6 27.5 %attention.4 = (bf16[4,1024,128]{2,1,0:T(8,128)(2,1)}, bf16[4,1024,128]{2,1,0:T(8,128)(2,1)}) custom-call(s32[1]{0:T(128)} %bitcast.1.c_ref, bf16[3,1024,384]{2,1,0:T(8,128)(2,1)} %get-tuple-element.65.own, bf16[3,1024,384]{2,1,0:T(8,128)(2,1)} %collective-permute-done.13.par, bf16[1024,384]{1,0:T(8,128)(2,1)} %get-tuple-element.68.gown, ...), custom_call_target="tpu_custom_call" | custom-call | flops 12884901888 | bytes 4194304 | tf_op jit(solution)/shard_map/attention/pallas_call | solution.py:134
  258.2 2.8 fusion.3
  264.7 27.2 %attention.5 = (bf16[4,1024,128]{2,1,0:T(8,128)(2,1)}, bf16[4,1024,128]{2,1,0:T(8,128)(2,1)}) custom-call(s32[1]{0:T(128)} %bitcast.1.c_ref, bf16[3,1024,384]{2,1,0:T(8,128)(2,1)} %get-tuple-element.65.own, bf16[3,1024,384]{2,1,0:T(8,128)(2,1)} %collective-permute-done.13.par, bf16[1024,384]{1,0:T(8,128)(2,1)} %get-tuple-element.68.gown, ...), custom_call_target="tpu_custom_call" | custom-call | flops 12884901888 | bytes 4194304 | tf_op jit(solution)/shard_map/attention/pallas_call | solution.py:134
  297.0 6.3 %layer_output.1 = (bf16[512,768]{1,0:T(8,128)(2,1)}, bf16[512,768]{1,0:T(8,128)(2,1)}) custom-call(s32[2]{0:T(128)} %pad_add_fusion.me, bf16[4,1024,128]{2,1,0:T(8,128)(2,1)} %get-tuple-element.70.refs_0_, bf16[4,1024,128]{2,1,0:T(8,128)(2,1)} %get-tuple-element.81.refs_1_, bf16[4,1024,128]{2,1,0:T(8,128)(2,1)} %get-tuple-element.83.refs_2_, ...), custom_call_target="tpu_custom_call" | custom-call | flops 1207959552 | bytes 7471104 | tf_op jit(solution)/shard_map/layer_output/pallas_call | solution.py:297
  303.3 23.2 %back.1 = (bf16[2,192,1664]{2,1,0:T(8,128)(2,1)}, bf16[2,192,1664]{2,1,0:T(8,128)(2,1)}, bf16[2,192,1536]{2,1,0:T(8,128)(2,1)}, bf16[2,192,1536]{2,1,0:T(8,128)(...) custom-call(s32[2]{0:T(128)} %pad_add_fusion.me, bf16[4,1024,128]{2,1,0:T(8,128)(2,1)} %get-tuple-element.70.refs_0_, ...), custom_call_target="tpu_custom_call" | custom-call | flops 8455716864 | bytes 33030144 | tf_op jit(solution)/shard_map/back/pallas_call | solution.py:378
  329.9 12.6 %collective-permute-done.49 = bf16[4,96,768]{2,1,0:T(8,128)(2,1)S(1)} collective-permute-done((bf16[4,96,768]{2,1,0:T(8,128)(2,1)S(1)}, bf16[4,96,768]{2,1,0:T(8,128)(2,1)S(1)}, u32[]{:S(2)}, u32[]{:S(2)}) %collective-permute-start.49) | collective-permute-done | bytes 589856 | tf_op jit(solution)/shard_map/ppermute | solution.py:493
  343.4 8.6 %collective-permute-start.50 = (bf16[2,96,768]{2,1,0:T(8,128)(2,1)S(1)}, bf16[2,96,768]{2,1,0:T(8,128)(2,1)S(1)}, u32[]{:S(2)}, u32[]{:S(2)}) collective-permute-start(bf16[2,96,768]{2,1,0:T(8,128)(2,1)S(1)} %get-tuple-element.114), channel_id=1, source_target_pairs={{0,2},{2,4},{4,6},{6,0},{1,3},{3,5},{5,7},{7,1},{8,10},{10,12},{12... | collective-permute-start | bytes 884744 | tf_op jit(solution)/shard_map/ppermute | solution.py:497
  359.2 9.7 %collective-permute-done.43 = bf16[2,4,24,1536]{3,2,1,0:T(8,128)(2,1)S(1)} collective-permute-done((bf16[2,4,24,1536]{3,2,1,0:T(8,128)(2,1)S(1)}, bf16[2,4,24,1536]{3,2,1,0:T(8,128)(2,1)S(1)}, u32[]{:S(2)}, u32[]{:S(2)}) %collective-permute-start.43) | collective-permute-done | bytes 589856 | tf_op jit(solution)/shard_map/ppermute | solution.py:493
  370.6 18.7 %collective-permute-done.40 = bf16[192,1664]{1,0:T(8,128)(2,1)S(1)} collective-permute-done((bf16[192,1664]{1,0:T(8,128)(2,1)S(1)}, bf16[192,1664]{1,0:T(8,128)(2,1)S(1)}, u32[]{:S(2)}, u32[]{:S(2)}) %collective-permute-start.40) | collective-permute-done | bytes 639008 | tf_op jit(solution)/shard_map/ppermute | solution.py:493
  391.0 5.0 %collective-permute-done.44 = bf16[4,24,1536]{2,1,0:T(8,128)(2,1)S(1)} collective-permute-done((bf16[4,24,1536]{2,1,0:T(8,128)(2,1)S(1)}, bf16[4,24,1536]{2,1,0:T(8,128)(2,1)S(1)}, u32[]{:S(2)}, u32[]{:S(2)}) %collective-permute-start.44) | collective-permute-done | bytes 294944 | tf_op jit(solution)/shard_map/ppermute | solution.py:493
  396.7 6.3 %collective-permute-done.41 = bf16[4,24,1664]{2,1,0:T(8,128)(2,1)S(1)} collective-permute-done((bf16[4,24,1664]{2,1,0:T(8,128)(2,1)S(1)}, bf16[4,24,1664]{2,1,0:T(8,128)(2,1)S(1)}, u32[]{:S(2)}, u32[]{:S(2)}) %collective-permute-start.41) | collective-permute-done | bytes 319520 | tf_op jit(solution)/shard_map/ppermute | solution.py:493
  403.8 2.7 collective-permute-start.45
  411.5 4.8 %collective-permute-done.46.refs_2_ = bf16[24,3200]{1,0:T(8,128)(2,1)S(1)} collective-permute-done((bf16[24,3200]{1,0:T(8,128)(2,1)S(1)}, bf16[24,3200]{1,0:T(8,128)(2,1)S(1)}, u32[]{:S(2)}, u32[]{:S(2)}) %collective-permute-start.46) | collective-permute-done | bytes 153632 | tf_op jit(solution)/shard_map/ppermute | solution.py:497
  (210 shorter events, 81.4 us)
Async XLA Ops:
  34.1 26.3 %collective-permute-start.6 = (bf16[192,1664]{1,0:T(8,128)(2,1)}, bf16[192,1664]{1,0:T(8,128)(2,1)}, u32[]{:S(2)}, u32[]{:S(2)}) collective-permute-start(bf16[192,1664]{1,0:T(8,128)(2,1)} %bitcast_select_fusion.5.refs_0_.refs_9_), channel_id=1, source_target_pairs={{0,16},{16,0},{1,17},{17,1},{2,18},{18,2},{3,19},{19,3},{4,20},{20... | collective-permute-start | bytes 1916936 | tf_op jit(solution)/shard_map/ppermute | solution.py:493
  60.4 25.9 %collective-permute-start.7 = (bf16[192,1664]{1,0:T(8,128)(2,1)}, bf16[192,1664]{1,0:T(8,128)(2,1)}, u32[]{:S(2)}, u32[]{:S(2)}) collective-permute-start(bf16[192,1664]{1,0:T(8,128)(2,1)} %collective-permute-done.6.refs_2_.refs_11_), channel_id=1, source_target_pairs={{0,8},{8,0},{1,9},{9,1},{2,10},{10,2},{3,11},{11,3},{4,12},{12,4},... | collective-permute-start | bytes 1916936 | tf_op jit(solution)/shard_map/ppermute | solution.py:493
  86.2 35.4 %collective-permute-start.25 = (bf16[2,96,768]{2,1,0:T(8,128)(2,1)S(1)}, bf16[2,96,768]{2,1,0:T(8,128)(2,1)S(1)}, u32[]{:S(2)}, u32[]{:S(2)}) collective-permute-start(bf16[2,96,768]{2,1,0:T(8,128)(2,1)S(1)} %pad_maximum_fusion.1), channel_id=1, source_target_pairs={{0,4},{2,6},{4,0},{6,2},{1,5},{3,7},{5,1},{7,3},{8,12},{10,14},{12... | collective-permute-start | bytes 884744 | tf_op jit(solution)/shard_map/ppermute | solution.py:497
  99.0 53.2 %collective-permute-start.13 = (bf16[3,1024,384]{2,1,0:T(8,128)(2,1)}, bf16[3,1024,384]{2,1,0:T(8,128)(2,1)}, u32[]{:S(2)}, u32[]{:S(2)}) collective-permute-start(bf16[3,1024,384]{2,1,0:T(8,128)(2,1)} %get-tuple-element.66), channel_id=1, source_target_pairs={{0,8},{8,0},{1,9},{9,1},{2,10},{10,2},{3,11},{11,3},{4,12},{12,4},... | collective-permute-start | bytes 7077896 | tf_op jit(solution)/shard_map/ppermute | solution.py:493
  121.9 28.0 %collective-permute-start.27 = (bf16[4,2,96,768]{3,2,0,1:T(8,128)(2,1)S(1)}, bf16[4,2,96,768]{3,2,0,1:T(8,128)(2,1)}, u32[]{:S(2)}, u32[]{:S(2)}) collective-permute-start(bf16[4,2,96,768]{3,2,0,1:T(8,128)(2,1)S(1)} %select_select_fusion), channel_id=1, source_target_pairs={{0,1},{1,0},{2,3},{3,2},{4,5},{5,4},{6,7},{7,6},{8,9},{9,8},{10,11... | collective-permute-start | bytes 3538952 | tf_op jit(solution)/shard_map/ppermute | solution.py:493
  122.6 28.9 %collective-permute-start.21 = (bf16[192,3072]{1,0:T(8,128)(2,1)S(1)}, bf16[192,3072]{1,0:T(8,128)(2,1)}, u32[]{:S(2)}, u32[]{:S(2)}) collective-permute-start(bf16[192,3072]{1,0:T(8,128)(2,1)S(1)} %bitcast_select_fusion.2.e0), channel_id=1, source_target_pairs={{0,16},{16,0},{1,17},{17,1},{2,18},{18,2},{3,19},{19,3},{4,20},{20... | collective-permute-start | bytes 3538952 | tf_op jit(solution)/shard_map/ppermute | solution.py:493
  129.9 49.5 %collective-permute-start.20 = (bf16[192,3072]{1,0:T(8,128)(2,1)S(1)}, bf16[192,3072]{1,0:T(8,128)(2,1)S(1)}, u32[]{:S(2)}, u32[]{:S(2)}) collective-permute-start(bf16[192,3072]{1,0:T(8,128)(2,1)S(1)} %bitcast_select_fusion.2.e0), channel_id=1, source_target_pairs={{0,8},{8,0},{1,9},{9,1},{2,10},{10,2},{3,11},{11,3},{4,12},{12,4},... | collective-permute-start | bytes 3538952 | tf_op jit(solution)/shard_map/ppermute | solution.py:493
  151.5 28.0 %collective-permute-start.28 = (bf16[768,768]{1,0:T(8,128)(2,1)S(1)}, bf16[768,768]{1,0:T(8,128)(2,1)S(1)}, u32[]{:S(2)}, u32[]{:S(2)}) collective-permute-start(bf16[768,768]{1,0:T(8,128)(2,1)S(1)} %get-tuple-element.129.r0), channel_id=1, source_target_pairs={{0,8},{8,0},{1,9},{9,1},{2,10},{10,2},{3,11},{11,3},{4,12},{12,4},... | collective-permute-start | bytes 3538952 | tf_op jit(solution)/shard_map/ppermute | solution.py:493
  151.6 27.9 %collective-permute-start.29 = (bf16[768,768]{1,0:T(8,128)(2,1)S(1)}, bf16[768,768]{1,0:T(8,128)(2,1)}, u32[]{:S(2)}, u32[]{:S(2)}) collective-permute-start(bf16[768,768]{1,0:T(8,128)(2,1)S(1)} %get-tuple-element.128.r2), channel_id=1, source_target_pairs={{0,8},{8,0},{1,9},{9,1},{2,10},{10,2},{3,11},{11,3},{4,12},{12,4},... | collective-permute-start | bytes 3538952 | tf_op jit(solution)/shard_map/ppermute | solution.py:493
  152.1 27.4 %collective-permute-start.22 = (bf16[192,3072]{1,0:T(8,128)(2,1)}, bf16[192,3072]{1,0:T(8,128)(2,1)}, u32[]{:S(2)}, u32[]{:S(2)}) collective-permute-start(bf16[192,3072]{1,0:T(8,128)(2,1)} %collective-permute-done.21.e2), channel_id=1, source_target_pairs={{0,8},{8,0},{1,9},{9,1},{2,10},{10,2},{3,11},{11,3},{4,12},{12,4},... | collective-permute-start | bytes 3538952 | tf_op jit(solution)/shard_map/ppermute | solution.py:493
  228.1 28.6 %collective-permute-start.30 = (bf16[2,768,768]{2,1,0:T(8,128)(2,1)}, bf16[2,768,768]{2,1,0:T(8,128)(2,1)S(1)}, u32[]{:S(2)}, u32[]{:S(2)}) collective-permute-start(bf16[2,768,768]{2,1,0:T(8,128)(2,1)} %get-tuple-element.76), channel_id=1, source_target_pairs={{0,8},{8,0},{1,9},{9,1},{2,10},{10,2},{3,11},{11,3},{4,12},{12,4},... | collective-permute-start | bytes 7077896 | tf_op jit(solution)/shard_map/ppermute | solution.py:493
  228.5 34.0 %collective-permute-start.32 = (bf16[2,192,3072]{2,1,0:T(8,128)(2,1)}, bf16[2,192,3072]{2,1,0:T(8,128)(2,1)}, u32[]{:S(2)}, u32[]{:S(2)}) collective-permute-start(bf16[2,192,3072]{2,1,0:T(8,128)(2,1)} %get-tuple-element.78), channel_id=1, source_target_pairs={{0,8},{8,0},{1,9},{9,1},{2,10},{10,2},{3,11},{11,3},{4,12},{12,4},... | collective-permute-start | bytes 7077896 | tf_op jit(solution)/shard_map/ppermute | solution.py:493
  256.2 40.8 %collective-permute-start.35 = (bf16[4,1024,128]{2,1,0:T(8,128)(2,1)}, bf16[4,1024,128]{2,1,0:T(8,128)(2,1)}, u32[]{:S(2)}, u32[]{:S(2)}) collective-permute-start(bf16[4,1024,128]{2,1,0:T(8,128)(2,1)} %get-tuple-element.86), channel_id=1, source_target_pairs={{0,8},{8,0},{1,9},{9,1},{2,10},{10,2},{3,11},{11,3},{4,12},{12,4},... | collective-permute-start | bytes 3145736 | tf_op jit(solution)/shard_map/ppermute | solution.py:493
  256.5 40.5 %collective-permute-start.34 = (bf16[4,1024,128]{2,1,0:T(8,128)(2,1)}, bf16[4,1024,128]{2,1,0:T(8,128)(2,1)}, u32[]{:S(2)}, u32[]{:S(2)}) collective-permute-start(bf16[4,1024,128]{2,1,0:T(8,128)(2,1)} %get-tuple-element.85), channel_id=1, source_target_pairs={{0,8},{8,0},{1,9},{9,1},{2,10},{10,2},{3,11},{11,3},{4,12},{12,4},... | collective-permute-start | bytes 3145736 | tf_op jit(solution)/shard_map/ppermute | solution.py:493
  260.9 34.3 %collective-permute-start.31 = (bf16[768,768]{1,0:T(8,128)(2,1)}, bf16[768,768]{1,0:T(8,128)(2,1)}, u32[]{:S(2)}, u32[]{:S(2)}) collective-permute-start(bf16[768,768]{1,0:T(8,128)(2,1)} %fusion.3), channel_id=1, source_target_pairs={{0,16},{16,0},{1,17},{17,1},{2,18},{18,2},{3,19},{19,3},{4,20},{20... | collective-permute-start | bytes 3538952 | tf_op jit(solution)/shard_map/ppermute | solution.py:493
  264.1 28.1 %collective-permute-start.33 = (bf16[2,4,24,3072]{3,2,1,0:T(8,128)(2,1)S(1)}, bf16[2,4,24,3072]{3,2,1,0:T(8,128)(2,1)}, u32[]{:S(2)}, u32[]{:S(2)}) collective-permute-start(bf16[2,4,24,3072]{3,2,1,0:T(8,128)(2,1)S(1)} %fusion.4), channel_id=1, source_target_pairs={{0,1},{1,0},{2,3},{3,2},{4,5},{5,4},{6,7},{7,6},{8,9},{9,8},{10,11... | collective-permute-start | bytes 3538952 | tf_op jit(solution)/shard_map/ppermute | solution.py:493
  294.6 35.0 %collective-permute-start.48 = (bf16[4,24,3072]{2,1,0:T(8,128)(2,1)S(1)}, bf16[4,24,3072]{2,1,0:T(8,128)(2,1)S(1)}, u32[]{:S(2)}, u32[]{:S(2)}) collective-permute-start(bf16[4,24,3072]{2,1,0:T(8,128)(2,1)S(1)} %slice_bitcast_fusion), channel_id=1, source_target_pairs={{0,16},{16,0},{1,17},{17,1},{2,18},{18,2},{3,19},{19,3},{4,20},{20... | collective-permute-start | bytes 1769480 | tf_op jit(solution)/shard_map/ppermute | solution.py:493
  326.5 25.6 %collective-permute-start.42 = (bf16[2,192,1536]{2,1,0:T(8,128)(2,1)}, bf16[2,192,1536]{2,1,0:T(8,128)(2,1)S(1)}, u32[]{:S(2)}, u32[]{:S(2)}) collective-permute-start(bf16[2,192,1536]{2,1,0:T(8,128)(2,1)} %get-tuple-element.100), channel_id=1, source_target_pairs={{0,8},{8,0},{1,9},{9,1},{2,10},{10,2},{3,11},{11,3},{4,12},{12,4},... | collective-permute-start | bytes 3538952 | tf_op jit(solution)/shard_map/ppermute | solution.py:493
  328.1 29.4 %collective-permute-start.39 = (bf16[2,192,1664]{2,1,0:T(8,128)(2,1)}, bf16[2,192,1664]{2,1,0:T(8,128)(2,1)S(1)}, u32[]{:S(2)}, u32[]{:S(2)}) collective-permute-start(bf16[2,192,1664]{2,1,0:T(8,128)(2,1)} %get-tuple-element.98), channel_id=1, source_target_pairs={{0,8},{8,0},{1,9},{9,1},{2,10},{10,2},{3,11},{11,3},{4,12},{12,4},... | collective-permute-start | bytes 3833864 | tf_op jit(solution)/shard_map/ppermute | solution.py:493
  328.1 26.5 %collective-permute-start.37 = (bf16[512,768]{1,0:T(8,128)(2,1)S(1)}, bf16[512,768]{1,0:T(8,128)(2,1)S(1)}, u32[]{:S(2)}, u32[]{:S(2)}) collective-permute-start(bf16[512,768]{1,0:T(8,128)(2,1)S(1)} %copy-done.29), channel_id=1, source_target_pairs={{0,16},{16,0},{1,17},{17,1},{2,18},{18,2},{3,19},{19,3},{4,20},{20... | collective-permute-start | bytes 2359304 | tf_op jit(solution)/shard_map/ppermute | solution.py:493
  343.4 63.0 %collective-permute-start.50 = (bf16[2,96,768]{2,1,0:T(8,128)(2,1)S(1)}, bf16[2,96,768]{2,1,0:T(8,128)(2,1)S(1)}, u32[]{:S(2)}, u32[]{:S(2)}) collective-permute-start(bf16[2,96,768]{2,1,0:T(8,128)(2,1)S(1)} %get-tuple-element.114), channel_id=1, source_target_pairs={{0,2},{2,4},{4,6},{6,0},{1,3},{3,5},{5,7},{7,1},{8,10},{10,12},{12... | collective-permute-start | bytes 884744 | tf_op jit(solution)/shard_map/ppermute | solution.py:497
  352.1 58.2 %collective-permute-start.51 = (bf16[2,96,768]{2,1,0:T(8,128)(2,1)S(1)}, bf16[2,96,768]{2,1,0:T(8,128)(2,1)S(1)}, u32[]{:S(2)}, u32[]{:S(2)}) collective-permute-start(bf16[2,96,768]{2,1,0:T(8,128)(2,1)S(1)} %get-tuple-element.115), channel_id=1, source_target_pairs={{0,4},{2,6},{4,0},{6,2},{1,5},{3,7},{5,1},{7,3},{8,12},{10,14},{12... | collective-permute-start | bytes 884744 | tf_op jit(solution)/shard_map/ppermute | solution.py:497
  352.1 58.2 %collective-permute-start.52 = (bf16[2,96,768]{2,1,0:T(8,128)(2,1)S(1)}, bf16[2,96,768]{2,1,0:T(8,128)(2,1)S(1)}, u32[]{:S(2)}, u32[]{:S(2)}) collective-permute-start(bf16[2,96,768]{2,1,0:T(8,128)(2,1)S(1)} %get-tuple-element.112), channel_id=1, source_target_pairs={{0,6},{2,0},{4,2},{6,4},{1,7},{3,1},{5,3},{7,5},{8,14},{10,8},{12,... | collective-permute-start | bytes 884744 | tf_op jit(solution)/shard_map/ppermute | solution.py:497
  357.5 49.0 %collective-permute-start.38 = (bf16[512,768]{1,0:T(8,128)(2,1)S(1)}, bf16[512,768]{1,0:T(8,128)(2,1)S(1)}, u32[]{:S(2)}, u32[]{:S(2)}) collective-permute-start(bf16[512,768]{1,0:T(8,128)(2,1)S(1)} %copy-done.28), channel_id=1, source_target_pairs={{0,16},{16,0},{1,17},{17,1},{2,18},{18,2},{3,19},{19,3},{4,20},{20... | collective-permute-start | bytes 2359304 | tf_op jit(solution)/shard_map/ppermute | solution.py:493
  (59 other events, 738.2 us)
